TPU v7x, 256 devices: a whole 4x4x8 slice. The times are simulated.
256 devices in a mesh: pipe: 8 (over y, x_lo), dp: 32 (over x_hi, z, core).
Axes of the slice: x: 4 (x_hi: 2, x_lo: 2; x = x_hi * 2 + x_lo), y: 4, z: 8, core: 2. Of those that a mesh axis runs over, the one named last changes fastest.
Arguments:
- acts: bfloat16 [8, 8192, 3072], P('pipe', 'dp'), may hold values from -24 to 24, as said below
- grad: float32 [24576, 4096], P('pipe', 'dp'), may hold values from -6 to 6
- owner_of: int32 [8, 12], replicated, may hold values from 0 to 7, as said below
Outputs:
- precond: float32 [24576, 4096], P('pipe', 'dp')
- held_inverse: float32 [8, 24, 256, 256], P('pipe', None, 'dp')
Inputs may be any that keep to these rules, and one draw needn't show every extreme that they name: `acts`: column and token scales of the activations vary; entries lie within the range. `owner_of`: no section index owns more than 24 blocks in all, and some section index owns exactly 24.
All inputs are finite; a program needn't handle non-finite values.
Results may differ from a plain program's by a relative error of at most 0.0003.
Values sent between devices are 32-bit elements; how exact they have to be, the bound alone decides.
No kernel may reach another device: no remote copies, remote signals or barrier semaphores. Data moves between devices by JAX's collectives and lax.ppermute only.
A program may use at most 64 MiB of HBM per device.

v0:
```python
import jax
import jax.numpy as jnp
from jax import lax
from jax.sharding import Mesh
from jax.sharding import PartitionSpec as P

BLK = 256
HOST = 24
DP = ("dp_0", "dp_1", "dp_2")


damping_ratio = 0.1


def in_blocks(value, dim, count):
    before, after = (value.shape[:dim], value.shape[dim + 1 :])
    return jnp.moveaxis(value.reshape(*before, count, -1, *after), dim, 0)


def summed_on_arrival(value, axis, dim):
    count = lax.axis_size(axis)
    tiles = lax.all_to_all(in_blocks(value, dim, count), axis, 0, 0, tiled=True)
    return jnp.sum(tiles, axis=0)


def from_everyone(value, axis):
    count = lax.axis_size(axis)
    return lax.all_to_all(
        jnp.broadcast_to(value[None], (count, *value.shape)), axis, 0, 0, tiled=True
    )


def in_order(tiles, dim):
    lengths = list(tiles.shape[1:])
    lengths[dim] *= tiles.shape[0]
    return jnp.moveaxis(tiles, 0, dim).reshape(lengths)


def collect(value, axis, dim):
    tiles = from_everyone(value, axis)
    return in_order(tiles, dim)


def turned_blocks(tiles, axes, sequence):
    inside = tiles.shape[1:]
    result = tiles.reshape(*(lax.axis_size(a) for a in axes), *inside)
    for k in sequence:
        result = lax.all_to_all(result, axes[k], k, k, tiled=True)
    return result.reshape(-1, *inside)


def exchange_by_chip(value, groups, sequence, split_dim, concat_dim):
    count = lax.axis_size(groups[0]) * lax.axis_size(groups[1])
    tiles = in_blocks(value, split_dim, count)
    return in_order(turned_blocks(tiles, groups, sequence), concat_dim)


def gather_in_order(value, axes, sequence):
    tiles = value[None]
    for k in sequence:
        tiles = lax.all_gather(tiles, axes[k], axis=0, tiled=True)
    carried = [lax.axis_size(axes[k]) for k in reversed(sequence)]
    tiles = tiles.reshape(*carried, *value.shape)
    turned = sorted(range(len(sequence)), key=lambda place: sequence[len(sequence) - 1 - place])
    return tiles.transpose(*turned, *range(len(sequence), tiles.ndim)).reshape(-1, *value.shape)


def gather_axes(value, axes, sequence, dim):
    return in_order(gather_in_order(value, axes, sequence), dim)


def invert_blocks(factor, vacant):
    order_size = factor.shape[-1]
    diagonal_sum = jnp.sum(jnp.diagonal(factor, axis1=1, axis2=2), axis=1)
    damping = damping_ratio * diagonal_sum / order_size
    identity = jnp.eye(order_size, dtype=factor.dtype)
    shifted = factor + (damping + vacant)[:, None, None] * identity
    cholesky_lower = jnp.linalg.cholesky(shifted)
    identity_stack = jnp.broadcast_to(identity, factor.shape)
    inv_lower = lax.linalg.triangular_solve(
        cholesky_lower, identity_stack, left_side=True, lower=True
    )
    return jnp.einsum("mkr,mkc->mrc", inv_lower, inv_lower, precision=lax.Precision.HIGHEST)


def slot_tables(owner_of):
    owners_flat = owner_of.reshape(-1)
    positions = jnp.arange(owners_flat.shape[0], dtype=jnp.int32)
    matches = owners_flat[:, None] == owners_flat[None, :]
    before = positions[None, :] < positions[:, None]
    slot_rank = jnp.sum((matches & before).astype(jnp.int32), axis=1)
    return (owners_flat, slot_rank)


def shards(acts, grad, owner_of):
    tokens = acts.shape[1]
    feature_count = acts.shape[2]
    nblocks = feature_count // BLK
    data_count = lax.axis_size(DP)
    section_count = lax.axis_size("pipe")
    row_share = BLK // data_count
    all_tokens = tokens * data_count
    section_index = lax.axis_index("pipe")
    member = lax.axis_index(DP)
    features = acts[0].reshape(tokens, nblocks, BLK)
    owners_flat, slot_rank = slot_tables(owner_of)
    slot_ids = jnp.arange(HOST, dtype=jnp.int32)
    pick_mine = (
        (owners_flat[None, :] == section_index) & (slot_rank[None, :] == slot_ids[:, None])
    ).astype(jnp.float32)
    own_owners = lax.dynamic_index_in_dim(owner_of, section_index, 0, keepdims=False)
    own_ranks = lax.dynamic_index_in_dim(
        slot_rank.reshape(section_count, nblocks), section_index, 0, keepdims=False
    )
    target = own_owners * HOST + own_ranks
    pick_back = (
        jnp.arange(section_count * HOST, dtype=jnp.int32)[None, :] == target[:, None]
    ).astype(jnp.float32)
    block_terms = jnp.einsum("tbr,tbc->rbc", features, features, preferred_element_type=jnp.float32)
    my_rows = summed_on_arrival(
        block_terms.reshape(row_share * lax.axis_size(DP), nblocks * BLK), DP, 0
    )
    pieces = collect(my_rows, "pipe", 0).reshape(section_count, row_share, nblocks, BLK)
    hosted = jnp.einsum(
        "jsb,srbc->jrc",
        pick_mine.reshape(HOST, section_count, nblocks),
        pieces,
        precision=lax.Precision.HIGHEST,
    )
    occupied = jnp.sum(pick_mine, axis=1)
    per_member = (HOST + data_count - 1) // data_count
    padded_count = per_member * data_count
    padded = jnp.pad(hosted, ((0, padded_count - HOST), (0, 0), (0, 0)))
    mine_blocks = lax.all_to_all(padded, DP, split_axis=0, concat_axis=1, tiled=True) / all_tokens
    padded_flags = jnp.pad(occupied, (0, padded_count - HOST))
    held_flags = lax.dynamic_slice_in_dim(padded_flags, member * per_member, per_member, 0)
    inverted = invert_blocks(mine_blocks, 1.0 - held_flags) * held_flags[:, None, None]
    spread_rows = exchange_by_chip(inverted, (("dp_0", "dp_1"), "dp_2"), (1, 0), 1, 0)
    held_rows = spread_rows[:HOST]
    returned = collect(held_rows, "pipe", 0)
    own_rows = jnp.einsum("bm,mrc->brc", pick_back, returned, precision=lax.Precision.HIGHEST)
    inverse = gather_axes(own_rows, DP, (0, 1, 2), 1)
    grad_blocks = grad.reshape(nblocks, BLK, grad.shape[1])
    precond = jnp.einsum("brk,bkc->brc", inverse, grad_blocks, precision=lax.Precision.HIGHEST)
    return (precond.reshape(feature_count, grad.shape[1]), held_rows[None])


def solution(mesh):
    torus = Mesh(
        mesh.devices.reshape(mesh.shape["pipe"], 2, 8, 2), ("pipe", "dp_0", "dp_1", "dp_2")
    )
    placed = (P("pipe", DP, None), P("pipe", DP), P())
    return jax.shard_map(
        shards,
        mesh=torus,
        in_specs=placed,
        out_specs=(P("pipe", DP), P("pipe", None, DP, None)),
        check_vma=False,
    )
```

profile of v0, /device:TPU:1, one launch (start us, length us, event | category | flops | bytes accessed | tf_op | source)
XLA Modules:
  0.0 336.6 jit_solution(11809143810914962391)
XLA Ops:
  7.2 1.8 copy.50
  9.0 2.3 convolution_bitcast_fusion
  11.3 5.2 %copy.52 = f32[256,12,256]{2,1,0:T(8,128)} copy(f32[256,12,256]{0,2,1:T(8,128)} %convolution_bitcast_fusion) | data formatting | bytes 6291456 | tf_op jit(solution)/shard_map/tbr,tbc->rbc/transpose | solution.py:119
  16.5 4.9 %reshape_reshape.7 = f32[32,8,3072]{2,1,0:T(8,128)} reshape(f32[256,12,256]{2,1,0:T(8,128)} %copy.52) | data formatting | bytes 6291456 | tf_op jit(solution)/shard_map/reshape;reshape | solution.py:17
  21.4 85.4 %all_to_all.34 = f32[32,8,3072]{2,1,0:T(8,128)} all-to-all(f32[32,8,3072]{2,1,0:T(8,128)} %reshape_reshape.7), channel_id=1, replica_groups=mesh['pipe'=8,'dp_0'=2,'dp_1'=8,'dp_2'=2] {'dp_0','dp_1','dp_2'}, dimensions={0} | all-to-all | bytes 6291456 | tf_op jit(solution)/shard_map/all_to_all | solution.py:22
  106.7 2.0 reduce_sum.37
  108.8 0.9 broadcast_in_dim.16
  109.7 4.2 %all-to-all-start.1 = ((f32[8,8,3072]{2,1,0:T(8,128)}), f32[8,8,3072]{2,1,0:T(8,128)S(1)}, u32[]{:S(2)}, u32[]{:S(2)}) async-start(f32[8,8,3072]{2,1,0:T(8,128)} %broadcast_in_dim.16), calls=%async_computation.1 | async-start | bytes 1572864 | tf_op jit(solution)/shard_map/all_to_all | solution.py:28
  114.0 0.2 convert_reduce_fusion
  114.3 10.0 %all-to-all-done.1 = f32[8,8,3072]{2,1,0:T(8,128)S(1)} async-done(((f32[8,8,3072]{2,1,0:T(8,128)}), f32[8,8,3072]{2,1,0:T(8,128)S(1)}, u32[]{:S(2)}, u32[]{:S(2)}) %all-to-all-start.1) | async-done | bytes 786464 | tf_op jit(solution)/shard_map/all_to_all | solution.py:28
  124.3 0.7 convolution_bitcast_fusion.1
  125.1 0.7 pad.9.clone
  125.8 9.9 %all-to-all-start.2 = ((f32[32,8,256]{2,1,0:T(8,128)}), f32[32,8,256]{2,1,0:T(8,128)S(1)}, u32[]{:S(2)}, u32[]{:S(2)}) async-start(f32[32,8,256]{2,1,0:T(8,128)} %pad.9.clone), calls=%async_computation.2 | async-start | bytes 524288 | tf_op jit(solution)/shard_map/all_to_all | solution.py:134
  135.7 0.1 convert_reduce_fusion.1
  135.9 0.7 fusion.26
  136.6 12.5 %all-to-all-done.2 = f32[32,8,256]{2,1,0:T(8,128)S(1)} async-done(((f32[32,8,256]{2,1,0:T(8,128)}), f32[32,8,256]{2,1,0:T(8,128)S(1)}, u32[]{:S(2)}, u32[]{:S(2)}) %all-to-all-start.2) | async-done | bytes 262176 | tf_op jit(solution)/shard_map/all_to_all | solution.py:134
  149.2 2.3 gather_fusion
  151.5 0.6 reduce.19
  152.1 0.1 copy.55
  153.5 0.1 copy.56
  153.7 11.7 %custom-call.16 = f32[1,128,128]{2,1,0:T(8,128)S(1)} custom-call(f32[1,128,128]{2,1,0:T(8,128)S(1)} %cholesky.114), custom_call_target="Cholesky" | custom-call | tf_op jit(solution)/shard_map/jit(cholesky)/cholesky | solution.py:78
  165.4 9.8 %custom-call.17 = f32[1,1,128,128]{2,3,1,0:T(8,128)S(1)} custom-call(f32[1,1,128,128]{3,2,1,0:T(8,128)S(1)} %get-tuple-element.39), custom_call_target="InvertDiagBlocksLowerTriangular" | custom-call | tf_op jit(solution)/shard_map/jit(cholesky)/cholesky | solution.py:78
  175.3 0.2 fusion.8
  175.5 0.3 fusion.2
  175.7 11.7 %custom-call.18 = f32[1,128,128]{2,1,0:T(8,128)S(1)} custom-call(f32[1,128,128]{2,1,0:T(8,128)S(1)} %fusion.2), custom_call_target="Cholesky" | custom-call | tf_op jit(solution)/shard_map/jit(cholesky)/cholesky | solution.py:78
  187.8 0.6 compare_reduce_fusion
  189.8 4.0 %while.1 = (s32[]{:T(128)}, f32[1,256,256]{1,2,0:T(8,128)S(1)}, s32[2,2]{1,0:T(2,128)S(1)}, f32[2,1,128,128]{3,2,1,0:T(8,128)S(1)}, s32[]{:T(128)}) while((s32[]{:T(128)}, f32[1,256,256]{1,2,0:T(8,128)S(1)}, s32[2,2]{1,0:T(2,128)S(1)}, f32[2,1,128,128]{3,2,1,0:T(8,128)S(1)}, s32[]{:T(128)}) %tuple.31), condition=%wide.while_cond, body=%wide.while_body.sunk | while | flops 2 | bytes 393325 | solution.py:80
  189.8 0.6 fusion.38
  190.4 1.3 constant_dynamic-slice_fusion.7
  191.8 0.6 fusion.38
  192.4 1.3 constant_dynamic-slice_fusion.7
  193.9 19.9 %custom-call.19 = f32[1,2,128,128]{2,3,1,0:T(8,128)S(1)} custom-call(f32[1,2,128,128]{3,2,1,0:T(8,128)S(1)} %bitcast.115), custom_call_target="InvertDiagBlocksLowerTriangular" | custom-call | tf_op jit(solution)/shard_map/triangular_solve | solution.py:80
  213.8 0.3 fusion.7
  214.0 0.4 fusion.1
  214.4 0.3 convolution_bitcast_fusion.2
  214.8 1.3 convolution_multiply_fusion
  216.1 5.1 %all_to_all.35 = f32[16,2,1,8,256]{4,3,0,2,1:T(8,128)S(1)} all-to-all(f32[16,2,1,8,256]{4,3,0,2,1:T(8,128)S(1)} %copy.62), channel_id=1, replica_groups=mesh['pipe'=8,'dp_0'=2,'dp_1'=8,'dp_2'=2] {'dp_2'}, dimensions={1} | all-to-all | bytes 524288 | tf_op jit(solution)/shard_map/all_to_all | solution.py:48
  221.2 13.1 %all_to_all.36 = f32[16,2,1,8,256]{4,3,1,2,0:T(8,128)S(1)} all-to-all(f32[16,2,1,8,256]{4,3,1,2,0:T(8,128)S(1)} %copy.63), channel_id=1, replica_groups=mesh['pipe'=8,'dp_0'=2,'dp_1'=8,'dp_2'=2] {'dp_0','dp_1'}, dimensions={0} | all-to-all | bytes 524288 | tf_op jit(solution)/shard_map/all_to_all | solution.py:48
  234.3 1.3 broadcast_in_dim.20
  235.6 3.6 %all-to-all-start.5 = ((f32[8,24,8,256]{3,1,2,0:T(8,128)}), f32[8,24,8,256]{3,1,2,0:T(8,128)S(1)}, u32[]{:S(2)}, u32[]{:S(2)}) async-start(f32[8,24,8,256]{3,1,2,0:T(8,128)} %broadcast_in_dim.20), calls=%async_computation.5 | async-start | bytes 3145728 | tf_op jit(solution)/shard_map/all_to_all | solution.py:28
  239.3 18.9 %all-to-all-done.5 = f32[8,24,8,256]{3,1,2,0:T(8,128)S(1)} async-done(((f32[8,24,8,256]{3,1,2,0:T(8,128)}), f32[8,24,8,256]{3,1,2,0:T(8,128)S(1)}, u32[]{:S(2)}, u32[]{:S(2)}) %all-to-all-start.5) | async-done | bytes 1572896 | tf_op jit(solution)/shard_map/all_to_all | solution.py:28
  258.2 0.1 copy.65
  258.3 0.6 fusion.17
  259.0 5.8 %all-gather = f32[24,8,256]{2,1,0:T(8,128)} all-gather(f32[12,8,256]{2,1,0:T(8,128)S(1)} %copy.66), channel_id=2, replica_groups=mesh['pipe'=8,'dp_0'=2,'dp_1'=8,'dp_2'=2] {'dp_0'}, dimensions={0}, use_global_device_ids=true | all-gather | bytes 294912 | tf_op jit(solution)/shard_map/all_gather | solution.py:61
  264.8 36.0 %all-gather.4.cloned.1.call-done = f32[16,12,8,256]{3,2,1,0:T(8,128)} async-done(((f32[2,12,8,256]{3,2,1,0:T(8,128)}), f32[16,12,8,256]{3,2,1,0:T(8,128)}) %all-gather.4.cloned.1.call-update) | async-done | bytes 1572880 | tf_op jit(solution)/shard_map/all_gather | solution.py:61
  300.9 22.4 %all-gather.6.cloned.1.call-done = f32[32,12,8,256]{3,2,1,0:T(8,128)} async-done(((f32[16,12,8,256]{3,2,1,0:T(8,128)}), f32[32,12,8,256]{3,2,1,0:T(8,128)}) %all-gather.6.cloned.1.call-update) | async-done | bytes 3145744 | tf_op jit(solution)/shard_map/all_gather | solution.py:61
  323.3 2.3 copy.67
  325.6 4.1 %fusion.27 = f32[12,256,128]{2,1,0:T(8,128)} fusion(f32[12,256,256]{2,1,0:T(8,128)S(1)} %bitcast.105, f32[12,256,128]{2,1,0:T(8,128)S(1)} %bitcast.102), kind=kOutput, calls=%fused_computation.70 | convolution fusion | flops 1207959552 | bytes 6291456 | tf_op jit(solution)/shard_map/brk,bkc->brc/dot_general | solution.py:144
  (45 shorter events, 1.4 us)
Async XLA Ops:
  7.2 318.5 %copy-start = (f32[3072,128]{1,0:T(8,128)S(1)}, f32[3072,128]{1,0:T(8,128)}, u32[]{:S(2)}) copy-start(f32[3072,128]{1,0:T(8,128)} %param.4) | copy-start | bytes 4718596
  108.8 5.2 %copy-start.2 = (s32[8,12]{1,0:T(8,128)S(1)}, s32[8,12]{1,0:T(8,128)}, u32[]{:S(2)}) copy-start(s32[8,12]{1,0:T(8,128)} %param.5) | copy-start | bytes 1156
  109.7 14.6 %all-to-all-start.1 = ((f32[8,8,3072]{2,1,0:T(8,128)}), f32[8,8,3072]{2,1,0:T(8,128)S(1)}, u32[]{:S(2)}, u32[]{:S(2)}) async-start(f32[8,8,3072]{2,1,0:T(8,128)} %broadcast_in_dim.16), calls=%async_computation.1 | async-start | bytes 1572864 | tf_op jit(solution)/shard_map/all_to_all | solution.py:28
  125.8 23.3 %all-to-all-start.2 = ((f32[32,8,256]{2,1,0:T(8,128)}), f32[32,8,256]{2,1,0:T(8,128)S(1)}, u32[]{:S(2)}, u32[]{:S(2)}) async-start(f32[32,8,256]{2,1,0:T(8,128)} %pad.9.clone), calls=%async_computation.2 | async-start | bytes 524288 | tf_op jit(solution)/shard_map/all_to_all | solution.py:134
  234.2 1.4 copy-start.1
  235.6 22.5 %all-to-all-start.5 = ((f32[8,24,8,256]{3,1,2,0:T(8,128)}), f32[8,24,8,256]{3,1,2,0:T(8,128)S(1)}, u32[]{:S(2)}, u32[]{:S(2)}) async-start(f32[8,24,8,256]{3,1,2,0:T(8,128)} %broadcast_in_dim.20), calls=%async_computation.5 | async-start | bytes 3145728 | tf_op jit(solution)/shard_map/all_to_all | solution.py:28
  239.2 61.7 %all-gather.4.cloned.1.call-start = ((), (), s32[]{:S(2)}) async-start(), calls=%async_computation.6 | async-start | bytes 1769472 | tf_op jit(solution)/shard_map/all_gather | solution.py:61
  264.8 58.6 %all-gather.6.cloned.1.call-start = ((), (), s32[]{:S(2)}) async-start(), calls=%async_computation.7 | async-start | bytes 4718592 | tf_op jit(solution)/shard_map/all_gather | solution.py:61
Sparse Core Ops, SparseCore 0:
  264.9 35.9 all-gather.3
  302.7 20.6 all-gather.5
where the time goes:
time: 337 us
  blocking collectives  109 us (32%)
  waiting for transfers between devices  100 us (30%)
  other arithmetic  57.6 us (17%)
  local copies, waits for them, and re-layouts  24.6 us (7%)
  starting transfers between devices  17.8 us (5%)
  between operations  16.8 us (5%)
  matrix products  10.4 us (3%)
    all_to_all x1, blocking collectives, summed_on_arrival(): tiles = lax.all_to_all(in_blocks(value, dim, count), axis, 0, 0, tiled=True)  85.4 us
    all_gather x2, waiting for transfers between devices, gather_in_order(): tiles = lax.all_gather(tiles, axes[k], axis=0, tiled=True)  58.5 us
    another operation x6, other arithmetic, invert_blocks(): cholesky_lower = jnp.linalg.cholesky(shifted)  33.9 us
    all_to_all x2, waiting for transfers between devices, from_everyone(): lax.all_to_all(jnp.broadcast_to(value[None], (count, *value.shape)), axis...  28.9 us
    another operation x3, other arithmetic, invert_blocks(): lax.linalg.triangular_solve(cholesky_lower, identity_stack, left_side=Tru...  19.9 us
    all_to_all x2, blocking collectives, turned_blocks(): result = lax.all_to_all(result, axes[k], k, k, tiled=True)  18.1 us
    all_to_all x1, waiting for transfers between devices, shards(): lax.all_to_all(padded, DP, split_axis=0, concat_axis=1, tiled=True)  12.5 us
    all_to_all x1, starting transfers between devices, shards(): lax.all_to_all(padded, DP, split_axis=0, concat_axis=1, tiled=True)  9.87 us
  transfers between devices with their start and end apart: 5, of which 5 were waited for; matrix products, arithmetic and copies ran while one was open for 0% of the time, Pallas kernels for 0%

commit v1 on v0

v1 whole, which is shorter than its diff:
```python
import functools

import jax
import jax.numpy as jnp
from jax import lax
from jax.experimental import pallas as pl
from jax.experimental.pallas import tpu as pltpu
from jax.sharding import Mesh
from jax.sharding import PartitionSpec as P

BLK = 256
HALF = BLK // 2
SUB = 8
NB = 12
PER_CORE = NB // 2
HOST = 24
TALL = HALF + SUB
N_Z = 8
DP = ("x", "z", "c")
damping_ratio = 0.1
VMEM = pltpu.VMEM
f32 = jnp.float32


def holds(z, c):
    return (z % 4) != jnp.where(c == 0, 3, 1)


def rank(z, c):
    return (z // 4) * 3 + jnp.where(c == 0, z % 4, (z % 4 + 1) // 2)


def held_by(z, c):
    return z % 4 != (3 if c == 0 else 1)


def place_of(zc_step):
    into = [
        (z * 2 + c, (z + zc_step) % N_Z * 2 + c)
        for z in range(N_Z)
        for c in range(2)
        if held_by((z + zc_step) % N_Z, c)
    ]
    out = [
        (z * 2 + c, (z + zc_step) % N_Z * 2 + c)
        for z in range(N_Z)
        for c in range(2)
        if held_by(z, c)
    ]
    return into, out


def grids():
    return (
        lax.broadcasted_iota(jnp.int32, (HALF, HALF), 0),
        lax.broadcasted_iota(jnp.int32, (HALF, HALF), 1),
    )


def store_packed(ref, upper, cross, lower):
    i, j = grids()
    ref[0:HALF, 0:HALF] = cross
    ref[0:HALF, HALF:BLK] = jnp.where(i >= j, upper, lower)
    ref[HALF:TALL, 0:HALF] = jnp.broadcast_to(
        jnp.sum(jnp.where(i == j, lower, 0.0), axis=0, keepdims=True), (SUB, HALF)
    )
    ref[HALF:TALL, HALF:BLK] = jnp.zeros((SUB, HALF), f32)


def unpacked(value):
    i, j = grids()
    cross, mixed, diagonal = value[0:HALF, 0:HALF], value[0:HALF, HALF:BLK], value[HALF : HALF + 1, 0:HALF]
    turned = mixed.T
    upper = jnp.where(i >= j, mixed, turned)
    lower = jnp.where(i < j, mixed, jnp.where(i > j, turned, diagonal))
    return upper, cross, lower


def gram_kernel(here_ref, acts_ref, out_ref, *, other):
    c = here_ref[2]
    first = (1 - c if other else c) * PER_CORE
    for k in range(PER_CORE):
        start = pl.multiple_of((first + k) * BLK, BLK)
        part = acts_ref[:, pl.ds(start, BLK)]
        total = lax.dot_general(part, part, (((0,), (0,)), ((), ())), preferred_element_type=f32)
        store_packed(
            out_ref.at[k], total[0:HALF, 0:HALF], total[HALF:BLK, 0:HALF], total[HALF:BLK, HALF:BLK]
        )


def parts_kernel(here_ref, mine_ref, got_ref, *out_refs):
    z, c = here_ref[1], here_ref[2]
    for step in range(N_Z):
        target = (z + step) % N_Z
        k = rank(target, c)

        @pl.when(holds(target, c))
        def _():
            out_refs[step][...] = mine_ref[k] + got_ref[k]


def small_inverse(d):
    d = dict(d)

    def at(i, j):
        return d[(i, j)] if i >= j else d[(j, i)]

    for k in range(SUB):
        inv = 1.0 / at(k, k)
        b = {i: at(i, k) * inv for i in range(SUB) if i != k}
        for i in b:
            for j in b:
                if j <= i:
                    d[(i, j)] = d[(i, j)] - b[i] * at(j, k)
        for i in b:
            d[(max(i, k), min(i, k))] = b[i]
        d[(k, k)] = -inv
    return d


def summed(terms):
    while len(terms) > 1:
        terms = [terms[n] + terms[n + 1] for n in range(0, len(terms), 2)]
    return terms[0]


def take_out(tiles, t):
    first = SUB * t
    lane = lax.broadcasted_iota(jnp.int32, (SUB, HALF), 1)
    line = lax.broadcasted_iota(jnp.int32, (SUB, HALF), 0)
    inside = (lane >= first) & (lane < first + SUB)
    pivot = tiles[t]

    def spread(v):
        return jnp.broadcast_to(v, (SUB, HALF))

    minus = small_inverse(
        {
            (i, j): spread(pivot[i : i + 1, first + j : first + j + 1])
            for i in range(SUB)
            for j in range(i + 1)
        }
    )
    rows = [
        jnp.where(lane == first + j, 1.0, jnp.where(inside, 0.0, spread(pivot[j : j + 1, :])))
        for j in range(SUB)
    ]
    new = [
        summed([minus[(max(i, j), min(i, j))] * rows[j] for j in range(SUB)]) for i in range(SUB)
    ]
    result = []
    for v, tile in enumerate(tiles):
        if v == t:
            own = jnp.zeros((SUB, HALF), f32)
            for j in range(SUB):
                own = jnp.where(line == j, -new[j], own)
            result.append(own)
        else:
            update = summed([spread(tile[:, first + j : first + j + 1]) * new[j] for j in range(SUB)])
            result.append(jnp.where(inside, 0.0, tile) + update)
    return result


def half_inverse(value):
    tiles = [value[SUB * v : SUB * v + SUB] for v in range(HALF // SUB)]
    for t in range(len(tiles)):
        tiles = take_out(tiles, t)
    return jnp.concatenate(tiles, axis=0)


def dot(a, b, dims=((1,), (0,))):
    return lax.dot_general(
        a, b, (dims, ((), ())), precision=lax.Precision.HIGHEST, preferred_element_type=f32
    )


def invert_kernel(here_ref, a_ref, b_ref, out_ref, *, all_tokens):
    z, c = here_ref[1], here_ref[2]

    @pl.when(holds(z, c))
    def _():
        upper, cross, lower = unpacked((a_ref[...] + b_ref[...]) * (1.0 / all_tokens))
        i, j = grids()
        same = i == j
        trace = jnp.sum(
            jnp.sum(jnp.where(same, upper + lower, 0.0), axis=0, keepdims=True), axis=1, keepdims=True
        )
        damping = damping_ratio * trace / BLK
        shift = jnp.where(same, damping, 0.0)
        first = half_inverse(upper + shift)
        w = dot(cross, first)
        second = half_inverse(lower + shift - dot(w, cross, ((1,), (1,))))
        x = dot(second, w)
        store_packed(out_ref, first + dot(w, x, ((0,), (0,))), -x, second)


def unpack_kernel(here_ref, *refs):
    in_refs, full_ref, rows_ref = refs[: 2 * N_Z], refs[2 * N_Z], refs[2 * N_Z + 1]
    x, z, c = here_ref[0], here_ref[1], here_ref[2]
    start = pl.multiple_of(((x * N_Z + z) * 2 + c) * SUB, SUB)
    for n, ref in enumerate(in_refs):
        core = c if n < N_Z else 1 - c
        source = (z + N_Z - n % N_Z) % N_Z
        block = core * PER_CORE + rank(source, core)

        @pl.when(holds(source, core))
        def _():
            upper, cross, lower = unpacked(ref[...])
            full_ref[block, 0:HALF, 0:HALF] = upper
            full_ref[block, 0:HALF, HALF:BLK] = cross.T
            full_ref[block, HALF:BLK, 0:HALF] = cross
            full_ref[block, HALF:BLK, HALF:BLK] = lower
            rows_ref[block] = full_ref[block, pl.ds(start, SUB), :]


def hosted_kernel(here_ref, owner_ref, rows_ref, out_ref):
    me = here_ref[3]
    out_ref[...] = jnp.zeros(out_ref.shape, f32)
    sections, nblocks = owner_ref.shape

    def section(s, count):
        for b in range(nblocks):
            mine = owner_ref[s, b] == me

            @pl.when(mine)
            def _(count=count):
                out_ref[count] = rows_ref[s, b]

            count = count + mine.astype(jnp.int32)
        return count

    lax.fori_loop(0, sections, section, jnp.int32(0))


def call(kernel, out_shape, n_smem, n_vmem):
    out_specs = jax.tree.map(lambda _: pl.BlockSpec(memory_space=VMEM), out_shape)
    return pl.pallas_call(
        kernel,
        out_shape=out_shape,
        in_specs=[pl.BlockSpec(memory_space=pltpu.SMEM)] * n_smem
        + [pl.BlockSpec(memory_space=VMEM)] * n_vmem,
        out_specs=out_specs,
        compiler_params=pltpu.CompilerParams(vmem_limit_bytes=40 * 1024 * 1024),
    )


def shape(*dims):
    return jax.ShapeDtypeStruct(dims, f32)


STEPS = (1, 7, 2, 6, 3, 5, 4)


def shards(acts, grad, owner_of):
    section_count = lax.axis_size("pipe")
    all_tokens = acts.shape[1] * lax.axis_size(DP)
    here = jnp.stack([lax.axis_index(a) for a in ("x", "z", "c", "pipe")]).astype(jnp.int32)
    features = acts[0]
    packed = shape(PER_CORE, TALL, BLK)
    theirs = call(functools.partial(gram_kernel, other=True), packed, 1, 1)(here, features)
    got = lax.ppermute(theirs, "c", [(0, 1), (1, 0)])
    mine = call(functools.partial(gram_kernel, other=False), packed, 1, 1)(here, features)
    parts = call(parts_kernel, [shape(TALL, BLK)] * N_Z, 1, 2)(here, mine, got)
    total = parts[0]
    arrived = [lax.ppermute(parts[step], ("z", "c"), place_of(step)[0]) for step in STEPS]
    for piece in arrived:
        total = total + piece
    other = lax.ppermute(total, "x", [(0, 1), (1, 0)])
    inverse = call(
        functools.partial(invert_kernel, all_tokens=all_tokens), shape(TALL, BLK), 1, 2
    )(here, total, other)
    near = {0: inverse}
    far = {0: lax.ppermute(inverse, "c", [(0, 1), (1, 0)])}
    for step in STEPS:
        near[step] = lax.ppermute(inverse, ("z", "c"), place_of(step)[1])
        far[step] = lax.ppermute(near[step], "c", [(0, 1), (1, 0)])
    gathered = [near[k] for k in range(N_Z)] + [far[k] for k in range(N_Z)]
    full, rows = call(unpack_kernel, [shape(NB, BLK, BLK), shape(NB, SUB, BLK)], 1, 2 * N_Z)(
        here, *gathered
    )
    everyone = lax.all_to_all(
        jnp.broadcast_to(rows[None], (section_count, *rows.shape)), "pipe", 0, 0, tiled=True
    )
    precond = jnp.einsum(
        "brk,bkc->brc", full, grad.reshape(NB, BLK, grad.shape[1]), precision=lax.Precision.HIGHEST
    )
    held = call(hosted_kernel, shape(HOST, SUB, BLK), 2, 1)(here, owner_of, everyone)
    return (precond.reshape(grad.shape), held[None])


def solution(mesh):
    torus = Mesh(mesh.devices.reshape(mesh.shape["pipe"], 2, N_Z, 2), ("pipe", "x", "z", "c"))
    placed = (P("pipe", DP, None), P("pipe", DP), P())
    return jax.shard_map(
        shards,
        mesh=torus,
        in_specs=placed,
        out_specs=(P("pipe", DP), P("pipe", None, DP, None)),
        check_vma=False,
    )
```

time: 337 us -> 126 us (0.37)
  blocking collectives: 109 us -> 0 us
  waiting for transfers between devices: 100 us -> 28.8 us
  other arithmetic: 57.6 us -> 0.16 us
  starting transfers between devices: 17.8 us -> 67.5 us
  local copies, waits for them, and re-layouts: 24.6 us -> 4.11 us
  Pallas kernels: 0 us -> 18 us
  between operations: 16.8 us -> 0.89 us
  matrix products: 10.4 us -> 5.93 us
    all_to_all x3 -> x0, blocking collectives: 104 us -> none  [the longest x1 85.4 us: summed_on_arrival(): tiles = lax.all_to_all(in_blocks(value, dim, count), axis, 0, 0, tiled=True)]
    ppermute x0 -> x24, starting transfers between devices: none -> 62.4 us  [the longest x7 24.2 us: shards(): lax.ppermute(parts[step], ('z', 'c'), place_of(step)[0])]
    all_gather x2 -> x0, waiting for transfers between devices: 58.5 us -> none  [gather_in_order(): tiles = lax.all_gather(tiles, axes[k], axis=0, tiled=True)]
    another operation x9 -> x1, other arithmetic: 53.9 us -> 0.08 us  [shards(): jnp.stack([lax.axis_index(a) for a in ('x', 'z', 'c', 'pipe')])]
    all_to_all x3 -> x1, waiting for transfers between devices: 41.4 us -> 6.63 us  [shards(): lax.all_to_all(jnp.broadcast_to(rows[None], (section_count, *rows.shape))...]
    ppermute x0 -> x24, waiting for transfers between devices: none -> 22.2 us  [the longest x7 11.9 us: shards(): lax.ppermute(parts[step], ('z', 'c'), place_of(step)[0])]
    pallas_call x0 -> x6, Pallas kernels: none -> 18 us  [the longest x1 11.1 us: shards(): call(functools.partial(invert_kernel, all_tokens=all_tokens), shape(TALL,...]
    all_to_all x3 -> x1, starting transfers between devices: 17.7 us -> 5.12 us  [shards(): lax.all_to_all(jnp.broadcast_to(rows[None], (section_count, *rows.shape))...]
  transfers between devices with their start and end apart: 5 -> 25, of which waited for: 5 -> 9; matrix products, arithmetic and copies ran while one was open for 0% -> 5% of each run, Pallas kernels for 0% -> 1%
where the time goes in v1:
time: 126 us; the launch traced here: 125 us
  starting transfers between devices  67.5 us (54%)
  waiting for transfers between devices  28.8 us (23%)
  Pallas kernels  18 us (14%)
  matrix products  5.93 us (5%)
  local copies, waits for them, and re-layouts  4.11 us (3%)
    ppermute x7, starting transfers between devices, shards(): lax.ppermute(parts[step], ('z', 'c'), place_of(step)[0])  24.2 us
    ppermute x7, starting transfers between devices, shards(): near[step] = lax.ppermute(inverse, ('z', 'c'), place_of(step)[1])  20.7 us
    ppermute x7, waiting for transfers between devices, shards(): lax.ppermute(parts[step], ('z', 'c'), place_of(step)[0])  11.9 us
    pallas_call x1, Pallas kernels, shards(): call(functools.partial(invert_kernel, all_tokens=all_tokens), shape(TALL,...  11.1 us
    ppermute x7, starting transfers between devices, shards(): far[step] = lax.ppermute(near[step], 'c', [(0, 1), (1, 0)])  9.77 us
    all_to_all x1, waiting for transfers between devices, shards(): lax.all_to_all(jnp.broadcast_to(rows[None], (section_count, *rows.shape))...  6.63 us
    dot_general x1, matrix products, shards(): jnp.einsum('brk,bkc->brc', full, grad.reshape(NB, BLK, grad.shape[1]), pr...  5.93 us
    all_to_all x1, starting transfers between devices, shards(): lax.all_to_all(jnp.broadcast_to(rows[None], (section_count, *rows.shape))...  5.12 us
  transfers between devices with their start and end apart: 25, of which 9 were waited for; matrix products, arithmetic and copies ran while one was open for 5% of the time, Pallas kernels for 1%

profile of v1, /device:TPU:1, one launch (start us, length us, event | category | flops | bytes accessed | tf_op | source)
XLA Modules:
  0.0 125.4 jit_solution(4581684964810479719)
XLA Ops:
  0.6 0.0 copy-start
  0.7 0.1 pad_add_fusion.here_ref
  0.7 1.5 %copy-done.1 = bf16[1,256,3072]{2,1,0:T(8,128)(2,1)S(1)} copy-done((bf16[1,256,3072]{2,1,0:T(8,128)(2,1)S(1)}, bf16[1,256,3072]{2,1,0:T(8,128)(2,1)}, u32[]{:S(2)}) %copy-start.1) | copy-done | bytes 1572888
  2.2 1.0 shard_map.51
  3.2 3.3 %collective-permute-start = (f32[6,136,256]{2,1,0:T(8,128)S(1)}, f32[6,136,256]{2,1,0:T(8,128)S(1)}, u32[]{:S(2)}, u32[]{:S(2)}) collective-permute-start(f32[6,136,256]{2,1,0:T(8,128)S(1)} %shard_map.51), channel_id=1, source_target_pairs={{0,1},{1,0},{2,3},{3,2},{4,5},{5,4},{6,7},{7,6},{8,9},{9,8},{10,11... | collective-permute-start | bytes 2506760 | tf_op jit(solution)/shard_map/ppermute | solution.py:261
  6.6 1.0 shard_map.50.mine_ref
  7.5 1.0 collective-permute-done.got_ref
  8.5 0.8 shard_map.52
  9.3 1.3 %collective-permute-start.1 = (f32[136,256]{1,0:T(8,128)S(1)}, f32[136,256]{1,0:T(8,128)S(1)}, u32[]{:S(2)}, u32[]{:S(2)}) collective-permute-start(f32[136,256]{1,0:T(8,128)S(1)} %get-tuple-element.13), channel_id=1, source_target_pairs={{0,2},{2,4},{3,5},{5,7},{6,8},{7,9},{8,10},{10,12},{11,13},{13,15}... | collective-permute-start | bytes 417800 | tf_op jit(solution)/shard_map/ppermute | solution.py:265
  10.6 6.4 %collective-permute-start.2 = (f32[136,256]{1,0:T(8,128)S(1)}, f32[136,256]{1,0:T(8,128)S(1)}, u32[]{:S(2)}, u32[]{:S(2)}) collective-permute-start(f32[136,256]{1,0:T(8,128)S(1)} %get-tuple-element.14), channel_id=1, source_target_pairs={{1,15},{2,0},{3,1},{4,2},{6,4},{7,5},{9,7},{10,8},{11,9},{12,10},{... | collective-permute-start | bytes 417800 | tf_op jit(solution)/shard_map/ppermute | solution.py:265
  17.0 1.9 %collective-permute-start.3 = (f32[136,256]{1,0:T(8,128)S(1)}, f32[136,256]{1,0:T(8,128)S(1)}, u32[]{:S(2)}, u32[]{:S(2)}) collective-permute-start(f32[136,256]{1,0:T(8,128)S(1)} %get-tuple-element.15), channel_id=1, source_target_pairs={{0,4},{1,5},{3,7},{4,8},{5,9},{6,10},{8,12},{9,13},{11,15},{12,0},... | collective-permute-start | bytes 417800 | tf_op jit(solution)/shard_map/ppermute | solution.py:265
  18.9 5.5 %collective-permute-start.4 = (f32[136,256]{1,0:T(8,128)S(1)}, f32[136,256]{1,0:T(8,128)S(1)}, u32[]{:S(2)}, u32[]{:S(2)}) collective-permute-start(f32[136,256]{1,0:T(8,128)S(1)} %get-tuple-element.16), channel_id=1, source_target_pairs={{0,12},{1,13},{3,15},{4,0},{5,1},{6,2},{8,4},{9,5},{11,7},{12,8},{... | collective-permute-start | bytes 417800 | tf_op jit(solution)/shard_map/ppermute | solution.py:265
  24.4 1.9 %collective-permute-start.5 = (f32[136,256]{1,0:T(8,128)S(1)}, f32[136,256]{1,0:T(8,128)S(1)}, u32[]{:S(2)}, u32[]{:S(2)}) collective-permute-start(f32[136,256]{1,0:T(8,128)S(1)} %get-tuple-element.17), channel_id=1, source_target_pairs={{1,7},{2,8},{3,9},{4,10},{6,12},{7,13},{9,15},{10,0},{11,1},{12,2}... | collective-permute-start | bytes 417800 | tf_op jit(solution)/shard_map/ppermute | solution.py:265
  26.4 1.3 %collective-permute-start.6 = (f32[136,256]{1,0:T(8,128)S(1)}, f32[136,256]{1,0:T(8,128)S(1)}, u32[]{:S(2)}, u32[]{:S(2)}) collective-permute-start(f32[136,256]{1,0:T(8,128)S(1)} %get-tuple-element.18), channel_id=1, source_target_pairs={{0,10},{2,12},{3,13},{5,15},{6,0},{7,1},{8,2},{10,4},{11,5},{13,7}... | collective-permute-start | bytes 417800 | tf_op jit(solution)/shard_map/ppermute | solution.py:265
  27.7 5.9 %collective-permute-start.7 = (f32[136,256]{1,0:T(8,128)S(1)}, f32[136,256]{1,0:T(8,128)S(1)}, u32[]{:S(2)}, u32[]{:S(2)}) collective-permute-start(f32[136,256]{1,0:T(8,128)S(1)} %get-tuple-element.19), channel_id=1, source_target_pairs={{0,8},{1,9},{2,10},{4,12},{5,13},{7,15},{8,0},{9,1},{10,2},{12,4},... | collective-permute-start | bytes 417800 | tf_op jit(solution)/shard_map/ppermute | solution.py:265
  33.6 11.8 %collective-permute-done.5 = f32[136,256]{1,0:T(8,128)S(1)} collective-permute-done((f32[136,256]{1,0:T(8,128)S(1)}, f32[136,256]{1,0:T(8,128)S(1)}, u32[]{:S(2)}, u32[]{:S(2)}) %collective-permute-start.5) | collective-permute-done | bytes 139296 | tf_op jit(solution)/shard_map/ppermute | solution.py:265
  45.5 0.1 add_add_fusion.a_ref
  45.5 2.8 %collective-permute-start.8 = (f32[136,256]{1,0:T(8,128)S(1)}, f32[136,256]{1,0:T(8,128)S(1)}, u32[]{:S(2)}, u32[]{:S(2)}) collective-permute-start(f32[136,256]{1,0:T(8,128)S(1)} %add_add_fusion.a_ref), channel_id=1, source_target_pairs={{0,16},{16,0},{1,17},{17,1},{2,18},{18,2},{3,19},{19,3},{4,20},{20... | collective-permute-start | bytes 417800 | tf_op jit(solution)/shard_map/ppermute | solution.py:268
  48.4 3.6 %collective-permute-done.8.b_ref = f32[136,256]{1,0:T(8,128)S(1)} collective-permute-done((f32[136,256]{1,0:T(8,128)S(1)}, f32[136,256]{1,0:T(8,128)S(1)}, u32[]{:S(2)}, u32[]{:S(2)}) %collective-permute-start.8) | collective-permute-done | bytes 139296 | tf_op jit(solution)/shard_map/ppermute | solution.py:268
  52.0 11.1 %shard_map.53.refs_0_ = f32[136,256]{1,0:T(8,128)S(1)} custom-call(s32[4]{0:T(128)S(1)} %pad_add_fusion.here_ref, f32[136,256]{1,0:T(8,128)S(1)} %add_add_fusion.a_ref, f32[136,256]{1,0:T(8,128)S(1)} %collective-permute-done.8.b_ref), custom_call_target="tpu_custom_call" | custom-call | tf_op jit(solution)/shard_map/pallas_call | solution.py:269
  63.1 1.5 %collective-permute-start.16 = (f32[136,256]{1,0:T(8,128)S(1)}, f32[136,256]{1,0:T(8,128)S(1)}, u32[]{:S(2)}, u32[]{:S(2)}) collective-permute-start(f32[136,256]{1,0:T(8,128)S(1)} %shard_map.53.refs_0_), channel_id=1, source_target_pairs={{0,1},{1,0},{2,3},{3,2},{4,5},{5,4},{6,7},{7,6},{8,9},{9,8},{10,11... | collective-permute-start | bytes 417800 | tf_op jit(solution)/shard_map/ppermute | solution.py:273
  64.6 1.3 %collective-permute-start.15 = (f32[136,256]{1,0:T(8,128)S(1)}, f32[136,256]{1,0:T(8,128)S(1)}, u32[]{:S(2)}, u32[]{:S(2)}) collective-permute-start(f32[136,256]{1,0:T(8,128)S(1)} %shard_map.53.refs_0_), channel_id=1, source_target_pairs={{0,14},{1,15},{2,0},{4,2},{5,3},{7,5},{8,6},{9,7},{10,8},{12,10},{... | collective-permute-start | bytes 417800 | tf_op jit(solution)/shard_map/ppermute | solution.py:275
  65.9 4.2 %collective-permute-start.14 = (f32[136,256]{1,0:T(8,128)S(1)}, f32[136,256]{1,0:T(8,128)S(1)}, u32[]{:S(2)}, u32[]{:S(2)}) collective-permute-start(f32[136,256]{1,0:T(8,128)S(1)} %shard_map.53.refs_0_), channel_id=1, source_target_pairs={{0,12},{1,13},{2,14},{4,0},{5,1},{7,3},{8,4},{9,5},{10,6},{12,8},{... | collective-permute-start | bytes 417800 | tf_op jit(solution)/shard_map/ppermute | solution.py:275
  70.1 1.9 %collective-permute-start.13 = (f32[136,256]{1,0:T(8,128)S(1)}, f32[136,256]{1,0:T(8,128)S(1)}, u32[]{:S(2)}, u32[]{:S(2)}) collective-permute-start(f32[136,256]{1,0:T(8,128)S(1)} %shard_map.53.refs_0_), channel_id=1, source_target_pairs={{0,10},{1,11},{2,12},{4,14},{5,15},{7,1},{8,2},{9,3},{10,4},{12,6}... | collective-permute-start | bytes 417800 | tf_op jit(solution)/shard_map/ppermute | solution.py:275
  72.1 4.3 %collective-permute-start.12 = (f32[136,256]{1,0:T(8,128)S(1)}, f32[136,256]{1,0:T(8,128)S(1)}, u32[]{:S(2)}, u32[]{:S(2)}) collective-permute-start(f32[136,256]{1,0:T(8,128)S(1)} %shard_map.53.refs_0_), channel_id=1, source_target_pairs={{0,8},{1,9},{2,10},{4,12},{5,13},{7,15},{8,0},{9,1},{10,2},{12,4},... | collective-permute-start | bytes 417800 | tf_op jit(solution)/shard_map/ppermute | solution.py:275
  76.4 5.2 %collective-permute-start.11 = (f32[136,256]{1,0:T(8,128)S(1)}, f32[136,256]{1,0:T(8,128)S(1)}, u32[]{:S(2)}, u32[]{:S(2)}) collective-permute-start(f32[136,256]{1,0:T(8,128)S(1)} %shard_map.53.refs_0_), channel_id=1, source_target_pairs={{0,6},{1,7},{2,8},{4,10},{5,11},{7,13},{8,14},{9,15},{10,0},{12,2}... | collective-permute-start | bytes 417800 | tf_op jit(solution)/shard_map/ppermute | solution.py:275
  81.6 1.9 %collective-permute-start.10 = (f32[136,256]{1,0:T(8,128)S(1)}, f32[136,256]{1,0:T(8,128)S(1)}, u32[]{:S(2)}, u32[]{:S(2)}) collective-permute-start(f32[136,256]{1,0:T(8,128)S(1)} %shard_map.53.refs_0_), channel_id=1, source_target_pairs={{0,4},{1,5},{2,6},{4,8},{5,9},{7,11},{8,12},{9,13},{10,14},{12,0},... | collective-permute-start | bytes 417800 | tf_op jit(solution)/shard_map/ppermute | solution.py:275
  83.5 1.9 %collective-permute-start.9 = (f32[136,256]{1,0:T(8,128)S(1)}, f32[136,256]{1,0:T(8,128)S(1)}, u32[]{:S(2)}, u32[]{:S(2)}) collective-permute-start(f32[136,256]{1,0:T(8,128)S(1)} %shard_map.53.refs_0_), channel_id=1, source_target_pairs={{0,2},{1,3},{2,4},{4,6},{5,7},{7,9},{8,10},{9,11},{10,12},{12,14},... | collective-permute-start | bytes 417800 | tf_op jit(solution)/shard_map/ppermute | solution.py:275
  85.5 1.8 %collective-permute-start.23 = (f32[136,256]{1,0:T(8,128)S(1)}, f32[136,256]{1,0:T(8,128)S(1)}, u32[]{:S(2)}, u32[]{:S(2)}) collective-permute-start(f32[136,256]{1,0:T(8,128)S(1)} %collective-permute-done.15.refs_7_), channel_id=1, source_target_pairs={{0,1},{1,0},{2,3},{3,2},{4,5},{5,4},{6,7},{7,6},{8,9},{9,8},{10,11... | collective-permute-start | bytes 417800 | tf_op jit(solution)/shard_map/ppermute | solution.py:276
  87.2 2.1 %collective-permute-start.22 = (f32[136,256]{1,0:T(8,128)S(1)}, f32[136,256]{1,0:T(8,128)S(1)}, u32[]{:S(2)}, u32[]{:S(2)}) collective-permute-start(f32[136,256]{1,0:T(8,128)S(1)} %collective-permute-done.14.refs_6_), channel_id=1, source_target_pairs={{0,1},{1,0},{2,3},{3,2},{4,5},{5,4},{6,7},{7,6},{8,9},{9,8},{10,11... | collective-permute-start | bytes 417800 | tf_op jit(solution)/shard_map/ppermute | solution.py:276
  89.3 3.3 %collective-permute-start.21 = (f32[136,256]{1,0:T(8,128)S(1)}, f32[136,256]{1,0:T(8,128)S(1)}, u32[]{:S(2)}, u32[]{:S(2)}) collective-permute-start(f32[136,256]{1,0:T(8,128)S(1)} %collective-permute-done.13.refs_5_), channel_id=1, source_target_pairs={{0,1},{1,0},{2,3},{3,2},{4,5},{5,4},{6,7},{7,6},{8,9},{9,8},{10,11... | collective-permute-start | bytes 417800 | tf_op jit(solution)/shard_map/ppermute | solution.py:276
  92.7 4.4 %collective-permute-done.10.refs_2_ = f32[136,256]{1,0:T(8,128)S(1)} collective-permute-done((f32[136,256]{1,0:T(8,128)S(1)}, f32[136,256]{1,0:T(8,128)S(1)}, u32[]{:S(2)}, u32[]{:S(2)}) %collective-permute-start.10) | collective-permute-done | bytes 139296 | tf_op jit(solution)/shard_map/ppermute | solution.py:275
  97.1 1.9 %collective-permute-start.20 = (f32[136,256]{1,0:T(8,128)S(1)}, f32[136,256]{1,0:T(8,128)S(1)}, u32[]{:S(2)}, u32[]{:S(2)}) collective-permute-start(f32[136,256]{1,0:T(8,128)S(1)} %collective-permute-done.12.refs_4_), channel_id=1, source_target_pairs={{0,1},{1,0},{2,3},{3,2},{4,5},{5,4},{6,7},{7,6},{8,9},{9,8},{10,11... | collective-permute-start | bytes 417800 | tf_op jit(solution)/shard_map/ppermute | solution.py:276
  99.1 0.0 collective-permute-start.19
  99.1 0.5 collective-permute-start.18
  99.6 0.1 collective-permute-start.17
  99.7 0.4 collective-permute-done.20.refs_12_
  100.1 0.4 collective-permute-done.19.refs_11_
  100.4 0.2 collective-permute-done.18.refs_10_
  100.6 0.3 collective-permute-done.17.refs_9_
  100.9 1.9 %shard_map.54 = (f32[12,256,256]{2,1,0:T(8,128)S(1)}, f32[12,8,256]{2,1,0:T(8,128)S(1)}) custom-call(s32[4]{0:T(128)S(1)} %pad_add_fusion.here_ref, f32[136,256]{1,0:T(8,128)S(1)} %shard_map.53.refs_0_, f32[136,256]{1,0:T(8,128)S(1)} %collective-permute-done.9.refs_1_, f32[136,256]{1,0:T(8,128)S(1)} %collective-permute-done.10.refs_2_, ...), custom_call_target="tpu_custom_call" | custom-call | tf_op jit(solution)/shard_map/pallas_call | solution.py:278
  102.9 1.6 %copy-done.2 = f32[12,256,256]{2,1,0:T(8,128)} copy-done((f32[12,256,256]{2,1,0:T(8,128)}, f32[12,256,256]{2,1,0:T(8,128)S(1)}, u32[]{:S(2)}) %copy-start.2) | copy-done | bytes 3145752
  104.5 1.0 broadcast_in_dim.4
  105.5 5.1 %all-to-all-start = ((f32[8,12,8,256]{3,2,1,0:T(8,128)}), f32[8,12,8,256]{3,2,1,0:T(8,128)S(1)}, u32[]{:S(2)}, u32[]{:S(2)}) async-start(f32[8,12,8,256]{3,2,1,0:T(8,128)} %broadcast_in_dim.4), calls=%async_computation | async-start | bytes 1572864 | tf_op jit(solution)/shard_map/all_to_all | solution.py:281
  110.6 0.0 copy-start.3
  110.6 5.9 %fusion = f32[12,256,128]{2,1,0:T(8,128)} fusion(f32[12,256,256]{2,1,0:T(8,128)} %copy-done.2, f32[12,256,128]{2,1,0:T(8,128)S(1)} %bitcast.10), kind=kOutput, calls=%fused_computation.2 | convolution fusion | flops 1207959552 | bytes 6291456 | tf_op jit(solution)/shard_map/brk,bkc->brc/dot_general | solution.py:284
  116.5 6.6 %all-to-all-done.rows_ref = f32[8,12,8,256]{3,2,1,0:T(8,128)S(1)} async-done(((f32[8,12,8,256]{3,2,1,0:T(8,128)}), f32[8,12,8,256]{3,2,1,0:T(8,128)S(1)}, u32[]{:S(2)}, u32[]{:S(2)}) %all-to-all-start) | async-done | bytes 786464 | tf_op jit(solution)/shard_map/all_to_all | solution.py:281
  123.2 2.2 %shard_map.55 = f32[24,8,256]{2,1,0:T(8,128)} custom-call(s32[4]{0:T(128)S(1)} %pad_add_fusion.here_ref, s32[8,12]{1,0:T(8,128)S(1)} %copy-done.3, f32[8,12,8,256]{3,2,1,0:T(8,128)S(1)} %all-to-all-done.rows_ref), custom_call_target="tpu_custom_call" | custom-call | tf_op jit(solution)/shard_map/pallas_call | solution.py:287
  (20 shorter events, 0.0 us)
Async XLA Ops:
  0.6 110.0 %copy-start = (f32[3072,128]{1,0:T(8,128)S(1)}, f32[3072,128]{1,0:T(8,128)}, u32[]{:S(2)}) copy-start(f32[3072,128]{1,0:T(8,128)} %param.4) | copy-start | bytes 4718596
  0.7 1.5 %copy-start.1 = (bf16[1,256,3072]{2,1,0:T(8,128)(2,1)S(1)}, bf16[1,256,3072]{2,1,0:T(8,128)(2,1)}, u32[]{:S(2)}) copy-start(bf16[1,256,3072]{2,1,0:T(8,128)(2,1)} %param.3) | copy-start | bytes 4718596
  3.2 5.3 %collective-permute-start = (f32[6,136,256]{2,1,0:T(8,128)S(1)}, f32[6,136,256]{2,1,0:T(8,128)S(1)}, u32[]{:S(2)}, u32[]{:S(2)}) collective-permute-start(f32[6,136,256]{2,1,0:T(8,128)S(1)} %shard_map.51), channel_id=1, source_target_pairs={{0,1},{1,0},{2,3},{3,2},{4,5},{5,4},{6,7},{7,6},{8,9},{9,8},{10,11... | collective-permute-start | bytes 2506760 | tf_op jit(solution)/shard_map/ppermute | solution.py:261
  9.3 17.0 %collective-permute-start.1 = (f32[136,256]{1,0:T(8,128)S(1)}, f32[136,256]{1,0:T(8,128)S(1)}, u32[]{:S(2)}, u32[]{:S(2)}) collective-permute-start(f32[136,256]{1,0:T(8,128)S(1)} %get-tuple-element.13), channel_id=1, source_target_pairs={{0,2},{2,4},{3,5},{5,7},{6,8},{7,9},{8,10},{10,12},{11,13},{13,15}... | collective-permute-start | bytes 417800 | tf_op jit(solution)/shard_map/ppermute | solution.py:265
  10.6 17.0 %collective-permute-start.2 = (f32[136,256]{1,0:T(8,128)S(1)}, f32[136,256]{1,0:T(8,128)S(1)}, u32[]{:S(2)}, u32[]{:S(2)}) collective-permute-start(f32[136,256]{1,0:T(8,128)S(1)} %get-tuple-element.14), channel_id=1, source_target_pairs={{1,15},{2,0},{3,1},{4,2},{6,4},{7,5},{9,7},{10,8},{11,9},{12,10},{... | collective-permute-start | bytes 417800 | tf_op jit(solution)/shard_map/ppermute | solution.py:265
  17.0 16.6 %collective-permute-start.3 = (f32[136,256]{1,0:T(8,128)S(1)}, f32[136,256]{1,0:T(8,128)S(1)}, u32[]{:S(2)}, u32[]{:S(2)}) collective-permute-start(f32[136,256]{1,0:T(8,128)S(1)} %get-tuple-element.15), channel_id=1, source_target_pairs={{0,4},{1,5},{3,7},{4,8},{5,9},{6,10},{8,12},{9,13},{11,15},{12,0},... | collective-permute-start | bytes 417800 | tf_op jit(solution)/shard_map/ppermute | solution.py:265
  18.9 14.7 %collective-permute-start.4 = (f32[136,256]{1,0:T(8,128)S(1)}, f32[136,256]{1,0:T(8,128)S(1)}, u32[]{:S(2)}, u32[]{:S(2)}) collective-permute-start(f32[136,256]{1,0:T(8,128)S(1)} %get-tuple-element.16), channel_id=1, source_target_pairs={{0,12},{1,13},{3,15},{4,0},{5,1},{6,2},{8,4},{9,5},{11,7},{12,8},{... | collective-permute-start | bytes 417800 | tf_op jit(solution)/shard_map/ppermute | solution.py:265
  24.4 21.0 %collective-permute-start.5 = (f32[136,256]{1,0:T(8,128)S(1)}, f32[136,256]{1,0:T(8,128)S(1)}, u32[]{:S(2)}, u32[]{:S(2)}) collective-permute-start(f32[136,256]{1,0:T(8,128)S(1)} %get-tuple-element.17), channel_id=1, source_target_pairs={{1,7},{2,8},{3,9},{4,10},{6,12},{7,13},{9,15},{10,0},{11,1},{12,2}... | collective-permute-start | bytes 417800 | tf_op jit(solution)/shard_map/ppermute | solution.py:265
  26.4 19.1 %collective-permute-start.6 = (f32[136,256]{1,0:T(8,128)S(1)}, f32[136,256]{1,0:T(8,128)S(1)}, u32[]{:S(2)}, u32[]{:S(2)}) collective-permute-start(f32[136,256]{1,0:T(8,128)S(1)} %get-tuple-element.18), channel_id=1, source_target_pairs={{0,10},{2,12},{3,13},{5,15},{6,0},{7,1},{8,2},{10,4},{11,5},{13,7}... | collective-permute-start | bytes 417800 | tf_op jit(solution)/shard_map/ppermute | solution.py:265
  27.7 17.8 %collective-permute-start.7 = (f32[136,256]{1,0:T(8,128)S(1)}, f32[136,256]{1,0:T(8,128)S(1)}, u32[]{:S(2)}, u32[]{:S(2)}) collective-permute-start(f32[136,256]{1,0:T(8,128)S(1)} %get-tuple-element.19), channel_id=1, source_target_pairs={{0,8},{1,9},{2,10},{4,12},{5,13},{7,15},{8,0},{9,1},{10,2},{12,4},... | collective-permute-start | bytes 417800 | tf_op jit(solution)/shard_map/ppermute | solution.py:265
  45.5 6.4 %collective-permute-start.8 = (f32[136,256]{1,0:T(8,128)S(1)}, f32[136,256]{1,0:T(8,128)S(1)}, u32[]{:S(2)}, u32[]{:S(2)}) collective-permute-start(f32[136,256]{1,0:T(8,128)S(1)} %add_add_fusion.a_ref), channel_id=1, source_target_pairs={{0,16},{16,0},{1,17},{17,1},{2,18},{18,2},{3,19},{19,3},{4,20},{20... | collective-permute-start | bytes 417800 | tf_op jit(solution)/shard_map/ppermute | solution.py:268
  63.1 13.3 %collective-permute-start.16 = (f32[136,256]{1,0:T(8,128)S(1)}, f32[136,256]{1,0:T(8,128)S(1)}, u32[]{:S(2)}, u32[]{:S(2)}) collective-permute-start(f32[136,256]{1,0:T(8,128)S(1)} %shard_map.53.refs_0_), channel_id=1, source_target_pairs={{0,1},{1,0},{2,3},{3,2},{4,5},{5,4},{6,7},{7,6},{8,9},{9,8},{10,11... | collective-permute-start | bytes 417800 | tf_op jit(solution)/shard_map/ppermute | solution.py:273
  64.6 16.9 %collective-permute-start.15 = (f32[136,256]{1,0:T(8,128)S(1)}, f32[136,256]{1,0:T(8,128)S(1)}, u32[]{:S(2)}, u32[]{:S(2)}) collective-permute-start(f32[136,256]{1,0:T(8,128)S(1)} %shard_map.53.refs_0_), channel_id=1, source_target_pairs={{0,14},{1,15},{2,0},{4,2},{5,3},{7,5},{8,6},{9,7},{10,8},{12,10},{... | collective-permute-start | bytes 417800 | tf_op jit(solution)/shard_map/ppermute | solution.py:275
  65.9 17.6 %collective-permute-start.14 = (f32[136,256]{1,0:T(8,128)S(1)}, f32[136,256]{1,0:T(8,128)S(1)}, u32[]{:S(2)}, u32[]{:S(2)}) collective-permute-start(f32[136,256]{1,0:T(8,128)S(1)} %shard_map.53.refs_0_), channel_id=1, source_target_pairs={{0,12},{1,13},{2,14},{4,0},{5,1},{7,3},{8,4},{9,5},{10,6},{12,8},{... | collective-permute-start | bytes 417800 | tf_op jit(solution)/shard_map/ppermute | solution.py:275
  70.1 15.3 %collective-permute-start.13 = (f32[136,256]{1,0:T(8,128)S(1)}, f32[136,256]{1,0:T(8,128)S(1)}, u32[]{:S(2)}, u32[]{:S(2)}) collective-permute-start(f32[136,256]{1,0:T(8,128)S(1)} %shard_map.53.refs_0_), channel_id=1, source_target_pairs={{0,10},{1,11},{2,12},{4,14},{5,15},{7,1},{8,2},{9,3},{10,4},{12,6}... | collective-permute-start | bytes 417800 | tf_op jit(solution)/shard_map/ppermute | solution.py:275
  72.1 15.2 %collective-permute-start.12 = (f32[136,256]{1,0:T(8,128)S(1)}, f32[136,256]{1,0:T(8,128)S(1)}, u32[]{:S(2)}, u32[]{:S(2)}) collective-permute-start(f32[136,256]{1,0:T(8,128)S(1)} %shard_map.53.refs_0_), channel_id=1, source_target_pairs={{0,8},{1,9},{2,10},{4,12},{5,13},{7,15},{8,0},{9,1},{10,2},{12,4},... | collective-permute-start | bytes 417800 | tf_op jit(solution)/shard_map/ppermute | solution.py:275
  76.4 12.9 %collective-permute-start.11 = (f32[136,256]{1,0:T(8,128)S(1)}, f32[136,256]{1,0:T(8,128)S(1)}, u32[]{:S(2)}, u32[]{:S(2)}) collective-permute-start(f32[136,256]{1,0:T(8,128)S(1)} %shard_map.53.refs_0_), channel_id=1, source_target_pairs={{0,6},{1,7},{2,8},{4,10},{5,11},{7,13},{8,14},{9,15},{10,0},{12,2}... | collective-permute-start | bytes 417800 | tf_op jit(solution)/shard_map/ppermute | solution.py:275
  81.6 15.6 %collective-permute-start.10 = (f32[136,256]{1,0:T(8,128)S(1)}, f32[136,256]{1,0:T(8,128)S(1)}, u32[]{:S(2)}, u32[]{:S(2)}) collective-permute-start(f32[136,256]{1,0:T(8,128)S(1)} %shard_map.53.refs_0_), channel_id=1, source_target_pairs={{0,4},{1,5},{2,6},{4,8},{5,9},{7,11},{8,12},{9,13},{10,14},{12,0},... | collective-permute-start | bytes 417800 | tf_op jit(solution)/shard_map/ppermute | solution.py:275
  83.5 15.6 %collective-permute-start.9 = (f32[136,256]{1,0:T(8,128)S(1)}, f32[136,256]{1,0:T(8,128)S(1)}, u32[]{:S(2)}, u32[]{:S(2)}) collective-permute-start(f32[136,256]{1,0:T(8,128)S(1)} %shard_map.53.refs_0_), channel_id=1, source_target_pairs={{0,2},{1,3},{2,4},{4,6},{5,7},{7,9},{8,10},{9,11},{10,12},{12,14},... | collective-permute-start | bytes 417800 | tf_op jit(solution)/shard_map/ppermute | solution.py:275
  85.5 13.6 %collective-permute-start.23 = (f32[136,256]{1,0:T(8,128)S(1)}, f32[136,256]{1,0:T(8,128)S(1)}, u32[]{:S(2)}, u32[]{:S(2)}) collective-permute-start(f32[136,256]{1,0:T(8,128)S(1)} %collective-permute-done.15.refs_7_), channel_id=1, source_target_pairs={{0,1},{1,0},{2,3},{3,2},{4,5},{5,4},{6,7},{7,6},{8,9},{9,8},{10,11... | collective-permute-start | bytes 417800 | tf_op jit(solution)/shard_map/ppermute | solution.py:276
  87.2 12.3 %collective-permute-start.22 = (f32[136,256]{1,0:T(8,128)S(1)}, f32[136,256]{1,0:T(8,128)S(1)}, u32[]{:S(2)}, u32[]{:S(2)}) collective-permute-start(f32[136,256]{1,0:T(8,128)S(1)} %collective-permute-done.14.refs_6_), channel_id=1, source_target_pairs={{0,1},{1,0},{2,3},{3,2},{4,5},{5,4},{6,7},{7,6},{8,9},{9,8},{10,11... | collective-permute-start | bytes 417800 | tf_op jit(solution)/shard_map/ppermute | solution.py:276
  89.3 10.3 %collective-permute-start.21 = (f32[136,256]{1,0:T(8,128)S(1)}, f32[136,256]{1,0:T(8,128)S(1)}, u32[]{:S(2)}, u32[]{:S(2)}) collective-permute-start(f32[136,256]{1,0:T(8,128)S(1)} %collective-permute-done.13.refs_5_), channel_id=1, source_target_pairs={{0,1},{1,0},{2,3},{3,2},{4,5},{5,4},{6,7},{7,6},{8,9},{9,8},{10,11... | collective-permute-start | bytes 417800 | tf_op jit(solution)/shard_map/ppermute | solution.py:276
  97.1 2.9 %collective-permute-start.20 = (f32[136,256]{1,0:T(8,128)S(1)}, f32[136,256]{1,0:T(8,128)S(1)}, u32[]{:S(2)}, u32[]{:S(2)}) collective-permute-start(f32[136,256]{1,0:T(8,128)S(1)} %collective-permute-done.12.refs_4_), channel_id=1, source_target_pairs={{0,1},{1,0},{2,3},{3,2},{4,5},{5,4},{6,7},{7,6},{8,9},{9,8},{10,11... | collective-permute-start | bytes 417800 | tf_op jit(solution)/shard_map/ppermute | solution.py:276
  99.1 1.4 %collective-permute-start.19 = (f32[136,256]{1,0:T(8,128)S(1)}, f32[136,256]{1,0:T(8,128)S(1)}, u32[]{:S(2)}, u32[]{:S(2)}) collective-permute-start(f32[136,256]{1,0:T(8,128)S(1)} %collective-permute-done.11.refs_3_), channel_id=1, source_target_pairs={{0,1},{1,0},{2,3},{3,2},{4,5},{5,4},{6,7},{7,6},{8,9},{9,8},{10,11... | collective-permute-start | bytes 417800 | tf_op jit(solution)/shard_map/ppermute | solution.py:276
  99.1 1.6 %collective-permute-start.18 = (f32[136,256]{1,0:T(8,128)S(1)}, f32[136,256]{1,0:T(8,128)S(1)}, u32[]{:S(2)}, u32[]{:S(2)}) collective-permute-start(f32[136,256]{1,0:T(8,128)S(1)} %collective-permute-done.10.refs_2_), channel_id=1, source_target_pairs={{0,1},{1,0},{2,3},{3,2},{4,5},{5,4},{6,7},{7,6},{8,9},{9,8},{10,11... | collective-permute-start | bytes 417800 | tf_op jit(solution)/shard_map/ppermute | solution.py:276
  99.6 1.4 %collective-permute-start.17 = (f32[136,256]{1,0:T(8,128)S(1)}, f32[136,256]{1,0:T(8,128)S(1)}, u32[]{:S(2)}, u32[]{:S(2)}) collective-permute-start(f32[136,256]{1,0:T(8,128)S(1)} %collective-permute-done.9.refs_1_), channel_id=1, source_target_pairs={{0,1},{1,0},{2,3},{3,2},{4,5},{5,4},{6,7},{7,6},{8,9},{9,8},{10,11... | collective-permute-start | bytes 417800 | tf_op jit(solution)/shard_map/ppermute | solution.py:276
  102.9 1.6 %copy-start.2 = (f32[12,256,256]{2,1,0:T(8,128)}, f32[12,256,256]{2,1,0:T(8,128)S(1)}, u32[]{:S(2)}) copy-start(f32[12,256,256]{2,1,0:T(8,128)S(1)} %get-tuple-element.20) | copy-start | bytes 9437188
  105.5 17.7 %all-to-all-start = ((f32[8,12,8,256]{3,2,1,0:T(8,128)}), f32[8,12,8,256]{3,2,1,0:T(8,128)S(1)}, u32[]{:S(2)}, u32[]{:S(2)}) async-start(f32[8,12,8,256]{3,2,1,0:T(8,128)} %broadcast_in_dim.4), calls=%async_computation | async-start | bytes 1572864 | tf_op jit(solution)/shard_map/all_to_all | solution.py:281
  110.6 12.6 %copy-start.3 = (s32[8,12]{1,0:T(8,128)S(1)}, s32[8,12]{1,0:T(8,128)}, u32[]{:S(2)}) copy-start(s32[8,12]{1,0:T(8,128)} %owner_ref.1) | copy-start | bytes 1156

commit v2 on v1

--- a/solution.py
+++ b/solution.py
@@ -18,36 +18,41 @@
 N_Z = 8
 DP = ("x", "z", "c")
 damping_ratio = 0.1
+LIMIT = 8 * 1024 * 1024
 VMEM = pltpu.VMEM
 f32 = jnp.float32
 
 
-def holds(z, c):
-    return (z % 4) != jnp.where(c == 0, 3, 1)
-
-
-def rank(z, c):
-    return (z // 4) * 3 + jnp.where(c == 0, z % 4, (z % 4 + 1) // 2)
-
-
-def held_by(z, c):
-    return z % 4 != (3 if c == 0 else 1)
-
-
-def place_of(zc_step):
-    into = [
-        (z * 2 + c, (z + zc_step) % N_Z * 2 + c)
-        for z in range(N_Z)
-        for c in range(2)
-        if held_by((z + zc_step) % N_Z, c)
-    ]
-    out = [
-        (z * 2 + c, (z + zc_step) % N_Z * 2 + c)
-        for z in range(N_Z)
-        for c in range(2)
-        if held_by(z, c)
-    ]
-    return into, out
+def own_slot(here_ref):
+    return (here_ref[1] + 4 * here_ref[0]) % N_Z
+
+
+def holds(slot, c):
+    return (slot % 4) != jnp.where(c == 0, 3, 1)
+
+
+def rank(slot, c):
+    return (slot // 4) * 3 + jnp.where(c == 0, slot % 4, (slot % 4 + 1) // 2)
+
+
+OFFSETS = (0, 1, -1, 2, -2, 3, 4, 5)
+
+
+def along_z(value, step):
+    return lax.ppermute(value, "z", [(z, (z + step) % N_Z) for z in range(N_Z)])
+
+
+def across_x(value):
+    return lax.ppermute(value, "x", [(0, 1), (1, 0)])
+
+
+def to_twin(value):
+    pairs = [(x * N_Z + z, (1 - x) * N_Z + (z + 4) % N_Z) for x in range(2) for z in range(N_Z)]
+    return lax.ppermute(value, ("x", "z"), pairs)
+
+
+def across_cores(value):
+    return lax.ppermute(value, "c", [(0, 1), (1, 0)])
 
 
 def grids():
@@ -89,14 +94,14 @@
 
 
 def parts_kernel(here_ref, mine_ref, got_ref, *out_refs):
-    z, c = here_ref[1], here_ref[2]
-    for step in range(N_Z):
-        target = (z + step) % N_Z
-        k = rank(target, c)
-
-        @pl.when(holds(target, c))
+    c, own = here_ref[2], own_slot(here_ref)
+    for offset, out_ref in zip(OFFSETS, out_refs):
+        slot = (own + N_Z + offset) % N_Z
+        k = rank(slot, c)
+
+        @pl.when(holds(slot, c))
         def _():
-            out_refs[step][...] = mine_ref[k] + got_ref[k]
+            out_ref[...] = mine_ref[k] + got_ref[k]
 
 
 def small_inverse(d):
@@ -175,9 +180,7 @@
 
 
 def invert_kernel(here_ref, a_ref, b_ref, out_ref, *, all_tokens):
-    z, c = here_ref[1], here_ref[2]
-
-    @pl.when(holds(z, c))
+    @pl.when(holds(own_slot(here_ref), here_ref[2]))
     def _():
         upper, cross, lower = unpacked((a_ref[...] + b_ref[...]) * (1.0 / all_tokens))
         i, j = grids()
@@ -194,42 +197,90 @@
         store_packed(out_ref, first + dot(w, x, ((0,), (0,))), -x, second)
 
 
-def unpack_kernel(here_ref, *refs):
-    in_refs, full_ref, rows_ref = refs[: 2 * N_Z], refs[2 * N_Z], refs[2 * N_Z + 1]
-    x, z, c = here_ref[0], here_ref[1], here_ref[2]
-    start = pl.multiple_of(((x * N_Z + z) * 2 + c) * SUB, SUB)
-    for n, ref in enumerate(in_refs):
-        core = c if n < N_Z else 1 - c
-        source = (z + N_Z - n % N_Z) % N_Z
-        block = core * PER_CORE + rank(source, core)
-
-        @pl.when(holds(source, core))
+def unpack_blocks(here_ref, in_refs, full_ref, rows_ref, block_ref, done, *, other, first):
+    c, own = here_ref[2], own_slot(here_ref)
+    core = 1 - c if other else c
+    start = pl.multiple_of(((here_ref[0] * N_Z + here_ref[1]) * 2 + c) * SUB, SUB)
+
+    def leave(k):
+        return pltpu.make_async_copy(block_ref.at[k], full_ref.at[core * PER_CORE + k], done.at[k])
+
+    for offset, ref in zip(OFFSETS, in_refs):
+        slot = (own + N_Z + offset) % N_Z
+        k = rank(slot, core)
+
+        @pl.when(holds(slot, core))
         def _():
             upper, cross, lower = unpacked(ref[...])
-            full_ref[block, 0:HALF, 0:HALF] = upper
-            full_ref[block, 0:HALF, HALF:BLK] = cross.T
-            full_ref[block, HALF:BLK, 0:HALF] = cross
-            full_ref[block, HALF:BLK, HALF:BLK] = lower
-            rows_ref[block] = full_ref[block, pl.ds(start, SUB), :]
-
-
-def hosted_kernel(here_ref, owner_ref, rows_ref, out_ref):
-    me = here_ref[3]
-    out_ref[...] = jnp.zeros(out_ref.shape, f32)
-    sections, nblocks = owner_ref.shape
-
-    def section(s, count):
-        for b in range(nblocks):
-            mine = owner_ref[s, b] == me
-
-            @pl.when(mine)
-            def _(count=count):
-                out_ref[count] = rows_ref[s, b]
-
-            count = count + mine.astype(jnp.int32)
-        return count
-
-    lax.fori_loop(0, sections, section, jnp.int32(0))
+            block_ref[k, 0:HALF, 0:HALF] = upper
+            block_ref[k, 0:HALF, HALF:BLK] = cross.T
+            block_ref[k, HALF:BLK, 0:HALF] = cross
+            block_ref[k, HALF:BLK, HALF:BLK] = lower
+            leave(k).start()
+            rows_ref[first + k] = block_ref[k, pl.ds(start, SUB), :]
+
+    return [leave(k) for k in range(PER_CORE)]
+
+
+def unpack_own_kernel(here_ref, *refs):
+    full_ref, rows_ref, block_ref, done = refs[N_Z:]
+    copies = unpack_blocks(
+        here_ref, refs[:N_Z], full_ref, rows_ref, block_ref, done, other=False, first=0
+    )
+    for copy in copies:
+        copy.wait()
+
+
+def unpack_other_kernel(here_ref, *refs):
+    own_rows_ref, _, full_ref, sent_ref, block_ref, rows_ref, done, gone = refs[N_Z:]
+    c = here_ref[2]
+    for k in range(PER_CORE):
+        rows_ref[c * PER_CORE + k] = own_rows_ref[k]
+    copies = unpack_blocks(
+        here_ref, refs[:N_Z], full_ref, rows_ref, block_ref, done, other=True, first=(1 - c) * PER_CORE
+    )
+    sends = [
+        pltpu.make_async_copy(rows_ref, sent_ref.at[s], gone.at[s]) for s in range(sent_ref.shape[0])
+    ]
+    for copy in sends:
+        copy.start()
+    for copy in copies + sends:
+        copy.wait()
+
+
+def precond_kernel(here_ref, owner_ref, full_ref, grad_ref, out_ref, table_ref):
+    out_ref[...] = dot(full_ref[0], grad_ref[...])
+
+    @pl.when(pl.program_id(0) == 0)
+    def _():
+        sections, nblocks = owner_ref.shape
+
+        def clear(j, carry):
+            table_ref[j] = -1
+            return carry
+
+        def section(s, count):
+            for b in range(nblocks):
+                hit = owner_ref[s, b] == here_ref[3]
+
+                @pl.when(hit)
+                def _(count=count):
+                    table_ref[count] = s * nblocks + b
+
+                count = count + hit.astype(jnp.int32)
+            return count
+
+        lax.fori_loop(0, HOST, clear, 0)
+        lax.fori_loop(0, sections, section, jnp.int32(0))
+
+
+def hosted_kernel(table_ref, rows_ref, out_ref):
+    nblocks = rows_ref.shape[1]
+    for j in range(HOST):
+        source = table_ref[j]
+        at = jnp.maximum(source, 0)
+        rows = rows_ref[at // nblocks, at % nblocks]
+        out_ref[j] = jnp.where(source >= 0, rows, 0.0)
 
 
 def call(kernel, out_shape, n_smem, n_vmem):
@@ -240,7 +291,7 @@
         in_specs=[pl.BlockSpec(memory_space=pltpu.SMEM)] * n_smem
         + [pl.BlockSpec(memory_space=VMEM)] * n_vmem,
         out_specs=out_specs,
-        compiler_params=pltpu.CompilerParams(vmem_limit_bytes=40 * 1024 * 1024),
+        compiler_params=pltpu.CompilerParams(vmem_limit_bytes=LIMIT),
     )
 
 
@@ -248,7 +299,54 @@
     return jax.ShapeDtypeStruct(dims, f32)
 
 
-STEPS = (1, 7, 2, 6, 3, 5, 4)
+IN_HBM = pl.BlockSpec(memory_space=pltpu.HBM)
+IN_VMEM = pl.BlockSpec(memory_space=VMEM)
+IN_SMEM = pl.BlockSpec(memory_space=pltpu.SMEM)
+
+
+def unpack_own(here, values):
+    return pl.pallas_call(
+        unpack_own_kernel,
+        out_shape=[shape(NB, BLK, BLK), shape(PER_CORE, SUB, BLK)],
+        in_specs=[IN_SMEM] + [IN_VMEM] * N_Z,
+        out_specs=[IN_HBM, IN_VMEM],
+        scratch_shapes=[VMEM((PER_CORE, BLK, BLK), f32), pltpu.SemaphoreType.DMA((PER_CORE,))],
+        compiler_params=pltpu.CompilerParams(vmem_limit_bytes=LIMIT),
+    )(here, *values)
+
+
+def unpack_other(here, values, own_rows, full, copies):
+    return pl.pallas_call(
+        unpack_other_kernel,
+        out_shape=[shape(NB, BLK, BLK), shape(copies, NB, SUB, BLK)],
+        in_specs=[IN_SMEM] + [IN_VMEM] * (N_Z + 1) + [IN_HBM],
+        out_specs=[IN_HBM, IN_HBM],
+        scratch_shapes=[
+            VMEM((PER_CORE, BLK, BLK), f32),
+            VMEM((NB, SUB, BLK), f32),
+            pltpu.SemaphoreType.DMA((PER_CORE,)),
+            pltpu.SemaphoreType.DMA((copies,)),
+        ],
+        input_output_aliases={2 + N_Z: 0},
+        compiler_params=pltpu.CompilerParams(vmem_limit_bytes=LIMIT),
+    )(here, *values, own_rows, full)
+
+
+def preconditioned(here, owner_of, full, grad):
+    rows, columns = grad.shape
+    part = pl.BlockSpec((BLK, columns), lambda i: (i, 0))
+    scalars = pl.BlockSpec(memory_space=pltpu.SMEM)
+    return pl.pallas_call(
+        precond_kernel,
+        grid=(rows // BLK,),
+        out_shape=[shape(rows, columns), jax.ShapeDtypeStruct((HOST,), jnp.int32)],
+        in_specs=[scalars, scalars, pl.BlockSpec((1, BLK, BLK), lambda i: (i, 0, 0)), part],
+        out_specs=[part, scalars],
+        cost_estimate=pl.CostEstimate(
+            flops=12 * rows * BLK * columns, bytes_accessed=16 * rows * columns, transcendentals=0
+        ),
+        compiler_params=pltpu.CompilerParams(vmem_limit_bytes=LIMIT),
+    )(here, owner_of, full, grad)
 
 
 def shards(acts, grad, owner_of):
@@ -257,35 +355,34 @@
     here = jnp.stack([lax.axis_index(a) for a in ("x", "z", "c", "pipe")]).astype(jnp.int32)
     features = acts[0]
     packed = shape(PER_CORE, TALL, BLK)
+    one = shape(TALL, BLK)
     theirs = call(functools.partial(gram_kernel, other=True), packed, 1, 1)(here, features)
-    got = lax.ppermute(theirs, "c", [(0, 1), (1, 0)])
+    got = across_cores(theirs)
     mine = call(functools.partial(gram_kernel, other=False), packed, 1, 1)(here, features)
-    parts = call(parts_kernel, [shape(TALL, BLK)] * N_Z, 1, 2)(here, mine, got)
-    total = parts[0]
-    arrived = [lax.ppermute(parts[step], ("z", "c"), place_of(step)[0]) for step in STEPS]
-    for piece in arrived:
-        total = total + piece
-    other = lax.ppermute(total, "x", [(0, 1), (1, 0)])
-    inverse = call(
-        functools.partial(invert_kernel, all_tokens=all_tokens), shape(TALL, BLK), 1, 2
-    )(here, total, other)
-    near = {0: inverse}
-    far = {0: lax.ppermute(inverse, "c", [(0, 1), (1, 0)])}
-    for step in STEPS:
-        near[step] = lax.ppermute(inverse, ("z", "c"), place_of(step)[1])
-        far[step] = lax.ppermute(near[step], "c", [(0, 1), (1, 0)])
-    gathered = [near[k] for k in range(N_Z)] + [far[k] for k in range(N_Z)]
-    full, rows = call(unpack_kernel, [shape(NB, BLK, BLK), shape(NB, SUB, BLK)], 1, 2 * N_Z)(
-        here, *gathered
-    )
-    everyone = lax.all_to_all(
-        jnp.broadcast_to(rows[None], (section_count, *rows.shape)), "pipe", 0, 0, tiled=True
-    )
-    precond = jnp.einsum(
-        "brk,bkc->brc", full, grad.reshape(NB, BLK, grad.shape[1]), precision=lax.Precision.HIGHEST
-    )
-    held = call(hosted_kernel, shape(HOST, SUB, BLK), 2, 1)(here, owner_of, everyone)
-    return (precond.reshape(grad.shape), held[None])
+    part = dict(zip(OFFSETS, call(parts_kernel, [one] * N_Z, 1, 2)(here, mine, got)))
+
+    across = {1: across_x(part[5]), -1: across_x(part[3])}
+    far = [along_z(part[2], 2), along_z(part[-2], -2)]
+    across[0] = across_x(part[4])
+    near = [along_z(part[1] + across[1], 1), along_z(part[-1] + across[-1], -1)]
+    half = part[0] + across[0] + far[0] + far[1] + near[0] + near[1]
+    other_half = to_twin(half)
+    inverse = call(functools.partial(invert_kernel, all_tokens=all_tokens), one, 1, 2)(
+        here, half, other_half
+    )
+
+    held = {0: inverse, -1: along_z(inverse, 1), 1: along_z(inverse, -1)}
+    held[4] = across_x(inverse)
+    held[-2], held[2] = along_z(inverse, 2), along_z(inverse, -2)
+    held[3], held[5] = across_x(held[-1]), across_x(held[1])
+    gathered = lax.optimization_barrier([held[k] for k in OFFSETS])
+    passed = [across_cores(value) for value in gathered]
+    full, own_rows = unpack_own(here, gathered)
+    full, sent = unpack_other(here, passed, own_rows, full, section_count)
+    everyone = lax.all_to_all(sent, "pipe", 0, 0, tiled=True)
+    precond, table = preconditioned(here, owner_of, full, grad)
+    hosted = call(hosted_kernel, shape(HOST, SUB, BLK), 1, 1)(table, everyone)
+    return (precond, hosted[None])
 
 
 def solution(mesh):

time: 126 us -> 99.6 us (0.79)
  starting transfers between devices: 67.5 us -> 44 us
  Pallas kernels: 18 us -> 28 us
  waiting for transfers between devices: 28.8 us -> 22.6 us
  matrix products: 5.93 us -> 0 us
    ppermute x24, starting transfers between devices: 62.4 us -> 39.7 us  [the longest x8 18 us: along_z(): return lax.ppermute(value, 'z', [(z, (z + step) % N_Z) for z in range(N_Z)])]
    pallas_call x4 -> x6, Pallas kernels: 16 us -> 26 us  [the longest x1 11.3 us: shards(): call(functools.partial(invert_kernel, all_tokens=all_tokens), one, 1, 2)]
    dot_general x1 -> x0, matrix products: 5.93 us -> none  [shards(): jnp.einsum('brk,bkc->brc', full, grad.reshape(NB, BLK, grad.shape[1]), pr...]
    ppermute x24, waiting for transfers between devices: 22.2 us -> 19 us  [the longest x8 10.2 us: along_z(): return lax.ppermute(value, 'z', [(z, (z + step) % N_Z) for z in range(N_Z)])]
    all_to_all x1, waiting for transfers between devices: 6.63 us -> 3.57 us  [shards(): everyone = lax.all_to_all(sent, 'pipe', 0, 0, tiled=True)]
  transfers between devices with their start and end apart: 25 -> 25, of which waited for: 9 -> 10; matrix products, arithmetic and copies ran while one was open for 5% -> 0% of each run, Pallas kernels for 1% -> 10%
where the time goes in v2:
time: 99.6 us; the launch traced here: 99.3 us
  starting transfers between devices  44 us (44%)
  Pallas kernels  28 us (28%)
  waiting for transfers between devices  22.6 us (23%)
  local copies, waits for them, and re-layouts  3.74 us (4%)
    ppermute x8, starting transfers between devices, along_z(): return lax.ppermute(value, 'z', [(z, (z + step) % N_Z) for z in range(N_Z)])  18 us
    pallas_call x1, Pallas kernels, shards(): call(functools.partial(invert_kernel, all_tokens=all_tokens), one, 1, 2)  11.3 us
    ppermute x8, waiting for transfers between devices, along_z(): return lax.ppermute(value, 'z', [(z, (z + step) % N_Z) for z in range(N_Z)])  10.2 us
    ppermute x9, starting transfers between devices, across_cores(): return lax.ppermute(value, 'c', [(0, 1), (1, 0)])  10.1 us
    pallas_call x1, Pallas kernels, preconditioned(): pl.pallas_call(precond_kernel, grid=(rows // BLK,), out_shape=[shape(rows...  7.67 us
    ppermute x6, starting transfers between devices, across_x(): return lax.ppermute(value, 'x', [(0, 1), (1, 0)])  7.13 us
    ppermute x1, waiting for transfers between devices, to_twin(): return lax.ppermute(value, ('x', 'z'), pairs)  5.84 us
    ppermute x1, starting transfers between devices, to_twin(): return lax.ppermute(value, ('x', 'z'), pairs)  4.46 us
  transfers between devices with their start and end apart: 25, of which 10 were waited for; matrix products, arithmetic and copies ran while one was open for 0% of the time, Pallas kernels for 10%

profile of v2, /device:TPU:1, one launch (start us, length us, event | category | flops | bytes accessed | tf_op | source)
XLA Modules:
  0.0 99.3 jit_solution(17294578044502678534)
XLA Ops:
  0.6 0.1 pad_add_fusion.here_ref
  0.7 1.4 %copy-done = bf16[1,256,3072]{2,1,0:T(8,128)(2,1)S(1)} copy-done((bf16[1,256,3072]{2,1,0:T(8,128)(2,1)S(1)}, bf16[1,256,3072]{2,1,0:T(8,128)(2,1)}, u32[]{:S(2)}) %copy-start) | copy-done | bytes 1572888
  2.1 1.0 shard_map.51
  3.1 3.3 %collective-permute-start = (f32[6,136,256]{2,1,0:T(8,128)S(1)}, f32[6,136,256]{2,1,0:T(8,128)S(1)}, u32[]{:S(2)}, u32[]{:S(2)}) collective-permute-start(f32[6,136,256]{2,1,0:T(8,128)S(1)} %shard_map.51), channel_id=1, source_target_pairs={{0,1},{1,0},{2,3},{3,2},{4,5},{5,4},{6,7},{7,6},{8,9},{9,8},{10,11... | collective-permute-start | bytes 2506760 | tf_op jit(solution)/shard_map/ppermute | solution.py:55
  6.4 1.0 shard_map.50.mine_ref
  7.4 1.0 %collective-permute-done.got_ref = f32[6,136,256]{2,1,0:T(8,128)S(1)} collective-permute-done((f32[6,136,256]{2,1,0:T(8,128)S(1)}, f32[6,136,256]{2,1,0:T(8,128)S(1)}, u32[]{:S(2)}, u32[]{:S(2)}) %collective-permute-start) | collective-permute-done | bytes 835616 | tf_op jit(solution)/shard_map/ppermute | solution.py:55
  8.4 0.8 shard_map.52
  9.2 1.1 %collective-permute-start.4 = (f32[136,256]{1,0:T(8,128)S(1)}, f32[136,256]{1,0:T(8,128)S(1)}, u32[]{:S(2)}, u32[]{:S(2)}) collective-permute-start(f32[136,256]{1,0:T(8,128)S(1)} %get-tuple-element.29), channel_id=1, source_target_pairs={{0,16},{16,0},{1,17},{17,1},{2,18},{18,2},{3,19},{19,3},{4,20},{20... | collective-permute-start | bytes 417800 | tf_op jit(solution)/shard_map/ppermute | solution.py:46
  10.3 2.0 %collective-permute-start.6 = (f32[136,256]{1,0:T(8,128)S(1)}, f32[136,256]{1,0:T(8,128)S(1)}, u32[]{:S(2)}, u32[]{:S(2)}) collective-permute-start(f32[136,256]{1,0:T(8,128)S(1)} %get-tuple-element.31), channel_id=1, source_target_pairs={{0,16},{16,0},{1,17},{17,1},{2,18},{18,2},{3,19},{19,3},{4,20},{20... | collective-permute-start | bytes 417800 | tf_op jit(solution)/shard_map/ppermute | solution.py:46
  12.3 1.0 %collective-permute-start.1 = (f32[136,256]{1,0:T(8,128)S(1)}, f32[136,256]{1,0:T(8,128)S(1)}, u32[]{:S(2)}, u32[]{:S(2)}) collective-permute-start(f32[136,256]{1,0:T(8,128)S(1)} %get-tuple-element.25), channel_id=1, source_target_pairs={{0,16},{16,0},{1,17},{17,1},{2,18},{18,2},{3,19},{19,3},{4,20},{20... | collective-permute-start | bytes 417800 | tf_op jit(solution)/shard_map/ppermute | solution.py:46
  13.3 3.0 %collective-permute-start.2 = (f32[136,256]{1,0:T(8,128)S(1)}, f32[136,256]{1,0:T(8,128)S(1)}, u32[]{:S(2)}, u32[]{:S(2)}) collective-permute-start(f32[136,256]{1,0:T(8,128)S(1)} %get-tuple-element.26), channel_id=1, source_target_pairs={{0,4},{2,6},{4,8},{6,10},{8,12},{10,14},{12,0},{14,2},{1,5},{3,7},... | collective-permute-start | bytes 417800 | tf_op jit(solution)/shard_map/ppermute | solution.py:42
  16.3 3.0 %collective-permute-start.3 = (f32[136,256]{1,0:T(8,128)S(1)}, f32[136,256]{1,0:T(8,128)S(1)}, u32[]{:S(2)}, u32[]{:S(2)}) collective-permute-start(f32[136,256]{1,0:T(8,128)S(1)} %get-tuple-element.27), channel_id=1, source_target_pairs={{0,12},{2,14},{4,0},{6,2},{8,4},{10,6},{12,8},{14,10},{1,13},{3,15... | collective-permute-start | bytes 417800 | tf_op jit(solution)/shard_map/ppermute | solution.py:42
  19.3 0.8 collective-permute-start.5
  20.2 2.3 %collective-permute-start.7 = (f32[136,256]{1,0:T(8,128)S(1)}, f32[136,256]{1,0:T(8,128)S(1)}, u32[]{:S(2)}, u32[]{:S(2)}) collective-permute-start(f32[136,256]{1,0:T(8,128)S(1)} %add.26), channel_id=1, source_target_pairs={{0,14},{2,0},{4,2},{6,4},{8,6},{10,8},{12,10},{14,12},{1,15},{3,1}... | collective-permute-start | bytes 417800 | tf_op jit(solution)/shard_map/ppermute | solution.py:42
  22.5 4.6 %collective-permute-done.3 = f32[136,256]{1,0:T(8,128)S(1)} collective-permute-done((f32[136,256]{1,0:T(8,128)S(1)}, f32[136,256]{1,0:T(8,128)S(1)}, u32[]{:S(2)}, u32[]{:S(2)}) %collective-permute-start.3) | collective-permute-done | bytes 139296 | tf_op jit(solution)/shard_map/ppermute | solution.py:42
  27.1 1.4 %collective-permute-done.5 = f32[136,256]{1,0:T(8,128)S(1)} collective-permute-done((f32[136,256]{1,0:T(8,128)S(1)}, f32[136,256]{1,0:T(8,128)S(1)}, u32[]{:S(2)}, u32[]{:S(2)}) %collective-permute-start.5) | collective-permute-done | bytes 139296 | tf_op jit(solution)/shard_map/ppermute | solution.py:42
  28.5 0.6 collective-permute-done.7
  29.0 0.1 add_add_fusion.a_ref
  29.1 4.5 %collective-permute-start.8 = (f32[136,256]{1,0:T(8,128)S(1)}, f32[136,256]{1,0:T(8,128)S(1)}, u32[]{:S(2)}, u32[]{:S(2)}) collective-permute-start(f32[136,256]{1,0:T(8,128)S(1)} %add_add_fusion.a_ref), channel_id=1, source_target_pairs={{0,24},{2,26},{4,28},{6,30},{8,16},{10,18},{12,20},{14,22},{16,8},... | collective-permute-start | bytes 417800 | tf_op jit(solution)/shard_map/ppermute | solution.py:51
  33.6 5.8 %collective-permute-done.8.b_ref = f32[136,256]{1,0:T(8,128)S(1)} collective-permute-done((f32[136,256]{1,0:T(8,128)S(1)}, f32[136,256]{1,0:T(8,128)S(1)}, u32[]{:S(2)}, u32[]{:S(2)}) %collective-permute-start.8) | collective-permute-done | bytes 139296 | tf_op jit(solution)/shard_map/ppermute | solution.py:51
  39.4 11.3 %shard_map.53.refs_0_ = f32[136,256]{1,0:T(8,128)S(1)} custom-call(s32[4]{0:T(128)S(1)} %pad_add_fusion.here_ref, f32[136,256]{1,0:T(8,128)S(1)} %add_add_fusion.a_ref, f32[136,256]{1,0:T(8,128)S(1)} %collective-permute-done.8.b_ref), custom_call_target="tpu_custom_call" | custom-call | tf_op jit(solution)/shard_map/pallas_call | solution.py:370
  50.7 0.1 collective-permute-start.10
  50.8 5.2 %collective-permute-start.9 = (f32[136,256]{1,0:T(8,128)S(1)}, f32[136,256]{1,0:T(8,128)S(1)}, u32[]{:S(2)}, u32[]{:S(2)}) collective-permute-start(f32[136,256]{1,0:T(8,128)S(1)} %shard_map.53.refs_0_), channel_id=1, source_target_pairs={{0,14},{2,0},{4,2},{6,4},{8,6},{10,8},{12,10},{14,12},{1,15},{3,1}... | collective-permute-start | bytes 417800 | tf_op jit(solution)/shard_map/ppermute | solution.py:42
  56.0 2.3 %collective-permute-start.12 = (f32[136,256]{1,0:T(8,128)S(1)}, f32[136,256]{1,0:T(8,128)S(1)}, u32[]{:S(2)}, u32[]{:S(2)}) collective-permute-start(f32[136,256]{1,0:T(8,128)S(1)} %shard_map.53.refs_0_), channel_id=1, source_target_pairs={{0,4},{2,6},{4,8},{6,10},{8,12},{10,14},{12,0},{14,2},{1,5},{3,7},... | collective-permute-start | bytes 417800 | tf_op jit(solution)/shard_map/ppermute | solution.py:42
  58.3 1.2 %collective-permute-start.11 = (f32[136,256]{1,0:T(8,128)S(1)}, f32[136,256]{1,0:T(8,128)S(1)}, u32[]{:S(2)}, u32[]{:S(2)}) collective-permute-start(f32[136,256]{1,0:T(8,128)S(1)} %shard_map.53.refs_0_), channel_id=1, source_target_pairs={{0,12},{2,14},{4,0},{6,2},{8,4},{10,6},{12,8},{14,10},{1,13},{3,15... | collective-permute-start | bytes 417800 | tf_op jit(solution)/shard_map/ppermute | solution.py:42
  59.6 3.0 %collective-permute-start.13 = (f32[136,256]{1,0:T(8,128)S(1)}, f32[136,256]{1,0:T(8,128)S(1)}, u32[]{:S(2)}, u32[]{:S(2)}) collective-permute-start(f32[136,256]{1,0:T(8,128)S(1)} %collective-permute-done.10.refs_2_), channel_id=1, source_target_pairs={{0,16},{16,0},{1,17},{17,1},{2,18},{18,2},{3,19},{19,3},{4,20},{20... | collective-permute-start | bytes 417800 | tf_op jit(solution)/shard_map/ppermute | solution.py:46
  62.5 0.1 collective-permute-start.15
  62.6 1.7 %collective-permute-done.12.refs_4_ = f32[136,256]{1,0:T(8,128)S(1)} collective-permute-done((f32[136,256]{1,0:T(8,128)S(1)}, f32[136,256]{1,0:T(8,128)S(1)}, u32[]{:S(2)}, u32[]{:S(2)}) %collective-permute-start.12) | collective-permute-done | bytes 139296 | tf_op jit(solution)/shard_map/ppermute | solution.py:42
  64.4 2.0 %collective-permute-done.11.refs_3_ = f32[136,256]{1,0:T(8,128)S(1)} collective-permute-done((f32[136,256]{1,0:T(8,128)S(1)}, f32[136,256]{1,0:T(8,128)S(1)}, u32[]{:S(2)}, u32[]{:S(2)}) %collective-permute-start.11) | collective-permute-done | bytes 139296 | tf_op jit(solution)/shard_map/ppermute | solution.py:42
  66.3 0.1 collective-permute-done.13.refs_5_
  66.4 1.9 %collective-permute-done.15.refs_7_ = f32[136,256]{1,0:T(8,128)S(1)} collective-permute-done((f32[136,256]{1,0:T(8,128)S(1)}, f32[136,256]{1,0:T(8,128)S(1)}, u32[]{:S(2)}, u32[]{:S(2)}) %collective-permute-start.15) | collective-permute-done | bytes 139296 | tf_op jit(solution)/shard_map/ppermute | solution.py:46
  68.3 4.9 %collective-permute-start.16 = (f32[136,256]{1,0:T(8,128)S(1)}, f32[136,256]{1,0:T(8,128)S(1)}, u32[]{:S(2)}, u32[]{:S(2)}) collective-permute-start(f32[136,256]{1,0:T(8,128)S(1)} %shard_map.53.refs_0_), channel_id=1, source_target_pairs={{0,1},{1,0},{2,3},{3,2},{4,5},{5,4},{6,7},{7,6},{8,9},{9,8},{10,11... | collective-permute-start | bytes 417800 | tf_op jit(solution)/shard_map/ppermute | solution.py:55
  73.2 0.0 collective-permute-start.17
  73.2 0.5 collective-permute-start.18
  73.7 0.0 collective-permute-start.19
  73.7 0.5 collective-permute-start.20
  74.2 0.3 collective-permute-start.21
  74.5 0.2 collective-permute-start.22
  74.7 0.3 collective-permute-start.23
  75.0 1.5 %shard_map.54 = (f32[12,256,256]{2,1,0:T(8,128)S(1)}, f32[6,8,256]{2,1,0:T(8,128)S(1)}) custom-call(s32[4]{0:T(128)S(1)} %pad_add_fusion.here_ref, f32[136,256]{1,0:T(8,128)S(1)} %shard_map.53.refs_0_, f32[136,256]{1,0:T(8,128)S(1)} %collective-permute-done.9.refs_1_, f32[136,256]{1,0:T(8,128)S(1)} %collective-permute-done.10.refs_2_, ...), custom_call_target="tpu_custom_call" | custom-call | tf_op jit(solution)/shard_map/pallas_call | solution.py:308
  76.6 2.8 %shard_map.55 = (f32[12,256,256]{2,1,0:T(8,128)S(1)}, f32[8,12,8,256]{3,2,1,0:T(8,128)S(1)}) custom-call(s32[4]{0:T(128)S(1)} %pad_add_fusion.here_ref, f32[136,256]{1,0:T(8,128)S(1)} %collective-permute-done.16.refs_0_, f32[136,256]{1,0:T(8,128)S(1)} %collective-permute-done.17.refs_1_, ...), custom_call_target="tpu_custom_call", output_to_operand_aliasing={{0}: (10, {})} | custom-call | tf_op jit(solution)/shard_map/pallas_call | solution.py:319
  79.4 0.9 copy-done.2
  80.3 4.3 %all-to-all-start = ((f32[8,12,8,256]{3,2,1,0:T(8,128)}), f32[8,12,8,256]{3,2,1,0:T(8,128)}, u32[]{:S(2)}, u32[]{:S(2)}) async-start(f32[8,12,8,256]{3,2,1,0:T(8,128)} %copy-done.2), calls=%async_computation | async-start | bytes 1572864 | tf_op jit(solution)/shard_map/all_to_all | solution.py:382
  84.6 0.0 copy-start.1
  84.7 1.4 %copy-done.1 = f32[3072,128]{1,0:T(8,128)S(1)} copy-done((f32[3072,128]{1,0:T(8,128)S(1)}, f32[3072,128]{1,0:T(8,128)}, u32[]{:S(2)}) %copy-start.1) | copy-done | bytes 1572888
  86.1 7.7 %shard_map.56 = (f32[3072,128]{1,0:T(8,128)}, s32[24]{0:T(128)S(1)}) custom-call(s32[4]{0:T(128)S(1)} %pad_add_fusion.here_ref, s32[8,12]{1,0:T(8,128)S(1)} %copy-done.3, f32[12,256,256]{2,1,0:T(8,128)S(1)} %get-tuple-element.42.full_ref, f32[3072,128]{1,0:T(8,128)S(1)} %copy-done.1), custom_call_target="tpu_custom_call" | custom-call | flops 1207959552 | bytes 6291456 | tf_op jit(solution)/shard_map/pallas_call | solution.py:339
  93.7 3.6 %all-to-all-done.rows_ref = f32[8,12,8,256]{3,2,1,0:T(8,128)} async-done(((f32[8,12,8,256]{3,2,1,0:T(8,128)}), f32[8,12,8,256]{3,2,1,0:T(8,128)}, u32[]{:S(2)}, u32[]{:S(2)}) %all-to-all-start) | async-done | bytes 786464 | tf_op jit(solution)/shard_map/all_to_all | solution.py:382
  97.3 2.0 %shard_map.57 = f32[24,8,256]{2,1,0:T(8,128)} custom-call(s32[24]{0:T(128)S(1)} %get-tuple-element.44.table_ref, f32[8,12,8,256]{3,2,1,0:T(8,128)} %all-to-all-done.rows_ref), custom_call_target="tpu_custom_call" | custom-call | tf_op jit(solution)/shard_map/pallas_call | solution.py:384
  (22 shorter events, 0.1 us)
Async XLA Ops:
  0.7 1.4 %copy-start = (bf16[1,256,3072]{2,1,0:T(8,128)(2,1)S(1)}, bf16[1,256,3072]{2,1,0:T(8,128)(2,1)}, u32[]{:S(2)}) copy-start(bf16[1,256,3072]{2,1,0:T(8,128)(2,1)} %param.3) | copy-start | bytes 4718596
  3.1 5.3 %collective-permute-start = (f32[6,136,256]{2,1,0:T(8,128)S(1)}, f32[6,136,256]{2,1,0:T(8,128)S(1)}, u32[]{:S(2)}, u32[]{:S(2)}) collective-permute-start(f32[6,136,256]{2,1,0:T(8,128)S(1)} %shard_map.51), channel_id=1, source_target_pairs={{0,1},{1,0},{2,3},{3,2},{4,5},{5,4},{6,7},{7,6},{8,9},{9,8},{10,11... | collective-permute-start | bytes 2506760 | tf_op jit(solution)/shard_map/ppermute | solution.py:55
  9.2 10.1 %collective-permute-start.4 = (f32[136,256]{1,0:T(8,128)S(1)}, f32[136,256]{1,0:T(8,128)S(1)}, u32[]{:S(2)}, u32[]{:S(2)}) collective-permute-start(f32[136,256]{1,0:T(8,128)S(1)} %get-tuple-element.29), channel_id=1, source_target_pairs={{0,16},{16,0},{1,17},{17,1},{2,18},{18,2},{3,19},{19,3},{4,20},{20... | collective-permute-start | bytes 417800 | tf_op jit(solution)/shard_map/ppermute | solution.py:46
  10.3 9.8 %collective-permute-start.6 = (f32[136,256]{1,0:T(8,128)S(1)}, f32[136,256]{1,0:T(8,128)S(1)}, u32[]{:S(2)}, u32[]{:S(2)}) collective-permute-start(f32[136,256]{1,0:T(8,128)S(1)} %get-tuple-element.31), channel_id=1, source_target_pairs={{0,16},{16,0},{1,17},{17,1},{2,18},{18,2},{3,19},{19,3},{4,20},{20... | collective-permute-start | bytes 417800 | tf_op jit(solution)/shard_map/ppermute | solution.py:46
  12.3 10.2 %collective-permute-start.1 = (f32[136,256]{1,0:T(8,128)S(1)}, f32[136,256]{1,0:T(8,128)S(1)}, u32[]{:S(2)}, u32[]{:S(2)}) collective-permute-start(f32[136,256]{1,0:T(8,128)S(1)} %get-tuple-element.25), channel_id=1, source_target_pairs={{0,16},{16,0},{1,17},{17,1},{2,18},{18,2},{3,19},{19,3},{4,20},{20... | collective-permute-start | bytes 417800 | tf_op jit(solution)/shard_map/ppermute | solution.py:46
  13.3 9.2 %collective-permute-start.2 = (f32[136,256]{1,0:T(8,128)S(1)}, f32[136,256]{1,0:T(8,128)S(1)}, u32[]{:S(2)}, u32[]{:S(2)}) collective-permute-start(f32[136,256]{1,0:T(8,128)S(1)} %get-tuple-element.26), channel_id=1, source_target_pairs={{0,4},{2,6},{4,8},{6,10},{8,12},{10,14},{12,0},{14,2},{1,5},{3,7},... | collective-permute-start | bytes 417800 | tf_op jit(solution)/shard_map/ppermute | solution.py:42
  16.3 10.8 %collective-permute-start.3 = (f32[136,256]{1,0:T(8,128)S(1)}, f32[136,256]{1,0:T(8,128)S(1)}, u32[]{:S(2)}, u32[]{:S(2)}) collective-permute-start(f32[136,256]{1,0:T(8,128)S(1)} %get-tuple-element.27), channel_id=1, source_target_pairs={{0,12},{2,14},{4,0},{6,2},{8,4},{10,6},{12,8},{14,10},{1,13},{3,15... | collective-permute-start | bytes 417800 | tf_op jit(solution)/shard_map/ppermute | solution.py:42
  19.3 9.1 %collective-permute-start.5 = (f32[136,256]{1,0:T(8,128)S(1)}, f32[136,256]{1,0:T(8,128)S(1)}, u32[]{:S(2)}, u32[]{:S(2)}) collective-permute-start(f32[136,256]{1,0:T(8,128)S(1)} %add.24), channel_id=1, source_target_pairs={{0,2},{2,4},{4,6},{6,8},{8,10},{10,12},{12,14},{14,0},{1,3},{3,5},... | collective-permute-start | bytes 417800 | tf_op jit(solution)/shard_map/ppermute | solution.py:42
  20.2 8.9 %collective-permute-start.7 = (f32[136,256]{1,0:T(8,128)S(1)}, f32[136,256]{1,0:T(8,128)S(1)}, u32[]{:S(2)}, u32[]{:S(2)}) collective-permute-start(f32[136,256]{1,0:T(8,128)S(1)} %add.26), channel_id=1, source_target_pairs={{0,14},{2,0},{4,2},{6,4},{8,6},{10,8},{12,10},{14,12},{1,15},{3,1}... | collective-permute-start | bytes 417800 | tf_op jit(solution)/shard_map/ppermute | solution.py:42
  29.1 10.3 %collective-permute-start.8 = (f32[136,256]{1,0:T(8,128)S(1)}, f32[136,256]{1,0:T(8,128)S(1)}, u32[]{:S(2)}, u32[]{:S(2)}) collective-permute-start(f32[136,256]{1,0:T(8,128)S(1)} %add_add_fusion.a_ref), channel_id=1, source_target_pairs={{0,24},{2,26},{4,28},{6,30},{8,16},{10,18},{12,20},{14,22},{16,8},... | collective-permute-start | bytes 417800 | tf_op jit(solution)/shard_map/ppermute | solution.py:51
  50.7 8.8 %collective-permute-start.10 = (f32[136,256]{1,0:T(8,128)S(1)}, f32[136,256]{1,0:T(8,128)S(1)}, u32[]{:S(2)}, u32[]{:S(2)}) collective-permute-start(f32[136,256]{1,0:T(8,128)S(1)} %shard_map.53.refs_0_), channel_id=1, source_target_pairs={{0,2},{2,4},{4,6},{6,8},{8,10},{10,12},{12,14},{14,0},{1,3},{3,5},... | collective-permute-start | bytes 417800 | tf_op jit(solution)/shard_map/ppermute | solution.py:42
  50.8 11.7 %collective-permute-start.9 = (f32[136,256]{1,0:T(8,128)S(1)}, f32[136,256]{1,0:T(8,128)S(1)}, u32[]{:S(2)}, u32[]{:S(2)}) collective-permute-start(f32[136,256]{1,0:T(8,128)S(1)} %shard_map.53.refs_0_), channel_id=1, source_target_pairs={{0,14},{2,0},{4,2},{6,4},{8,6},{10,8},{12,10},{14,12},{1,15},{3,1}... | collective-permute-start | bytes 417800 | tf_op jit(solution)/shard_map/ppermute | solution.py:42
  56.0 6.6 %collective-permute-start.14 = (f32[136,256]{1,0:T(8,128)S(1)}, f32[136,256]{1,0:T(8,128)S(1)}, u32[]{:S(2)}, u32[]{:S(2)}) collective-permute-start(f32[136,256]{1,0:T(8,128)S(1)} %shard_map.53.refs_0_), channel_id=1, source_target_pairs={{0,16},{16,0},{1,17},{17,1},{2,18},{18,2},{3,19},{19,3},{4,20},{20... | collective-permute-start | bytes 417800 | tf_op jit(solution)/shard_map/ppermute | solution.py:46
  56.0 8.4 %collective-permute-start.12 = (f32[136,256]{1,0:T(8,128)S(1)}, f32[136,256]{1,0:T(8,128)S(1)}, u32[]{:S(2)}, u32[]{:S(2)}) collective-permute-start(f32[136,256]{1,0:T(8,128)S(1)} %shard_map.53.refs_0_), channel_id=1, source_target_pairs={{0,4},{2,6},{4,8},{6,10},{8,12},{10,14},{12,0},{14,2},{1,5},{3,7},... | collective-permute-start | bytes 417800 | tf_op jit(solution)/shard_map/ppermute | solution.py:42
  58.3 8.0 %collective-permute-start.11 = (f32[136,256]{1,0:T(8,128)S(1)}, f32[136,256]{1,0:T(8,128)S(1)}, u32[]{:S(2)}, u32[]{:S(2)}) collective-permute-start(f32[136,256]{1,0:T(8,128)S(1)} %shard_map.53.refs_0_), channel_id=1, source_target_pairs={{0,12},{2,14},{4,0},{6,2},{8,4},{10,6},{12,8},{14,10},{1,13},{3,15... | collective-permute-start | bytes 417800 | tf_op jit(solution)/shard_map/ppermute | solution.py:42
  59.6 6.8 %collective-permute-start.13 = (f32[136,256]{1,0:T(8,128)S(1)}, f32[136,256]{1,0:T(8,128)S(1)}, u32[]{:S(2)}, u32[]{:S(2)}) collective-permute-start(f32[136,256]{1,0:T(8,128)S(1)} %collective-permute-done.10.refs_2_), channel_id=1, source_target_pairs={{0,16},{16,0},{1,17},{17,1},{2,18},{18,2},{3,19},{19,3},{4,20},{20... | collective-permute-start | bytes 417800 | tf_op jit(solution)/shard_map/ppermute | solution.py:46
  62.5 5.7 %collective-permute-start.15 = (f32[136,256]{1,0:T(8,128)S(1)}, f32[136,256]{1,0:T(8,128)S(1)}, u32[]{:S(2)}, u32[]{:S(2)}) collective-permute-start(f32[136,256]{1,0:T(8,128)S(1)} %collective-permute-done.9.refs_1_), channel_id=1, source_target_pairs={{0,16},{16,0},{1,17},{17,1},{2,18},{18,2},{3,19},{19,3},{4,20},{20... | collective-permute-start | bytes 417800 | tf_op jit(solution)/shard_map/ppermute | solution.py:46
  68.3 5.9 %collective-permute-start.16 = (f32[136,256]{1,0:T(8,128)S(1)}, f32[136,256]{1,0:T(8,128)S(1)}, u32[]{:S(2)}, u32[]{:S(2)}) collective-permute-start(f32[136,256]{1,0:T(8,128)S(1)} %shard_map.53.refs_0_), channel_id=1, source_target_pairs={{0,1},{1,0},{2,3},{3,2},{4,5},{5,4},{6,7},{7,6},{8,9},{9,8},{10,11... | collective-permute-start | bytes 417800 | tf_op jit(solution)/shard_map/ppermute | solution.py:55
  73.2 1.4 %collective-permute-start.17 = (f32[136,256]{1,0:T(8,128)S(1)}, f32[136,256]{1,0:T(8,128)S(1)}, u32[]{:S(2)}, u32[]{:S(2)}) collective-permute-start(f32[136,256]{1,0:T(8,128)S(1)} %collective-permute-done.9.refs_1_), channel_id=1, source_target_pairs={{0,1},{1,0},{2,3},{3,2},{4,5},{5,4},{6,7},{7,6},{8,9},{9,8},{10,11... | collective-permute-start | bytes 417800 | tf_op jit(solution)/shard_map/ppermute | solution.py:55
  73.2 1.6 %collective-permute-start.18 = (f32[136,256]{1,0:T(8,128)S(1)}, f32[136,256]{1,0:T(8,128)S(1)}, u32[]{:S(2)}, u32[]{:S(2)}) collective-permute-start(f32[136,256]{1,0:T(8,128)S(1)} %collective-permute-done.10.refs_2_), channel_id=1, source_target_pairs={{0,1},{1,0},{2,3},{3,2},{4,5},{5,4},{6,7},{7,6},{8,9},{9,8},{10,11... | collective-permute-start | bytes 417800 | tf_op jit(solution)/shard_map/ppermute | solution.py:55
  73.7 2.8 %collective-permute-start.19 = (f32[136,256]{1,0:T(8,128)S(1)}, f32[136,256]{1,0:T(8,128)S(1)}, u32[]{:S(2)}, u32[]{:S(2)}) collective-permute-start(f32[136,256]{1,0:T(8,128)S(1)} %collective-permute-done.11.refs_3_), channel_id=1, source_target_pairs={{0,1},{1,0},{2,3},{3,2},{4,5},{5,4},{6,7},{7,6},{8,9},{9,8},{10,11... | collective-permute-start | bytes 417800 | tf_op jit(solution)/shard_map/ppermute | solution.py:55
  73.7 2.8 %collective-permute-start.20 = (f32[136,256]{1,0:T(8,128)S(1)}, f32[136,256]{1,0:T(8,128)S(1)}, u32[]{:S(2)}, u32[]{:S(2)}) collective-permute-start(f32[136,256]{1,0:T(8,128)S(1)} %collective-permute-done.12.refs_4_), channel_id=1, source_target_pairs={{0,1},{1,0},{2,3},{3,2},{4,5},{5,4},{6,7},{7,6},{8,9},{9,8},{10,11... | collective-permute-start | bytes 417800 | tf_op jit(solution)/shard_map/ppermute | solution.py:55
  74.2 2.3 %collective-permute-start.21 = (f32[136,256]{1,0:T(8,128)S(1)}, f32[136,256]{1,0:T(8,128)S(1)}, u32[]{:S(2)}, u32[]{:S(2)}) collective-permute-start(f32[136,256]{1,0:T(8,128)S(1)} %collective-permute-done.13.refs_5_), channel_id=1, source_target_pairs={{0,1},{1,0},{2,3},{3,2},{4,5},{5,4},{6,7},{7,6},{8,9},{9,8},{10,11... | collective-permute-start | bytes 417800 | tf_op jit(solution)/shard_map/ppermute | solution.py:55
  74.5 2.0 %collective-permute-start.22 = (f32[136,256]{1,0:T(8,128)S(1)}, f32[136,256]{1,0:T(8,128)S(1)}, u32[]{:S(2)}, u32[]{:S(2)}) collective-permute-start(f32[136,256]{1,0:T(8,128)S(1)} %collective-permute-done.14.refs_6_), channel_id=1, source_target_pairs={{0,1},{1,0},{2,3},{3,2},{4,5},{5,4},{6,7},{7,6},{8,9},{9,8},{10,11... | collective-permute-start | bytes 417800 | tf_op jit(solution)/shard_map/ppermute | solution.py:55
  74.7 1.8 %collective-permute-start.23 = (f32[136,256]{1,0:T(8,128)S(1)}, f32[136,256]{1,0:T(8,128)S(1)}, u32[]{:S(2)}, u32[]{:S(2)}) collective-permute-start(f32[136,256]{1,0:T(8,128)S(1)} %collective-permute-done.15.refs_7_), channel_id=1, source_target_pairs={{0,1},{1,0},{2,3},{3,2},{4,5},{5,4},{6,7},{7,6},{8,9},{9,8},{10,11... | collective-permute-start | bytes 417800 | tf_op jit(solution)/shard_map/ppermute | solution.py:55
  79.4 0.9 copy-start.2
  80.3 4.4 %copy-start.3 = (s32[8,12]{1,0:T(8,128)S(1)}, s32[8,12]{1,0:T(8,128)}, u32[]{:S(2)}) copy-start(s32[8,12]{1,0:T(8,128)} %owner_ref.1) | copy-start | bytes 1156
  80.3 17.0 %all-to-all-start = ((f32[8,12,8,256]{3,2,1,0:T(8,128)}), f32[8,12,8,256]{3,2,1,0:T(8,128)}, u32[]{:S(2)}, u32[]{:S(2)}) async-start(f32[8,12,8,256]{3,2,1,0:T(8,128)} %copy-done.2), calls=%async_computation | async-start | bytes 1572864 | tf_op jit(solution)/shard_map/all_to_all | solution.py:382
  84.6 1.4 %copy-start.1 = (f32[3072,128]{1,0:T(8,128)S(1)}, f32[3072,128]{1,0:T(8,128)}, u32[]{:S(2)}) copy-start(f32[3072,128]{1,0:T(8,128)} %grad_ref.1) | copy-start | bytes 4718596

commit v3 on v2

--- a/solution.py
+++ b/solution.py
@@ -19,6 +19,7 @@
 DP = ("x", "z", "c")
 damping_ratio = 0.1
 LIMIT = 8 * 1024 * 1024
+ALMOST_ALL = 65 * 1000 * 1000
 VMEM = pltpu.VMEM
 f32 = jnp.float32
 
@@ -81,12 +82,19 @@
     return upper, cross, lower
 
 
-def gram_kernel(here_ref, acts_ref, out_ref, *, other):
+def gram_kernel(here_ref, acts_ref, out_ref, part_ref, got, *, other):
     c = here_ref[2]
     first = (1 - c if other else c) * PER_CORE
+
+    def fetch(k):
+        columns = pl.ds(pl.multiple_of((first + k) * BLK, BLK), BLK)
+        return pltpu.make_async_copy(acts_ref.at[:, columns], part_ref.at[k], got.at[k])
+
     for k in range(PER_CORE):
-        start = pl.multiple_of((first + k) * BLK, BLK)
-        part = acts_ref[:, pl.ds(start, BLK)]
+        fetch(k).start()
+    for k in range(PER_CORE):
+        fetch(k).wait()
+        part = part_ref[k]
         total = lax.dot_general(part, part, (((0,), (0,)), ((), ())), preferred_element_type=f32)
         store_packed(
             out_ref.at[k], total[0:HALF, 0:HALF], total[HALF:BLK, 0:HALF], total[HALF:BLK, HALF:BLK]
@@ -197,67 +205,55 @@
         store_packed(out_ref, first + dot(w, x, ((0,), (0,))), -x, second)
 
 
-def unpack_blocks(here_ref, in_refs, full_ref, rows_ref, block_ref, done, *, other, first):
+def unpack_kernel(here_ref, *refs):
+    in_refs, (full_ref, mine_ref, theirs_ref) = refs[:N_Z], refs[N_Z:]
     c, own = here_ref[2], own_slot(here_ref)
-    core = 1 - c if other else c
-    start = pl.multiple_of(((here_ref[0] * N_Z + here_ref[1]) * 2 + c) * SUB, SUB)
-
-    def leave(k):
-        return pltpu.make_async_copy(block_ref.at[k], full_ref.at[core * PER_CORE + k], done.at[k])
+    start = (here_ref[0] * N_Z + here_ref[1]) * 2
+
+    def rows(k, core):
+        return full_ref[k, pl.ds(pl.multiple_of((start + core) * SUB, SUB), SUB), :]
 
     for offset, ref in zip(OFFSETS, in_refs):
         slot = (own + N_Z + offset) % N_Z
-        k = rank(slot, core)
-
-        @pl.when(holds(slot, core))
+        k = rank(slot, c)
+
+        @pl.when(holds(slot, c))
         def _():
             upper, cross, lower = unpacked(ref[...])
-            block_ref[k, 0:HALF, 0:HALF] = upper
-            block_ref[k, 0:HALF, HALF:BLK] = cross.T
-            block_ref[k, HALF:BLK, 0:HALF] = cross
-            block_ref[k, HALF:BLK, HALF:BLK] = lower
-            leave(k).start()
-            rows_ref[first + k] = block_ref[k, pl.ds(start, SUB), :]
-
-    return [leave(k) for k in range(PER_CORE)]
-
-
-def unpack_own_kernel(here_ref, *refs):
-    full_ref, rows_ref, block_ref, done = refs[N_Z:]
-    copies = unpack_blocks(
-        here_ref, refs[:N_Z], full_ref, rows_ref, block_ref, done, other=False, first=0
-    )
-    for copy in copies:
-        copy.wait()
-
-
-def unpack_other_kernel(here_ref, *refs):
-    own_rows_ref, _, full_ref, sent_ref, block_ref, rows_ref, done, gone = refs[N_Z:]
+            full_ref[k, 0:HALF, 0:HALF] = upper
+            full_ref[k, 0:HALF, HALF:BLK] = cross.T
+            full_ref[k, HALF:BLK, 0:HALF] = cross
+            full_ref[k, HALF:BLK, HALF:BLK] = lower
+            mine_ref[k] = rows(k, c)
+            theirs_ref[k] = rows(k, 1 - c)
+
+
+def spread_kernel(here_ref, own_ref, other_ref, out_ref):
     c = here_ref[2]
     for k in range(PER_CORE):
-        rows_ref[c * PER_CORE + k] = own_rows_ref[k]
-    copies = unpack_blocks(
-        here_ref, refs[:N_Z], full_ref, rows_ref, block_ref, done, other=True, first=(1 - c) * PER_CORE
-    )
-    sends = [
-        pltpu.make_async_copy(rows_ref, sent_ref.at[s], gone.at[s]) for s in range(sent_ref.shape[0])
-    ]
-    for copy in sends:
-        copy.start()
-    for copy in copies + sends:
-        copy.wait()
-
-
-def precond_kernel(here_ref, owner_ref, full_ref, grad_ref, out_ref, table_ref):
-    out_ref[...] = dot(full_ref[0], grad_ref[...])
-
-    @pl.when(pl.program_id(0) == 0)
+        own, other = own_ref[k], other_ref[k]
+        for s in range(out_ref.shape[0]):
+            out_ref[s, c * PER_CORE + k] = own
+            out_ref[s, (1 - c) * PER_CORE + k] = other
+
+
+def precond_kernel(here_ref, owner_ref, own_ref, other_ref, grad_ref, out_ref, pick_ref, table_ref):
+    step = pl.program_id(0)
+    k = step % PER_CORE
+
+    @pl.when(step < PER_CORE)
+    def _():
+        out_ref[...] = dot(own_ref[k], grad_ref[...])
+
+    @pl.when(step >= PER_CORE)
+    def _():
+        out_ref[...] = dot(other_ref[k], grad_ref[...])
+
+    @pl.when(step == 0)
     def _():
         sections, nblocks = owner_ref.shape
-
-        def clear(j, carry):
+        for j in range(HOST):
             table_ref[j] = -1
-            return carry
 
         def section(s, count):
             for b in range(nblocks):
@@ -270,17 +266,10 @@
                 count = count + hit.astype(jnp.int32)
             return count
 
-        lax.fori_loop(0, HOST, clear, 0)
         lax.fori_loop(0, sections, section, jnp.int32(0))
-
-
-def hosted_kernel(table_ref, rows_ref, out_ref):
-    nblocks = rows_ref.shape[1]
-    for j in range(HOST):
-        source = table_ref[j]
-        at = jnp.maximum(source, 0)
-        rows = rows_ref[at // nblocks, at % nblocks]
-        out_ref[j] = jnp.where(source >= 0, rows, 0.0)
+        block = lax.broadcasted_iota(jnp.int32, (1, sections * nblocks), 1)
+        for j in range(HOST):
+            pick_ref[j : j + 1, :] = (block == table_ref[j]).astype(f32)
 
 
 def call(kernel, out_shape, n_smem, n_vmem):
@@ -299,54 +288,48 @@
     return jax.ShapeDtypeStruct(dims, f32)
 
 
-IN_HBM = pl.BlockSpec(memory_space=pltpu.HBM)
 IN_VMEM = pl.BlockSpec(memory_space=VMEM)
 IN_SMEM = pl.BlockSpec(memory_space=pltpu.SMEM)
 
 
-def unpack_own(here, values):
+def grams(here, features, other):
     return pl.pallas_call(
-        unpack_own_kernel,
-        out_shape=[shape(NB, BLK, BLK), shape(PER_CORE, SUB, BLK)],
-        in_specs=[IN_SMEM] + [IN_VMEM] * N_Z,
-        out_specs=[IN_HBM, IN_VMEM],
-        scratch_shapes=[VMEM((PER_CORE, BLK, BLK), f32), pltpu.SemaphoreType.DMA((PER_CORE,))],
-        compiler_params=pltpu.CompilerParams(vmem_limit_bytes=LIMIT),
-    )(here, *values)
-
-
-def unpack_other(here, values, own_rows, full, copies):
-    return pl.pallas_call(
-        unpack_other_kernel,
-        out_shape=[shape(NB, BLK, BLK), shape(copies, NB, SUB, BLK)],
-        in_specs=[IN_SMEM] + [IN_VMEM] * (N_Z + 1) + [IN_HBM],
-        out_specs=[IN_HBM, IN_HBM],
+        functools.partial(gram_kernel, other=other),
+        out_shape=shape(PER_CORE, TALL, BLK),
+        in_specs=[IN_SMEM, pl.BlockSpec(memory_space=pl.ANY)],
+        out_specs=IN_VMEM,
         scratch_shapes=[
-            VMEM((PER_CORE, BLK, BLK), f32),
-            VMEM((NB, SUB, BLK), f32),
+            VMEM((PER_CORE, features.shape[0], BLK), features.dtype),
             pltpu.SemaphoreType.DMA((PER_CORE,)),
-            pltpu.SemaphoreType.DMA((copies,)),
         ],
-        input_output_aliases={2 + N_Z: 0},
-        compiler_params=pltpu.CompilerParams(vmem_limit_bytes=LIMIT),
-    )(here, *values, own_rows, full)
-
-
-def preconditioned(here, owner_of, full, grad):
+        compiler_params=pltpu.CompilerParams(vmem_limit_bytes=ALMOST_ALL if other else LIMIT),
+    )(here, features)
+
+
+def preconditioned(here, owner_of, own, other, grad):
     rows, columns = grad.shape
-    part = pl.BlockSpec((BLK, columns), lambda i: (i, 0))
-    scalars = pl.BlockSpec(memory_space=pltpu.SMEM)
+
+    def block(i, here_ref):
+        c = here_ref[2]
+        return jnp.where(i < PER_CORE, c * PER_CORE + i, (1 - c) * PER_CORE + i - PER_CORE), 0
+
+    part = pl.BlockSpec((BLK, columns), block)
+    pick = shape(HOST, owner_of.size)
     return pl.pallas_call(
         precond_kernel,
-        grid=(rows // BLK,),
-        out_shape=[shape(rows, columns), jax.ShapeDtypeStruct((HOST,), jnp.int32)],
-        in_specs=[scalars, scalars, pl.BlockSpec((1, BLK, BLK), lambda i: (i, 0, 0)), part],
-        out_specs=[part, scalars],
+        grid_spec=pltpu.PrefetchScalarGridSpec(
+            num_scalar_prefetch=1,
+            grid=(rows // BLK,),
+            in_specs=[IN_SMEM, IN_VMEM, IN_VMEM, part],
+            out_specs=[part, pl.BlockSpec(pick.shape, lambda i, here_ref: (0, 0))],
+            scratch_shapes=[pltpu.SMEM((HOST,), jnp.int32)],
+        ),
+        out_shape=[shape(rows, columns), pick],
         cost_estimate=pl.CostEstimate(
             flops=12 * rows * BLK * columns, bytes_accessed=16 * rows * columns, transcendentals=0
         ),
         compiler_params=pltpu.CompilerParams(vmem_limit_bytes=LIMIT),
-    )(here, owner_of, full, grad)
+    )(here, owner_of, own, other, grad)
 
 
 def shards(acts, grad, owner_of):
@@ -354,11 +337,9 @@
     all_tokens = acts.shape[1] * lax.axis_size(DP)
     here = jnp.stack([lax.axis_index(a) for a in ("x", "z", "c", "pipe")]).astype(jnp.int32)
     features = acts[0]
-    packed = shape(PER_CORE, TALL, BLK)
     one = shape(TALL, BLK)
-    theirs = call(functools.partial(gram_kernel, other=True), packed, 1, 1)(here, features)
-    got = across_cores(theirs)
-    mine = call(functools.partial(gram_kernel, other=False), packed, 1, 1)(here, features)
+    got = across_cores(grams(here, features, True))
+    mine = grams(here, features, False)
     part = dict(zip(OFFSETS, call(parts_kernel, [one] * N_Z, 1, 2)(here, mine, got)))
 
     across = {1: across_x(part[5]), -1: across_x(part[3])}
@@ -375,13 +356,16 @@
     held[4] = across_x(inverse)
     held[-2], held[2] = along_z(inverse, 2), along_z(inverse, -2)
     held[3], held[5] = across_x(held[-1]), across_x(held[1])
-    gathered = lax.optimization_barrier([held[k] for k in OFFSETS])
-    passed = [across_cores(value) for value in gathered]
-    full, own_rows = unpack_own(here, gathered)
-    full, sent = unpack_other(here, passed, own_rows, full, section_count)
+    opened = [shape(PER_CORE, BLK, BLK)] + [shape(PER_CORE, SUB, BLK)] * 2
+    own, own_rows, their_rows = call(unpack_kernel, opened, 1, N_Z)(here, *[held[k] for k in OFFSETS])
+    other_rows = across_cores(their_rows)
+    other = across_cores(own)
+    sent = call(spread_kernel, shape(section_count, NB, SUB, BLK), 1, 2)(here, own_rows, other_rows)
     everyone = lax.all_to_all(sent, "pipe", 0, 0, tiled=True)
-    precond, table = preconditioned(here, owner_of, full, grad)
-    hosted = call(hosted_kernel, shape(HOST, SUB, BLK), 1, 1)(table, everyone)
+    precond, pick = preconditioned(here, owner_of, own, other, grad)
+    hosted = jnp.einsum(
+        "jk,krc->jrc", pick, everyone.reshape(-1, SUB, BLK), precision=lax.Precision.HIGHEST
+    )
     return (precond, hosted[None])
 
 

time: 99.6 us -> 102 us (1.024)
  local copies, waits for them, and re-layouts: 3.74 us -> 0.76 us
  waiting for transfers between devices: 22.6 us -> 25.1 us
  Pallas kernels: 28 us -> 30.3 us
  starting transfers between devices: 44 us -> 41.9 us
  matrix products: 0 us -> 1.81 us
    ppermute x6, starting transfers between devices: 7.13 us -> 14 us  [across_x(): return lax.ppermute(value, 'x', [(0, 1), (1, 0)])]
    ppermute x8, starting transfers between devices: 18 us -> 12.7 us  [along_z(): return lax.ppermute(value, 'z', [(z, (z + step) % N_Z) for z in range(N_Z)])]
    ppermute x8, waiting for transfers between devices: 10.2 us -> 5.45 us  [along_z(): return lax.ppermute(value, 'z', [(z, (z + step) % N_Z) for z in range(N_Z)])]
    ppermute x6, waiting for transfers between devices: 1.97 us -> 5.85 us  [across_x(): return lax.ppermute(value, 'x', [(0, 1), (1, 0)])]
    ppermute x9 -> x3, starting transfers between devices: 10.1 us -> 6.76 us  [across_cores(): return lax.ppermute(value, 'c', [(0, 1), (1, 0)])]
    unnamed x8 -> x9, local copies, waits for them, and re-layouts: 3.74 us -> 0.76 us
    pallas_call x6 -> x5, Pallas kernels: 15.9 us -> 18.2 us  [the longest x1 9.09 us: preconditioned(): pl.pallas_call(precond_kernel, grid_spec=pltpu.PrefetchScalarGridSpec(num...]
    ppermute x9 -> x3, waiting for transfers between devices: 1.02 us -> 2.88 us  [across_cores(): return lax.ppermute(value, 'c', [(0, 1), (1, 0)])]
  transfers between devices with their start and end apart: 25 -> 19, of which waited for: 10 -> 8; matrix products, arithmetic and copies ran while one was open for 0% -> 0% of each run, Pallas kernels for 10% -> 13%
where the time goes in v3:
time: 102 us; the launch traced here: 101 us
  starting transfers between devices  41.9 us (41%)
  Pallas kernels  30.3 us (30%)
  waiting for transfers between devices  25.1 us (25%)
  matrix products  1.81 us (2%)
    ppermute x6, starting transfers between devices, across_x(): return lax.ppermute(value, 'x', [(0, 1), (1, 0)])  14 us
    ppermute x8, starting transfers between devices, along_z(): return lax.ppermute(value, 'z', [(z, (z + step) % N_Z) for z in range(N_Z)])  12.7 us
    pallas_call x1, Pallas kernels, shards(): call(functools.partial(invert_kernel, all_tokens=all_tokens), one, 1, 2)  11.3 us
    pallas_call x1, Pallas kernels, preconditioned(): pl.pallas_call(precond_kernel, grid_spec=pltpu.PrefetchScalarGridSpec(num...  9.09 us
    ppermute x1, waiting for transfers between devices, to_twin(): return lax.ppermute(value, ('x', 'z'), pairs)  7.27 us
    ppermute x3, starting transfers between devices, across_cores(): return lax.ppermute(value, 'c', [(0, 1), (1, 0)])  6.76 us
    pallas_call x2, Pallas kernels, grams(): pl.pallas_call(functools.partial(gram_kernel, other=other), out_shape=sha...  6.31 us
    ppermute x6, waiting for transfers between devices, across_x(): return lax.ppermute(value, 'x', [(0, 1), (1, 0)])  5.85 us
  transfers between devices with their start and end apart: 19, of which 8 were waited for; matrix products, arithmetic and copies ran while one was open for 0% of the time, Pallas kernels for 13%

profile of v3, /device:TPU:1, one launch (start us, length us, event | category | flops | bytes accessed | tf_op | source)
XLA Modules:
  0.0 101.3 jit_solution(6921069831490116378)
XLA Ops:
  0.6 0.0 copy-start
  0.6 0.7 pad_add_fusion.here_ref
  1.3 4.1 %shard_map.51 = f32[6,136,256]{2,1,0:T(8,128)} custom-call(s32[4]{0:T(128)} %pad_add_fusion.here_ref, bf16[256,3072]{1,0:T(8,128)(2,1)} %bitcast.11), custom_call_target="tpu_custom_call" | custom-call | tf_op jit(solution)/shard_map/pallas_call | solution.py:296
  5.4 3.3 %collective-permute-start = (f32[6,136,256]{2,1,0:T(8,128)}, f32[6,136,256]{2,1,0:T(8,128)S(1)}, u32[]{:S(2)}, u32[]{:S(2)}) collective-permute-start(f32[6,136,256]{2,1,0:T(8,128)} %shard_map.51), channel_id=1, source_target_pairs={{0,1},{1,0},{2,3},{3,2},{4,5},{5,4},{6,7},{7,6},{8,9},{9,8},{10,11... | collective-permute-start | bytes 2506760 | tf_op jit(solution)/shard_map/ppermute | solution.py:56
  8.8 2.2 %shard_map.50.mine_ref = f32[6,136,256]{2,1,0:T(8,128)S(1)} custom-call(s32[4]{0:T(128)S(1)} %copy-done.2, bf16[256,3072]{1,0:T(8,128)(2,1)S(1)} %bitcast.12), custom_call_target="tpu_custom_call" | custom-call | tf_op jit(solution)/shard_map/pallas_call | solution.py:296
  11.0 0.0 collective-permute-done.got_ref
  11.0 0.8 shard_map.52
  11.8 1.1 %collective-permute-start.6 = (f32[136,256]{1,0:T(8,128)S(1)}, f32[136,256]{1,0:T(8,128)S(1)}, u32[]{:S(2)}, u32[]{:S(2)}) collective-permute-start(f32[136,256]{1,0:T(8,128)S(1)} %get-tuple-element.22), channel_id=1, source_target_pairs={{0,16},{16,0},{1,17},{17,1},{2,18},{18,2},{3,19},{19,3},{4,20},{20... | collective-permute-start | bytes 417800 | tf_op jit(solution)/shard_map/ppermute | solution.py:47
  12.9 2.0 %collective-permute-start.4 = (f32[136,256]{1,0:T(8,128)S(1)}, f32[136,256]{1,0:T(8,128)S(1)}, u32[]{:S(2)}, u32[]{:S(2)}) collective-permute-start(f32[136,256]{1,0:T(8,128)S(1)} %get-tuple-element.20), channel_id=1, source_target_pairs={{0,16},{16,0},{1,17},{17,1},{2,18},{18,2},{3,19},{19,3},{4,20},{20... | collective-permute-start | bytes 417800 | tf_op jit(solution)/shard_map/ppermute | solution.py:47
  14.8 4.3 %collective-permute-start.3 = (f32[136,256]{1,0:T(8,128)S(1)}, f32[136,256]{1,0:T(8,128)S(1)}, u32[]{:S(2)}, u32[]{:S(2)}) collective-permute-start(f32[136,256]{1,0:T(8,128)S(1)} %get-tuple-element.18), channel_id=1, source_target_pairs={{0,12},{2,14},{4,0},{6,2},{8,4},{10,6},{12,8},{14,10},{1,13},{3,15... | collective-permute-start | bytes 417800 | tf_op jit(solution)/shard_map/ppermute | solution.py:43
  19.1 0.0 collective-permute-start.2
  19.1 2.7 %collective-permute-start.1 = (f32[136,256]{1,0:T(8,128)S(1)}, f32[136,256]{1,0:T(8,128)S(1)}, u32[]{:S(2)}, u32[]{:S(2)}) collective-permute-start(f32[136,256]{1,0:T(8,128)S(1)} %get-tuple-element.16), channel_id=1, source_target_pairs={{0,16},{16,0},{1,17},{17,1},{2,18},{18,2},{3,19},{19,3},{4,20},{20... | collective-permute-start | bytes 417800 | tf_op jit(solution)/shard_map/ppermute | solution.py:47
  21.9 0.0 collective-permute-done.6
  21.9 3.2 %collective-permute-start.7 = (f32[136,256]{1,0:T(8,128)S(1)}, f32[136,256]{1,0:T(8,128)S(1)}, u32[]{:S(2)}, u32[]{:S(2)}) collective-permute-start(f32[136,256]{1,0:T(8,128)S(1)} %add.26), channel_id=1, source_target_pairs={{0,14},{2,0},{4,2},{6,4},{8,6},{10,8},{12,10},{14,12},{1,15},{3,1}... | collective-permute-start | bytes 417800 | tf_op jit(solution)/shard_map/ppermute | solution.py:43
  25.1 0.0 collective-permute-done.4
  25.1 0.1 collective-permute-start.5
  25.2 1.1 %collective-permute-done.2 = f32[136,256]{1,0:T(8,128)S(1)} collective-permute-done((f32[136,256]{1,0:T(8,128)S(1)}, f32[136,256]{1,0:T(8,128)S(1)}, u32[]{:S(2)}, u32[]{:S(2)}) %collective-permute-start.2) | collective-permute-done | bytes 139296 | tf_op jit(solution)/shard_map/ppermute | solution.py:43
  26.3 0.0 collective-permute-done.1
  26.3 2.9 %collective-permute-done.7 = f32[136,256]{1,0:T(8,128)S(1)} collective-permute-done((f32[136,256]{1,0:T(8,128)S(1)}, f32[136,256]{1,0:T(8,128)S(1)}, u32[]{:S(2)}, u32[]{:S(2)}) %collective-permute-start.7) | collective-permute-done | bytes 139296 | tf_op jit(solution)/shard_map/ppermute | solution.py:43
  29.2 1.5 %collective-permute-done.5 = f32[136,256]{1,0:T(8,128)S(1)} collective-permute-done((f32[136,256]{1,0:T(8,128)S(1)}, f32[136,256]{1,0:T(8,128)S(1)}, u32[]{:S(2)}, u32[]{:S(2)}) %collective-permute-start.5) | collective-permute-done | bytes 139296 | tf_op jit(solution)/shard_map/ppermute | solution.py:43
  30.7 0.1 add_add_fusion.a_ref
  30.7 4.0 %collective-permute-start.8 = (f32[136,256]{1,0:T(8,128)S(1)}, f32[136,256]{1,0:T(8,128)S(1)}, u32[]{:S(2)}, u32[]{:S(2)}) collective-permute-start(f32[136,256]{1,0:T(8,128)S(1)} %add_add_fusion.a_ref), channel_id=1, source_target_pairs={{0,24},{2,26},{4,28},{6,30},{8,16},{10,18},{12,20},{14,22},{16,8},... | collective-permute-start | bytes 417800 | tf_op jit(solution)/shard_map/ppermute | solution.py:52
  34.8 7.3 %collective-permute-done.8.b_ref = f32[136,256]{1,0:T(8,128)S(1)} collective-permute-done((f32[136,256]{1,0:T(8,128)S(1)}, f32[136,256]{1,0:T(8,128)S(1)}, u32[]{:S(2)}, u32[]{:S(2)}) %collective-permute-start.8) | collective-permute-done | bytes 139296 | tf_op jit(solution)/shard_map/ppermute | solution.py:52
  42.0 11.3 %shard_map.53.refs_0_ = f32[136,256]{1,0:T(8,128)S(1)} custom-call(s32[4]{0:T(128)S(1)} %copy-done.2, f32[136,256]{1,0:T(8,128)S(1)} %add_add_fusion.a_ref, f32[136,256]{1,0:T(8,128)S(1)} %collective-permute-done.8.b_ref), custom_call_target="tpu_custom_call" | custom-call | tf_op jit(solution)/shard_map/pallas_call | solution.py:351
  53.4 0.0 copy-start.1
  53.4 0.0 copy-start.3
  53.4 0.1 collective-permute-start.10
  53.5 2.7 %collective-permute-start.9 = (f32[136,256]{1,0:T(8,128)S(1)}, f32[136,256]{1,0:T(8,128)S(1)}, u32[]{:S(2)}, u32[]{:S(2)}) collective-permute-start(f32[136,256]{1,0:T(8,128)S(1)} %shard_map.53.refs_0_), channel_id=1, source_target_pairs={{0,14},{2,0},{4,2},{6,4},{8,6},{10,8},{12,10},{14,12},{1,15},{3,1}... | collective-permute-start | bytes 417800 | tf_op jit(solution)/shard_map/ppermute | solution.py:43
  56.1 0.6 collective-permute-start.11
  56.7 1.8 %collective-permute-start.12 = (f32[136,256]{1,0:T(8,128)S(1)}, f32[136,256]{1,0:T(8,128)S(1)}, u32[]{:S(2)}, u32[]{:S(2)}) collective-permute-start(f32[136,256]{1,0:T(8,128)S(1)} %shard_map.53.refs_0_), channel_id=1, source_target_pairs={{0,4},{2,6},{4,8},{6,10},{8,12},{10,14},{12,0},{14,2},{1,5},{3,7},... | collective-permute-start | bytes 417800 | tf_op jit(solution)/shard_map/ppermute | solution.py:43
  58.5 5.2 %collective-permute-start.14 = (f32[136,256]{1,0:T(8,128)S(1)}, f32[136,256]{1,0:T(8,128)S(1)}, u32[]{:S(2)}, u32[]{:S(2)}) collective-permute-start(f32[136,256]{1,0:T(8,128)S(1)} %shard_map.53.refs_0_), channel_id=1, source_target_pairs={{0,16},{16,0},{1,17},{17,1},{2,18},{18,2},{3,19},{19,3},{4,20},{20... | collective-permute-start | bytes 417800 | tf_op jit(solution)/shard_map/ppermute | solution.py:47
  63.7 0.0 collective-permute-done.10.refs_2_
  63.7 0.0 collective-permute-start.13
  63.8 0.0 collective-permute-done.9.refs_1_
  63.8 2.9 %collective-permute-start.15 = (f32[136,256]{1,0:T(8,128)S(1)}, f32[136,256]{1,0:T(8,128)S(1)}, u32[]{:S(2)}, u32[]{:S(2)}) collective-permute-start(f32[136,256]{1,0:T(8,128)S(1)} %collective-permute-done.9.refs_1_), channel_id=1, source_target_pairs={{0,16},{16,0},{1,17},{17,1},{2,18},{18,2},{3,19},{19,3},{4,20},{20... | collective-permute-start | bytes 417800 | tf_op jit(solution)/shard_map/ppermute | solution.py:47
  66.7 0.0 collective-permute-done.11.refs_3_
  66.7 3.4 %collective-permute-done.13.refs_5_ = f32[136,256]{1,0:T(8,128)S(1)} collective-permute-done((f32[136,256]{1,0:T(8,128)S(1)}, f32[136,256]{1,0:T(8,128)S(1)}, u32[]{:S(2)}, u32[]{:S(2)}) %collective-permute-start.13) | collective-permute-done | bytes 139296 | tf_op jit(solution)/shard_map/ppermute | solution.py:47
  70.2 2.4 %collective-permute-done.15.refs_7_ = f32[136,256]{1,0:T(8,128)S(1)} collective-permute-done((f32[136,256]{1,0:T(8,128)S(1)}, f32[136,256]{1,0:T(8,128)S(1)}, u32[]{:S(2)}, u32[]{:S(2)}) %collective-permute-start.15) | collective-permute-done | bytes 139296 | tf_op jit(solution)/shard_map/ppermute | solution.py:47
  72.6 1.3 %shard_map.54 = (f32[6,256,256]{2,1,0:T(8,128)S(1)}, f32[6,8,256]{2,1,0:T(8,128)S(1)}, f32[6,8,256]{2,1,0:T(8,128)S(1)}) custom-call(s32[4]{0:T(128)S(1)} %copy-done.2, f32[136,256]{1,0:T(8,128)S(1)} %shard_map.53.refs_0_, f32[136,256]{1,0:T(8,128)S(1)} %collective-permute-done.9.refs_1_, f32[136,256]{1,0:T(8,128)S(1)} %collective-permute-done.10.refs_2_, ...), custom_call_target="tpu_custom_call" | custom-call | tf_op jit(solution)/shard_map/pallas_call | solution.py:360
  73.8 3.3 %collective-permute-start.16 = (f32[6,256,256]{2,1,0:T(8,128)S(1)}, f32[6,256,256]{2,1,0:T(8,128)}, u32[]{:S(2)}, u32[]{:S(2)}) collective-permute-start(f32[6,256,256]{2,1,0:T(8,128)S(1)} %get-tuple-element.23.own_ref), channel_id=1, source_target_pairs={{0,1},{1,0},{2,3},{3,2},{4,5},{5,4},{6,7},{7,6},{8,9},{9,8},{10,11... | collective-permute-start | bytes 4718600 | tf_op jit(solution)/shard_map/ppermute | solution.py:56
  77.2 0.1 collective-permute-start.17
  77.3 2.9 %collective-permute-done.17.other_ref = f32[6,8,256]{2,1,0:T(8,128)S(1)} collective-permute-done((f32[6,8,256]{2,1,0:T(8,128)S(1)}, f32[6,8,256]{2,1,0:T(8,128)S(1)}, u32[]{:S(2)}, u32[]{:S(2)}) %collective-permute-start.17) | collective-permute-done | bytes 49184 | tf_op jit(solution)/shard_map/ppermute | solution.py:56
  80.1 1.5 %shard_map.56 = f32[8,12,8,256]{3,2,1,0:T(8,128)} custom-call(s32[4]{0:T(128)S(1)} %copy-done.2, f32[6,8,256]{2,1,0:T(8,128)S(1)} %get-tuple-element.26.own_ref, f32[6,8,256]{2,1,0:T(8,128)S(1)} %collective-permute-done.17.other_ref), custom_call_target="tpu_custom_call" | custom-call | tf_op jit(solution)/shard_map/pallas_call | solution.py:363
  81.6 4.4 %all-to-all-start = ((f32[8,12,8,256]{3,2,1,0:T(8,128)}), f32[8,12,8,256]{3,2,1,0:T(8,128)}, u32[]{:S(2)}, u32[]{:S(2)}) async-start(f32[8,12,8,256]{3,2,1,0:T(8,128)} %shard_map.56), calls=%async_computation | async-start | bytes 1572864 | tf_op jit(solution)/shard_map/all_to_all | solution.py:364
  86.1 9.1 %shard_map.55 = (f32[3072,128]{1,0:T(8,128)}, f32[24,96]{1,0:T(8,128)S(1)}) custom-call(s32[4]{0:T(128)S(1)} %copy-done.2, s32[8,12]{1,0:T(8,128)S(1)} %copy-done.3, f32[6,256,256]{2,1,0:T(8,128)S(1)} %get-tuple-element.23.own_ref, f32[6,256,256]{2,1,0:T(8,128)} %collective-permute-done.16.other_ref, f32[3072,128]{1,0:T(8,128)S(1)} %copy-done.1), custom_call_target="tpu_custom_call" | custom-call | flops 1207959552 | bytes 6291456 | tf_op jit(solution)/shard_map/pallas_call | solution.py:318
  95.1 3.6 %all-to-all-done = f32[8,12,8,256]{3,2,1,0:T(8,128)} async-done(((f32[8,12,8,256]{3,2,1,0:T(8,128)}), f32[8,12,8,256]{3,2,1,0:T(8,128)}, u32[]{:S(2)}, u32[]{:S(2)}) %all-to-all-start) | async-done | bytes 786464 | tf_op jit(solution)/shard_map/all_to_all | solution.py:364
  98.7 1.8 %convolution_bitcast_fusion = f32[1,24,8,256]{3,1,2,0:T(8,128)S(1)} fusion(f32[96,8,256]{2,1,0:T(8,128)} %bitcast.6, f32[24,96]{1,0:T(8,128)S(1)} %get-tuple-element.25), kind=kOutput, calls=%fused_computation | convolution fusion | flops 56623104 | bytes 992256 | tf_op jit(solution)/shard_map/jk,krc->jrc/dot_general | solution.py:366
  100.6 0.7 copy.6
  (11 shorter events, 0.1 us)
Async XLA Ops:
  0.6 8.2 %copy-start = (bf16[1,256,3072]{2,1,0:T(8,128)(2,1)S(1)}, bf16[1,256,3072]{2,1,0:T(8,128)(2,1)}, u32[]{:S(2)}) copy-start(bf16[1,256,3072]{2,1,0:T(8,128)(2,1)} %param.3) | copy-start | bytes 4718596
  1.3 7.5 %copy-start.2 = (s32[4]{0:T(128)S(1)}, s32[4]{0:T(128)}, u32[]{:S(2)}) copy-start(s32[4]{0:T(128)} %pad_add_fusion.here_ref) | copy-start | bytes 52
  5.4 5.5 %collective-permute-start = (f32[6,136,256]{2,1,0:T(8,128)}, f32[6,136,256]{2,1,0:T(8,128)S(1)}, u32[]{:S(2)}, u32[]{:S(2)}) collective-permute-start(f32[6,136,256]{2,1,0:T(8,128)} %shard_map.51), channel_id=1, source_target_pairs={{0,1},{1,0},{2,3},{3,2},{4,5},{5,4},{6,7},{7,6},{8,9},{9,8},{10,11... | collective-permute-start | bytes 2506760 | tf_op jit(solution)/shard_map/ppermute | solution.py:56
  11.8 10.1 %collective-permute-start.6 = (f32[136,256]{1,0:T(8,128)S(1)}, f32[136,256]{1,0:T(8,128)S(1)}, u32[]{:S(2)}, u32[]{:S(2)}) collective-permute-start(f32[136,256]{1,0:T(8,128)S(1)} %get-tuple-element.22), channel_id=1, source_target_pairs={{0,16},{16,0},{1,17},{17,1},{2,18},{18,2},{3,19},{19,3},{4,20},{20... | collective-permute-start | bytes 417800 | tf_op jit(solution)/shard_map/ppermute | solution.py:47
  12.9 12.2 %collective-permute-start.4 = (f32[136,256]{1,0:T(8,128)S(1)}, f32[136,256]{1,0:T(8,128)S(1)}, u32[]{:S(2)}, u32[]{:S(2)}) collective-permute-start(f32[136,256]{1,0:T(8,128)S(1)} %get-tuple-element.20), channel_id=1, source_target_pairs={{0,16},{16,0},{1,17},{17,1},{2,18},{18,2},{3,19},{19,3},{4,20},{20... | collective-permute-start | bytes 417800 | tf_op jit(solution)/shard_map/ppermute | solution.py:47
  14.8 10.4 %collective-permute-start.3 = (f32[136,256]{1,0:T(8,128)S(1)}, f32[136,256]{1,0:T(8,128)S(1)}, u32[]{:S(2)}, u32[]{:S(2)}) collective-permute-start(f32[136,256]{1,0:T(8,128)S(1)} %get-tuple-element.18), channel_id=1, source_target_pairs={{0,12},{2,14},{4,0},{6,2},{8,4},{10,6},{12,8},{14,10},{1,13},{3,15... | collective-permute-start | bytes 417800 | tf_op jit(solution)/shard_map/ppermute | solution.py:43
  19.1 7.2 %collective-permute-start.2 = (f32[136,256]{1,0:T(8,128)S(1)}, f32[136,256]{1,0:T(8,128)S(1)}, u32[]{:S(2)}, u32[]{:S(2)}) collective-permute-start(f32[136,256]{1,0:T(8,128)S(1)} %get-tuple-element.17), channel_id=1, source_target_pairs={{0,4},{2,6},{4,8},{6,10},{8,12},{10,14},{12,0},{14,2},{1,5},{3,7},... | collective-permute-start | bytes 417800 | tf_op jit(solution)/shard_map/ppermute | solution.py:43
  19.1 7.2 %collective-permute-start.1 = (f32[136,256]{1,0:T(8,128)S(1)}, f32[136,256]{1,0:T(8,128)S(1)}, u32[]{:S(2)}, u32[]{:S(2)}) collective-permute-start(f32[136,256]{1,0:T(8,128)S(1)} %get-tuple-element.16), channel_id=1, source_target_pairs={{0,16},{16,0},{1,17},{17,1},{2,18},{18,2},{3,19},{19,3},{4,20},{20... | collective-permute-start | bytes 417800 | tf_op jit(solution)/shard_map/ppermute | solution.py:47
  21.9 7.3 %collective-permute-start.7 = (f32[136,256]{1,0:T(8,128)S(1)}, f32[136,256]{1,0:T(8,128)S(1)}, u32[]{:S(2)}, u32[]{:S(2)}) collective-permute-start(f32[136,256]{1,0:T(8,128)S(1)} %add.26), channel_id=1, source_target_pairs={{0,14},{2,0},{4,2},{6,4},{8,6},{10,8},{12,10},{14,12},{1,15},{3,1}... | collective-permute-start | bytes 417800 | tf_op jit(solution)/shard_map/ppermute | solution.py:43
  25.1 5.5 %collective-permute-start.5 = (f32[136,256]{1,0:T(8,128)S(1)}, f32[136,256]{1,0:T(8,128)S(1)}, u32[]{:S(2)}, u32[]{:S(2)}) collective-permute-start(f32[136,256]{1,0:T(8,128)S(1)} %add.24), channel_id=1, source_target_pairs={{0,2},{2,4},{4,6},{6,8},{8,10},{10,12},{12,14},{14,0},{1,3},{3,5},... | collective-permute-start | bytes 417800 | tf_op jit(solution)/shard_map/ppermute | solution.py:43
  30.7 11.3 %collective-permute-start.8 = (f32[136,256]{1,0:T(8,128)S(1)}, f32[136,256]{1,0:T(8,128)S(1)}, u32[]{:S(2)}, u32[]{:S(2)}) collective-permute-start(f32[136,256]{1,0:T(8,128)S(1)} %add_add_fusion.a_ref), channel_id=1, source_target_pairs={{0,24},{2,26},{4,28},{6,30},{8,16},{10,18},{12,20},{14,22},{16,8},... | collective-permute-start | bytes 417800 | tf_op jit(solution)/shard_map/ppermute | solution.py:52
  53.4 32.7 %copy-start.1 = (f32[3072,128]{1,0:T(8,128)S(1)}, f32[3072,128]{1,0:T(8,128)}, u32[]{:S(2)}) copy-start(f32[3072,128]{1,0:T(8,128)} %grad_ref.1) | copy-start | bytes 4718596
  53.4 32.7 %copy-start.3 = (s32[8,12]{1,0:T(8,128)S(1)}, s32[8,12]{1,0:T(8,128)}, u32[]{:S(2)}) copy-start(s32[8,12]{1,0:T(8,128)} %owner_ref.1) | copy-start | bytes 1156
  53.4 10.3 %collective-permute-start.10 = (f32[136,256]{1,0:T(8,128)S(1)}, f32[136,256]{1,0:T(8,128)S(1)}, u32[]{:S(2)}, u32[]{:S(2)}) collective-permute-start(f32[136,256]{1,0:T(8,128)S(1)} %shard_map.53.refs_0_), channel_id=1, source_target_pairs={{0,2},{2,4},{4,6},{6,8},{8,10},{10,12},{12,14},{14,0},{1,3},{3,5},... | collective-permute-start | bytes 417800 | tf_op jit(solution)/shard_map/ppermute | solution.py:43
  53.5 10.3 %collective-permute-start.9 = (f32[136,256]{1,0:T(8,128)S(1)}, f32[136,256]{1,0:T(8,128)S(1)}, u32[]{:S(2)}, u32[]{:S(2)}) collective-permute-start(f32[136,256]{1,0:T(8,128)S(1)} %shard_map.53.refs_0_), channel_id=1, source_target_pairs={{0,14},{2,0},{4,2},{6,4},{8,6},{10,8},{12,10},{14,12},{1,15},{3,1}... | collective-permute-start | bytes 417800 | tf_op jit(solution)/shard_map/ppermute | solution.py:43
  56.1 10.6 %collective-permute-start.11 = (f32[136,256]{1,0:T(8,128)S(1)}, f32[136,256]{1,0:T(8,128)S(1)}, u32[]{:S(2)}, u32[]{:S(2)}) collective-permute-start(f32[136,256]{1,0:T(8,128)S(1)} %shard_map.53.refs_0_), channel_id=1, source_target_pairs={{0,12},{2,14},{4,0},{6,2},{8,4},{10,6},{12,8},{14,10},{1,13},{3,15... | collective-permute-start | bytes 417800 | tf_op jit(solution)/shard_map/ppermute | solution.py:43
  56.7 10.0 %collective-permute-start.12 = (f32[136,256]{1,0:T(8,128)S(1)}, f32[136,256]{1,0:T(8,128)S(1)}, u32[]{:S(2)}, u32[]{:S(2)}) collective-permute-start(f32[136,256]{1,0:T(8,128)S(1)} %shard_map.53.refs_0_), channel_id=1, source_target_pairs={{0,4},{2,6},{4,8},{6,10},{8,12},{10,14},{12,0},{14,2},{1,5},{3,7},... | collective-permute-start | bytes 417800 | tf_op jit(solution)/shard_map/ppermute | solution.py:43
  58.5 8.2 %collective-permute-start.14 = (f32[136,256]{1,0:T(8,128)S(1)}, f32[136,256]{1,0:T(8,128)S(1)}, u32[]{:S(2)}, u32[]{:S(2)}) collective-permute-start(f32[136,256]{1,0:T(8,128)S(1)} %shard_map.53.refs_0_), channel_id=1, source_target_pairs={{0,16},{16,0},{1,17},{17,1},{2,18},{18,2},{3,19},{19,3},{4,20},{20... | collective-permute-start | bytes 417800 | tf_op jit(solution)/shard_map/ppermute | solution.py:47
  63.7 6.4 %collective-permute-start.13 = (f32[136,256]{1,0:T(8,128)S(1)}, f32[136,256]{1,0:T(8,128)S(1)}, u32[]{:S(2)}, u32[]{:S(2)}) collective-permute-start(f32[136,256]{1,0:T(8,128)S(1)} %collective-permute-done.10.refs_2_), channel_id=1, source_target_pairs={{0,16},{16,0},{1,17},{17,1},{2,18},{18,2},{3,19},{19,3},{4,20},{20... | collective-permute-start | bytes 417800 | tf_op jit(solution)/shard_map/ppermute | solution.py:47
  63.8 8.8 %collective-permute-start.15 = (f32[136,256]{1,0:T(8,128)S(1)}, f32[136,256]{1,0:T(8,128)S(1)}, u32[]{:S(2)}, u32[]{:S(2)}) collective-permute-start(f32[136,256]{1,0:T(8,128)S(1)} %collective-permute-done.9.refs_1_), channel_id=1, source_target_pairs={{0,16},{16,0},{1,17},{17,1},{2,18},{18,2},{3,19},{19,3},{4,20},{20... | collective-permute-start | bytes 417800 | tf_op jit(solution)/shard_map/ppermute | solution.py:47
  73.8 12.2 %collective-permute-start.16 = (f32[6,256,256]{2,1,0:T(8,128)S(1)}, f32[6,256,256]{2,1,0:T(8,128)}, u32[]{:S(2)}, u32[]{:S(2)}) collective-permute-start(f32[6,256,256]{2,1,0:T(8,128)S(1)} %get-tuple-element.23.own_ref), channel_id=1, source_target_pairs={{0,1},{1,0},{2,3},{3,2},{4,5},{5,4},{6,7},{7,6},{8,9},{9,8},{10,11... | collective-permute-start | bytes 4718600 | tf_op jit(solution)/shard_map/ppermute | solution.py:56
  77.2 3.0 %collective-permute-start.17 = (f32[6,8,256]{2,1,0:T(8,128)S(1)}, f32[6,8,256]{2,1,0:T(8,128)S(1)}, u32[]{:S(2)}, u32[]{:S(2)}) collective-permute-start(f32[6,8,256]{2,1,0:T(8,128)S(1)} %get-tuple-element.27), channel_id=1, source_target_pairs={{0,1},{1,0},{2,3},{3,2},{4,5},{5,4},{6,7},{7,6},{8,9},{9,8},{10,11... | collective-permute-start | bytes 147464 | tf_op jit(solution)/shard_map/ppermute | solution.py:56
  81.6 17.1 %all-to-all-start = ((f32[8,12,8,256]{3,2,1,0:T(8,128)}), f32[8,12,8,256]{3,2,1,0:T(8,128)}, u32[]{:S(2)}, u32[]{:S(2)}) async-start(f32[8,12,8,256]{3,2,1,0:T(8,128)} %shard_map.56), calls=%async_computation | async-start | bytes 1572864 | tf_op jit(solution)/shard_map/all_to_all | solution.py:364

commit v4 on v3

--- a/solution.py
+++ b/solution.py
@@ -19,7 +19,6 @@
 DP = ("x", "z", "c")
 damping_ratio = 0.1
 LIMIT = 8 * 1024 * 1024
-ALMOST_ALL = 65 * 1000 * 1000
 VMEM = pltpu.VMEM
 f32 = jnp.float32
 
@@ -37,6 +36,7 @@
 
 
 OFFSETS = (0, 1, -1, 2, -2, 3, 4, 5)
+PAIR = (5, 3)
 
 
 def along_z(value, step):
@@ -82,28 +82,23 @@
     return upper, cross, lower
 
 
-def gram_kernel(here_ref, acts_ref, out_ref, part_ref, got, *, other):
+def gram_kernel(here_ref, acts_ref, out_ref, *, other):
     c = here_ref[2]
     first = (1 - c if other else c) * PER_CORE
-
-    def fetch(k):
-        columns = pl.ds(pl.multiple_of((first + k) * BLK, BLK), BLK)
-        return pltpu.make_async_copy(acts_ref.at[:, columns], part_ref.at[k], got.at[k])
-
     for k in range(PER_CORE):
-        fetch(k).start()
-    for k in range(PER_CORE):
-        fetch(k).wait()
-        part = part_ref[k]
+        start = pl.multiple_of((first + k) * BLK, BLK)
+        part = acts_ref[:, pl.ds(start, BLK)]
         total = lax.dot_general(part, part, (((0,), (0,)), ((), ())), preferred_element_type=f32)
         store_packed(
             out_ref.at[k], total[0:HALF, 0:HALF], total[HALF:BLK, 0:HALF], total[HALF:BLK, HALF:BLK]
         )
 
 
-def parts_kernel(here_ref, mine_ref, got_ref, *out_refs):
+def parts_kernel(here_ref, mine_ref, got_ref, pair_ref, *out_refs):
     c, own = here_ref[2], own_slot(here_ref)
-    for offset, out_ref in zip(OFFSETS, out_refs):
+    single = [offset for offset in OFFSETS if offset not in PAIR]
+    targets = [(offset, pair_ref.at[n]) for n, offset in enumerate(PAIR)] + list(zip(single, out_refs))
+    for offset, out_ref in targets:
         slot = (own + N_Z + offset) % N_Z
         k = rank(slot, c)
 
@@ -228,16 +223,7 @@
             theirs_ref[k] = rows(k, 1 - c)
 
 
-def spread_kernel(here_ref, own_ref, other_ref, out_ref):
-    c = here_ref[2]
-    for k in range(PER_CORE):
-        own, other = own_ref[k], other_ref[k]
-        for s in range(out_ref.shape[0]):
-            out_ref[s, c * PER_CORE + k] = own
-            out_ref[s, (1 - c) * PER_CORE + k] = other
-
-
-def precond_kernel(here_ref, owner_ref, own_ref, other_ref, grad_ref, out_ref, pick_ref, table_ref):
+def precond_kernel(here_ref, owner_ref, own_ref, other_ref, grad_ref, out_ref, table_ref):
     step = pl.program_id(0)
     k = step % PER_CORE
 
@@ -261,15 +247,21 @@
 
                 @pl.when(hit)
                 def _(count=count):
-                    table_ref[count] = s * nblocks + b
+                    table_ref[count] = s * nblocks + (b + here_ref[2] * PER_CORE) % nblocks
 
                 count = count + hit.astype(jnp.int32)
             return count
 
         lax.fori_loop(0, sections, section, jnp.int32(0))
-        block = lax.broadcasted_iota(jnp.int32, (1, sections * nblocks), 1)
-        for j in range(HOST):
-            pick_ref[j : j + 1, :] = (block == table_ref[j]).astype(f32)
+
+
+def hosted_kernel(table_ref, rows_ref, out_ref):
+    nblocks = rows_ref.shape[1]
+    for j in range(HOST):
+        source = table_ref[j]
+        at = jnp.maximum(source, 0)
+        rows = rows_ref[at // nblocks, at % nblocks]
+        out_ref[j] = jnp.where(source >= 0, rows, 0.0)
 
 
 def call(kernel, out_shape, n_smem, n_vmem):
@@ -292,20 +284,6 @@
 IN_SMEM = pl.BlockSpec(memory_space=pltpu.SMEM)
 
 
-def grams(here, features, other):
-    return pl.pallas_call(
-        functools.partial(gram_kernel, other=other),
-        out_shape=shape(PER_CORE, TALL, BLK),
-        in_specs=[IN_SMEM, pl.BlockSpec(memory_space=pl.ANY)],
-        out_specs=IN_VMEM,
-        scratch_shapes=[
-            VMEM((PER_CORE, features.shape[0], BLK), features.dtype),
-            pltpu.SemaphoreType.DMA((PER_CORE,)),
-        ],
-        compiler_params=pltpu.CompilerParams(vmem_limit_bytes=ALMOST_ALL if other else LIMIT),
-    )(here, features)
-
-
 def preconditioned(here, owner_of, own, other, grad):
     rows, columns = grad.shape
 
@@ -314,17 +292,15 @@
         return jnp.where(i < PER_CORE, c * PER_CORE + i, (1 - c) * PER_CORE + i - PER_CORE), 0
 
     part = pl.BlockSpec((BLK, columns), block)
-    pick = shape(HOST, owner_of.size)
     return pl.pallas_call(
         precond_kernel,
         grid_spec=pltpu.PrefetchScalarGridSpec(
             num_scalar_prefetch=1,
             grid=(rows // BLK,),
             in_specs=[IN_SMEM, IN_VMEM, IN_VMEM, part],
-            out_specs=[part, pl.BlockSpec(pick.shape, lambda i, here_ref: (0, 0))],
-            scratch_shapes=[pltpu.SMEM((HOST,), jnp.int32)],
+            out_specs=[part, IN_SMEM],
         ),
-        out_shape=[shape(rows, columns), pick],
+        out_shape=[shape(rows, columns), jax.ShapeDtypeStruct((HOST,), jnp.int32)],
         cost_estimate=pl.CostEstimate(
             flops=12 * rows * BLK * columns, bytes_accessed=16 * rows * columns, transcendentals=0
         ),
@@ -338,15 +314,18 @@
     here = jnp.stack([lax.axis_index(a) for a in ("x", "z", "c", "pipe")]).astype(jnp.int32)
     features = acts[0]
     one = shape(TALL, BLK)
-    got = across_cores(grams(here, features, True))
-    mine = grams(here, features, False)
-    part = dict(zip(OFFSETS, call(parts_kernel, [one] * N_Z, 1, 2)(here, mine, got)))
-
-    across = {1: across_x(part[5]), -1: across_x(part[3])}
+    packed = shape(PER_CORE, TALL, BLK)
+    got = across_cores(call(functools.partial(gram_kernel, other=True), packed, 1, 1)(here, features))
+    mine = call(functools.partial(gram_kernel, other=False), packed, 1, 1)(here, features)
+    single = [offset for offset in OFFSETS if offset not in PAIR]
+    parts = call(parts_kernel, [shape(2, TALL, BLK)] + [one] * len(single), 1, 2)(here, mine, got)
+    part = dict(zip(single, parts[1:]))
+
+    pair = across_x(parts[0])
     far = [along_z(part[2], 2), along_z(part[-2], -2)]
-    across[0] = across_x(part[4])
-    near = [along_z(part[1] + across[1], 1), along_z(part[-1] + across[-1], -1)]
-    half = part[0] + across[0] + far[0] + far[1] + near[0] + near[1]
+    across = across_x(part[4])
+    near = [along_z(part[1] + pair[0], 1), along_z(part[-1] + pair[1], -1)]
+    half = part[0] + across + far[0] + far[1] + near[0] + near[1]
     other_half = to_twin(half)
     inverse = call(functools.partial(invert_kernel, all_tokens=all_tokens), one, 1, 2)(
         here, half, other_half
@@ -359,13 +338,13 @@
     opened = [shape(PER_CORE, BLK, BLK)] + [shape(PER_CORE, SUB, BLK)] * 2
     own, own_rows, their_rows = call(unpack_kernel, opened, 1, N_Z)(here, *[held[k] for k in OFFSETS])
     other_rows = across_cores(their_rows)
+    rows = jnp.concatenate([own_rows, other_rows])
+    sent = jnp.broadcast_to(rows[None], (section_count, *rows.shape))
+    own, sent = lax.optimization_barrier((own, sent))
     other = across_cores(own)
-    sent = call(spread_kernel, shape(section_count, NB, SUB, BLK), 1, 2)(here, own_rows, other_rows)
     everyone = lax.all_to_all(sent, "pipe", 0, 0, tiled=True)
-    precond, pick = preconditioned(here, owner_of, own, other, grad)
-    hosted = jnp.einsum(
-        "jk,krc->jrc", pick, everyone.reshape(-1, SUB, BLK), precision=lax.Precision.HIGHEST
-    )
+    precond, table = preconditioned(here, owner_of, own, other, grad)
+    hosted = call(hosted_kernel, shape(HOST, SUB, BLK), 1, 1)(table, everyone)
     return (precond, hosted[None])
 
 

time: 102 us -> 93.6 us (0.918)
  waiting for transfers between devices: 25.1 us -> 20.7 us
  Pallas kernels: 30.3 us -> 27.7 us
  matrix products: 1.81 us -> 0 us
  local copies, waits for them, and re-layouts: 0.76 us -> 2.37 us
    ppermute x6 -> x5, starting transfers between devices: 14 us -> 9.11 us  [across_x(): return lax.ppermute(value, 'x', [(0, 1), (1, 0)])]
    pallas_call x4, Pallas kernels: 8.59 us -> 4.14 us  [the longest x1 1.38 us: shards(): hosted = call(hosted_kernel, shape(HOST, SUB, BLK), 1, 1)(table, everyone)]
    ppermute x6 -> x5, waiting for transfers between devices: 5.85 us -> 2.12 us  [across_x(): return lax.ppermute(value, 'x', [(0, 1), (1, 0)])]
    ppermute x8, waiting for transfers between devices: 5.45 us -> 8.85 us  [along_z(): return lax.ppermute(value, 'z', [(z, (z + step) % N_Z) for z in range(N_Z)])]
    ppermute x8, starting transfers between devices: 12.7 us -> 15.8 us  [along_z(): return lax.ppermute(value, 'z', [(z, (z + step) % N_Z) for z in range(N_Z)])]
    ppermute x1, waiting for transfers between devices: 7.27 us -> 5.15 us  [to_twin(): return lax.ppermute(value, ('x', 'z'), pairs)]
    dot_general x1 -> x0, matrix products: 1.81 us -> none  [shards(): jnp.einsum('jk,krc->jrc', pick, everyone.reshape(-1, SUB, BLK), precision...]
    ppermute x1, starting transfers between devices: 4.02 us -> 5.25 us  [to_twin(): return lax.ppermute(value, ('x', 'z'), pairs)]
  transfers between devices with their start and end apart: 19 -> 18, of which waited for: 8 -> 10; matrix products, arithmetic and copies ran while one was open for 0% -> 0% of each run, Pallas kernels for 13% -> 12%
where the time goes in v4:
time: 93.6 us; the launch traced here: 93.2 us
  starting transfers between devices  41.5 us (44%)
  Pallas kernels  27.7 us (30%)
  waiting for transfers between devices  20.7 us (22%)
  local copies, waits for them, and re-layouts  2.37 us (3%)
    ppermute x8, starting transfers between devices, along_z(): return lax.ppermute(value, 'z', [(z, (z + step) % N_Z) for z in range(N_Z)])  15.8 us
    pallas_call x1, Pallas kernels, shards(): call(functools.partial(invert_kernel, all_tokens=all_tokens), one, 1, 2)  11.3 us
    pallas_call x1, Pallas kernels, preconditioned(): pl.pallas_call(precond_kernel, grid_spec=pltpu.PrefetchScalarGridSpec(num...  9.84 us
    ppermute x5, starting transfers between devices, across_x(): return lax.ppermute(value, 'x', [(0, 1), (1, 0)])  9.11 us
    ppermute x8, waiting for transfers between devices, along_z(): return lax.ppermute(value, 'z', [(z, (z + step) % N_Z) for z in range(N_Z)])  8.85 us
    ppermute x3, starting transfers between devices, across_cores(): return lax.ppermute(value, 'c', [(0, 1), (1, 0)])  7.19 us
    ppermute x1, starting transfers between devices, to_twin(): return lax.ppermute(value, ('x', 'z'), pairs)  5.25 us
    ppermute x1, waiting for transfers between devices, to_twin(): return lax.ppermute(value, ('x', 'z'), pairs)  5.15 us
  transfers between devices with their start and end apart: 18, of which 10 were waited for; matrix products, arithmetic and copies ran while one was open for 0% of the time, Pallas kernels for 12%

profile of v4, /device:TPU:1, one launch (start us, length us, event | category | flops | bytes accessed | tf_op | source)
XLA Modules:
  0.0 93.2 jit_solution(6871037343668522405)
XLA Ops:
  0.6 0.1 pad_add_fusion.here_ref
  0.7 1.4 %copy-done = bf16[1,256,3072]{2,1,0:T(8,128)(2,1)S(1)} copy-done((bf16[1,256,3072]{2,1,0:T(8,128)(2,1)S(1)}, bf16[1,256,3072]{2,1,0:T(8,128)(2,1)}, u32[]{:S(2)}) %copy-start) | copy-done | bytes 1572888
  2.1 1.0 %shard_map.51 = f32[6,136,256]{2,1,0:T(8,128)S(1)} custom-call(s32[4]{0:T(128)S(1)} %pad_add_fusion.here_ref, bf16[256,3072]{1,0:T(8,128)(2,1)S(1)} %bitcast.14), custom_call_target="tpu_custom_call" | custom-call | tf_op jit(solution)/shard_map/pallas_call | solution.py:318
  3.1 3.3 %collective-permute-start = (f32[6,136,256]{2,1,0:T(8,128)S(1)}, f32[6,136,256]{2,1,0:T(8,128)S(1)}, u32[]{:S(2)}, u32[]{:S(2)}) collective-permute-start(f32[6,136,256]{2,1,0:T(8,128)S(1)} %shard_map.51), channel_id=1, source_target_pairs={{0,1},{1,0},{2,3},{3,2},{4,5},{5,4},{6,7},{7,6},{8,9},{9,8},{10,11... | collective-permute-start | bytes 2506760 | tf_op jit(solution)/shard_map/ppermute | solution.py:56
  6.4 1.0 %shard_map.50.mine_ref = f32[6,136,256]{2,1,0:T(8,128)S(1)} custom-call(s32[4]{0:T(128)S(1)} %pad_add_fusion.here_ref, bf16[256,3072]{1,0:T(8,128)(2,1)S(1)} %bitcast.15), custom_call_target="tpu_custom_call" | custom-call | tf_op jit(solution)/shard_map/pallas_call | solution.py:319
  7.4 1.0 %collective-permute-done.got_ref = f32[6,136,256]{2,1,0:T(8,128)S(1)} collective-permute-done((f32[6,136,256]{2,1,0:T(8,128)S(1)}, f32[6,136,256]{2,1,0:T(8,128)S(1)}, u32[]{:S(2)}, u32[]{:S(2)}) %collective-permute-start) | collective-permute-done | bytes 835616 | tf_op jit(solution)/shard_map/ppermute | solution.py:56
  8.4 0.8 shard_map.52
  9.2 1.1 %collective-permute-start.4 = (f32[2,136,256]{2,1,0:T(8,128)S(1)}, f32[2,136,256]{2,1,0:T(8,128)S(1)}, u32[]{:S(2)}, u32[]{:S(2)}) collective-permute-start(f32[2,136,256]{2,1,0:T(8,128)S(1)} %get-tuple-element.21), channel_id=1, source_target_pairs={{0,16},{16,0},{1,17},{17,1},{2,18},{18,2},{3,19},{19,3},{4,20},{20... | collective-permute-start | bytes 835592 | tf_op jit(solution)/shard_map/ppermute | solution.py:47
  10.3 2.0 %collective-permute-start.1 = (f32[136,256]{1,0:T(8,128)S(1)}, f32[136,256]{1,0:T(8,128)S(1)}, u32[]{:S(2)}, u32[]{:S(2)}) collective-permute-start(f32[136,256]{1,0:T(8,128)S(1)} %get-tuple-element.17), channel_id=1, source_target_pairs={{0,16},{16,0},{1,17},{17,1},{2,18},{18,2},{3,19},{19,3},{4,20},{20... | collective-permute-start | bytes 417800 | tf_op jit(solution)/shard_map/ppermute | solution.py:47
  12.3 1.3 %collective-permute-start.2 = (f32[136,256]{1,0:T(8,128)S(1)}, f32[136,256]{1,0:T(8,128)S(1)}, u32[]{:S(2)}, u32[]{:S(2)}) collective-permute-start(f32[136,256]{1,0:T(8,128)S(1)} %get-tuple-element.18), channel_id=1, source_target_pairs={{0,4},{2,6},{4,8},{6,10},{8,12},{10,14},{12,0},{14,2},{1,5},{3,7},... | collective-permute-start | bytes 417800 | tf_op jit(solution)/shard_map/ppermute | solution.py:43
  13.5 3.0 %collective-permute-start.3 = (f32[136,256]{1,0:T(8,128)S(1)}, f32[136,256]{1,0:T(8,128)S(1)}, u32[]{:S(2)}, u32[]{:S(2)}) collective-permute-start(f32[136,256]{1,0:T(8,128)S(1)} %get-tuple-element.19), channel_id=1, source_target_pairs={{0,12},{2,14},{4,0},{6,2},{8,4},{10,6},{12,8},{14,10},{1,13},{3,15... | collective-permute-start | bytes 417800 | tf_op jit(solution)/shard_map/ppermute | solution.py:43
  16.6 2.1 %collective-permute-done.4 = f32[2,136,256]{2,1,0:T(8,128)S(1)} collective-permute-done((f32[2,136,256]{2,1,0:T(8,128)S(1)}, f32[2,136,256]{2,1,0:T(8,128)S(1)}, u32[]{:S(2)}, u32[]{:S(2)}) %collective-permute-start.4) | collective-permute-done | bytes 278560 | tf_op jit(solution)/shard_map/ppermute | solution.py:47
  18.7 0.1 collective-permute-start.5
  18.8 3.9 %collective-permute-start.6 = (f32[136,256]{1,0:T(8,128)S(1)}, f32[136,256]{1,0:T(8,128)S(1)}, u32[]{:S(2)}, u32[]{:S(2)}) collective-permute-start(f32[136,256]{1,0:T(8,128)S(1)} %get-tuple-element.31), channel_id=1, source_target_pairs={{0,14},{2,0},{4,2},{6,4},{8,6},{10,8},{12,10},{14,12},{1,15},{3,1}... | collective-permute-start | bytes 417800 | tf_op jit(solution)/shard_map/ppermute | solution.py:43
  22.7 0.0 collective-permute-done.1
  22.7 0.0 collective-permute-done.2
  22.7 1.6 %collective-permute-done.3 = f32[136,256]{1,0:T(8,128)S(1)} collective-permute-done((f32[136,256]{1,0:T(8,128)S(1)}, f32[136,256]{1,0:T(8,128)S(1)}, u32[]{:S(2)}, u32[]{:S(2)}) %collective-permute-start.3) | collective-permute-done | bytes 139296 | tf_op jit(solution)/shard_map/ppermute | solution.py:43
  24.3 0.9 collective-permute-done.5
  25.2 1.7 %collective-permute-done.6 = f32[136,256]{1,0:T(8,128)S(1)} collective-permute-done((f32[136,256]{1,0:T(8,128)S(1)}, f32[136,256]{1,0:T(8,128)S(1)}, u32[]{:S(2)}, u32[]{:S(2)}) %collective-permute-start.6) | collective-permute-done | bytes 139296 | tf_op jit(solution)/shard_map/ppermute | solution.py:43
  26.9 0.1 add_add_fusion.a_ref
  27.0 5.3 %collective-permute-start.7 = (f32[136,256]{1,0:T(8,128)S(1)}, f32[136,256]{1,0:T(8,128)S(1)}, u32[]{:S(2)}, u32[]{:S(2)}) collective-permute-start(f32[136,256]{1,0:T(8,128)S(1)} %add_add_fusion.a_ref), channel_id=1, source_target_pairs={{0,24},{2,26},{4,28},{6,30},{8,16},{10,18},{12,20},{14,22},{16,8},... | collective-permute-start | bytes 417800 | tf_op jit(solution)/shard_map/ppermute | solution.py:52
  32.3 5.1 %collective-permute-done.7.b_ref = f32[136,256]{1,0:T(8,128)S(1)} collective-permute-done((f32[136,256]{1,0:T(8,128)S(1)}, f32[136,256]{1,0:T(8,128)S(1)}, u32[]{:S(2)}, u32[]{:S(2)}) %collective-permute-start.7) | collective-permute-done | bytes 139296 | tf_op jit(solution)/shard_map/ppermute | solution.py:52
  37.4 11.3 %shard_map.53.refs_0_ = f32[136,256]{1,0:T(8,128)S(1)} custom-call(s32[4]{0:T(128)S(1)} %pad_add_fusion.here_ref, f32[136,256]{1,0:T(8,128)S(1)} %add_add_fusion.a_ref, f32[136,256]{1,0:T(8,128)S(1)} %collective-permute-done.7.b_ref), custom_call_target="tpu_custom_call" | custom-call | tf_op jit(solution)/shard_map/pallas_call | solution.py:330
  48.7 0.1 collective-permute-start.9
  48.8 2.7 %collective-permute-start.8 = (f32[136,256]{1,0:T(8,128)S(1)}, f32[136,256]{1,0:T(8,128)S(1)}, u32[]{:S(2)}, u32[]{:S(2)}) collective-permute-start(f32[136,256]{1,0:T(8,128)S(1)} %shard_map.53.refs_0_), channel_id=1, source_target_pairs={{0,14},{2,0},{4,2},{6,4},{8,6},{10,8},{12,10},{14,12},{1,15},{3,1}... | collective-permute-start | bytes 417800 | tf_op jit(solution)/shard_map/ppermute | solution.py:43
  51.5 3.1 %collective-permute-start.13 = (f32[136,256]{1,0:T(8,128)S(1)}, f32[136,256]{1,0:T(8,128)S(1)}, u32[]{:S(2)}, u32[]{:S(2)}) collective-permute-start(f32[136,256]{1,0:T(8,128)S(1)} %shard_map.53.refs_0_), channel_id=1, source_target_pairs={{0,16},{16,0},{1,17},{17,1},{2,18},{18,2},{3,19},{19,3},{4,20},{20... | collective-permute-start | bytes 417800 | tf_op jit(solution)/shard_map/ppermute | solution.py:47
  54.6 4.8 %collective-permute-start.11 = (f32[136,256]{1,0:T(8,128)S(1)}, f32[136,256]{1,0:T(8,128)S(1)}, u32[]{:S(2)}, u32[]{:S(2)}) collective-permute-start(f32[136,256]{1,0:T(8,128)S(1)} %shard_map.53.refs_0_), channel_id=1, source_target_pairs={{0,4},{2,6},{4,8},{6,10},{8,12},{10,14},{12,0},{14,2},{1,5},{3,7},... | collective-permute-start | bytes 417800 | tf_op jit(solution)/shard_map/ppermute | solution.py:43
  59.3 0.0 collective-permute-start.10
  59.3 0.0 collective-permute-done.9.refs_2_
  59.3 0.1 collective-permute-start.12
  59.4 0.0 collective-permute-done.8.refs_1_
  59.4 2.9 %collective-permute-start.14 = (f32[136,256]{1,0:T(8,128)S(1)}, f32[136,256]{1,0:T(8,128)S(1)}, u32[]{:S(2)}, u32[]{:S(2)}) collective-permute-start(f32[136,256]{1,0:T(8,128)S(1)} %collective-permute-done.8.refs_1_), channel_id=1, source_target_pairs={{0,16},{16,0},{1,17},{17,1},{2,18},{18,2},{3,19},{19,3},{4,20},{20... | collective-permute-start | bytes 417800 | tf_op jit(solution)/shard_map/ppermute | solution.py:47
  62.3 0.0 collective-permute-done.13.refs_6_
  62.3 1.5 %collective-permute-done.11.refs_4_ = f32[136,256]{1,0:T(8,128)S(1)} collective-permute-done((f32[136,256]{1,0:T(8,128)S(1)}, f32[136,256]{1,0:T(8,128)S(1)}, u32[]{:S(2)}, u32[]{:S(2)}) %collective-permute-start.11) | collective-permute-done | bytes 139296 | tf_op jit(solution)/shard_map/ppermute | solution.py:43
  63.8 3.1 %collective-permute-done.10.refs_3_ = f32[136,256]{1,0:T(8,128)S(1)} collective-permute-done((f32[136,256]{1,0:T(8,128)S(1)}, f32[136,256]{1,0:T(8,128)S(1)}, u32[]{:S(2)}, u32[]{:S(2)}) %collective-permute-start.10) | collective-permute-done | bytes 139296 | tf_op jit(solution)/shard_map/ppermute | solution.py:43
  67.0 0.0 collective-permute-done.12.refs_5_
  67.0 0.0 collective-permute-done.14.refs_7_
  67.0 2.4 %shard_map.54 = (f32[6,256,256]{2,1,0:T(8,128)}, f32[6,8,256]{2,1,0:T(8,128)S(1)}, f32[6,8,256]{2,1,0:T(8,128)S(1)}) custom-call(s32[4]{0:T(128)S(1)} %pad_add_fusion.here_ref, f32[136,256]{1,0:T(8,128)S(1)} %shard_map.53.refs_0_, f32[136,256]{1,0:T(8,128)S(1)} %collective-permute-done.8.refs_1_, f32[136,256]{1,0:T(8,128)S(1)} %collective-permute-done.9.refs_2_, ...), custom_call_target="tpu_custom_call" | custom-call | tf_op jit(solution)/shard_map/pallas_call | solution.py:339
  69.4 3.5 %collective-permute-start.15 = (f32[6,8,256]{2,1,0:T(8,128)S(1)}, f32[6,8,256]{2,1,0:T(8,128)S(1)}, u32[]{:S(2)}, u32[]{:S(2)}) collective-permute-start(f32[6,8,256]{2,1,0:T(8,128)S(1)} %get-tuple-element.25), channel_id=1, source_target_pairs={{0,1},{1,0},{2,3},{3,2},{4,5},{5,4},{6,7},{7,6},{8,9},{9,8},{10,11... | collective-permute-start | bytes 147464 | tf_op jit(solution)/shard_map/ppermute | solution.py:56
  72.9 0.9 collective-permute-done.15
  73.8 1.0 %broadcast_in_dim.4 = f32[8,12,8,256]{3,2,1,0:T(8,128)} broadcast(f32[12,8,256]{2,1,0:T(8,128)S(1)} %pad_maximum_fusion), dimensions={1,2,3} | broadcast | bytes 884736 | tf_op jit(solution)/shard_map/broadcast_in_dim | solution.py:342
  74.8 0.4 collective-permute-start.16
  75.1 4.1 %all-to-all-start = ((f32[8,12,8,256]{3,2,1,0:T(8,128)}), f32[8,12,8,256]{3,2,1,0:T(8,128)S(1)}, u32[]{:S(2)}, u32[]{:S(2)}) async-start(f32[8,12,8,256]{3,2,1,0:T(8,128)} %broadcast_in_dim.4), calls=%async_computation | async-start | bytes 1572864 | tf_op jit(solution)/shard_map/all_to_all | solution.py:345
  79.2 0.0 collective-permute-done.16.other_ref
  79.2 0.0 copy-done.1
  79.2 9.8 %shard_map.55 = (f32[3072,128]{1,0:T(8,128)}, s32[24]{0:T(128)S(1)}) custom-call(s32[4]{0:T(128)S(1)} %pad_add_fusion.here_ref, s32[8,12]{1,0:T(8,128)S(1)} %copy-done.2, f32[6,256,256]{2,1,0:T(8,128)} %get-tuple-element.26.own_ref, f32[6,256,256]{2,1,0:T(8,128)} %collective-permute-done.16.other_ref, f32[3072,128]{1,0:T(8,128)S(1)} %copy-done.1), custom_call_target="tpu_custom_call" | custom-call | flops 1207959552 | bytes 6291456 | tf_op jit(solution)/shard_map/pallas_call | solution.py:295
  89.1 2.7 %all-to-all-done.rows_ref = f32[8,12,8,256]{3,2,1,0:T(8,128)S(1)} async-done(((f32[8,12,8,256]{3,2,1,0:T(8,128)}), f32[8,12,8,256]{3,2,1,0:T(8,128)S(1)}, u32[]{:S(2)}, u32[]{:S(2)}) %all-to-all-start) | async-done | bytes 786464 | tf_op jit(solution)/shard_map/all_to_all | solution.py:345
  91.8 1.4 %shard_map.56 = f32[24,8,256]{2,1,0:T(8,128)} custom-call(s32[24]{0:T(128)S(1)} %get-tuple-element.28.table_ref, f32[8,12,8,256]{3,2,1,0:T(8,128)S(1)} %all-to-all-done.rows_ref), custom_call_target="tpu_custom_call" | custom-call | tf_op jit(solution)/shard_map/pallas_call | solution.py:347
  (6 shorter events, 0.1 us)
Async XLA Ops:
  0.7 1.4 %copy-start = (bf16[1,256,3072]{2,1,0:T(8,128)(2,1)S(1)}, bf16[1,256,3072]{2,1,0:T(8,128)(2,1)}, u32[]{:S(2)}) copy-start(bf16[1,256,3072]{2,1,0:T(8,128)(2,1)} %param.3) | copy-start | bytes 4718596
  3.1 5.3 %collective-permute-start = (f32[6,136,256]{2,1,0:T(8,128)S(1)}, f32[6,136,256]{2,1,0:T(8,128)S(1)}, u32[]{:S(2)}, u32[]{:S(2)}) collective-permute-start(f32[6,136,256]{2,1,0:T(8,128)S(1)} %shard_map.51), channel_id=1, source_target_pairs={{0,1},{1,0},{2,3},{3,2},{4,5},{5,4},{6,7},{7,6},{8,9},{9,8},{10,11... | collective-permute-start | bytes 2506760 | tf_op jit(solution)/shard_map/ppermute | solution.py:56
  9.2 9.5 %collective-permute-start.4 = (f32[2,136,256]{2,1,0:T(8,128)S(1)}, f32[2,136,256]{2,1,0:T(8,128)S(1)}, u32[]{:S(2)}, u32[]{:S(2)}) collective-permute-start(f32[2,136,256]{2,1,0:T(8,128)S(1)} %get-tuple-element.21), channel_id=1, source_target_pairs={{0,16},{16,0},{1,17},{17,1},{2,18},{18,2},{3,19},{19,3},{4,20},{20... | collective-permute-start | bytes 835592 | tf_op jit(solution)/shard_map/ppermute | solution.py:47
  10.3 12.4 %collective-permute-start.1 = (f32[136,256]{1,0:T(8,128)S(1)}, f32[136,256]{1,0:T(8,128)S(1)}, u32[]{:S(2)}, u32[]{:S(2)}) collective-permute-start(f32[136,256]{1,0:T(8,128)S(1)} %get-tuple-element.17), channel_id=1, source_target_pairs={{0,16},{16,0},{1,17},{17,1},{2,18},{18,2},{3,19},{19,3},{4,20},{20... | collective-permute-start | bytes 417800 | tf_op jit(solution)/shard_map/ppermute | solution.py:47
  12.3 10.5 %collective-permute-start.2 = (f32[136,256]{1,0:T(8,128)S(1)}, f32[136,256]{1,0:T(8,128)S(1)}, u32[]{:S(2)}, u32[]{:S(2)}) collective-permute-start(f32[136,256]{1,0:T(8,128)S(1)} %get-tuple-element.18), channel_id=1, source_target_pairs={{0,4},{2,6},{4,8},{6,10},{8,12},{10,14},{12,0},{14,2},{1,5},{3,7},... | collective-permute-start | bytes 417800 | tf_op jit(solution)/shard_map/ppermute | solution.py:43
  13.5 10.8 %collective-permute-start.3 = (f32[136,256]{1,0:T(8,128)S(1)}, f32[136,256]{1,0:T(8,128)S(1)}, u32[]{:S(2)}, u32[]{:S(2)}) collective-permute-start(f32[136,256]{1,0:T(8,128)S(1)} %get-tuple-element.19), channel_id=1, source_target_pairs={{0,12},{2,14},{4,0},{6,2},{8,4},{10,6},{12,8},{14,10},{1,13},{3,15... | collective-permute-start | bytes 417800 | tf_op jit(solution)/shard_map/ppermute | solution.py:43
  18.7 6.5 %collective-permute-start.5 = (f32[136,256]{1,0:T(8,128)S(1)}, f32[136,256]{1,0:T(8,128)S(1)}, u32[]{:S(2)}, u32[]{:S(2)}) collective-permute-start(f32[136,256]{1,0:T(8,128)S(1)} %get-tuple-element.30), channel_id=1, source_target_pairs={{0,2},{2,4},{4,6},{6,8},{8,10},{10,12},{12,14},{14,0},{1,3},{3,5},... | collective-permute-start | bytes 417800 | tf_op jit(solution)/shard_map/ppermute | solution.py:43
  18.8 8.1 %collective-permute-start.6 = (f32[136,256]{1,0:T(8,128)S(1)}, f32[136,256]{1,0:T(8,128)S(1)}, u32[]{:S(2)}, u32[]{:S(2)}) collective-permute-start(f32[136,256]{1,0:T(8,128)S(1)} %get-tuple-element.31), channel_id=1, source_target_pairs={{0,14},{2,0},{4,2},{6,4},{8,6},{10,8},{12,10},{14,12},{1,15},{3,1}... | collective-permute-start | bytes 417800 | tf_op jit(solution)/shard_map/ppermute | solution.py:43
  27.0 10.4 %collective-permute-start.7 = (f32[136,256]{1,0:T(8,128)S(1)}, f32[136,256]{1,0:T(8,128)S(1)}, u32[]{:S(2)}, u32[]{:S(2)}) collective-permute-start(f32[136,256]{1,0:T(8,128)S(1)} %add_add_fusion.a_ref), channel_id=1, source_target_pairs={{0,24},{2,26},{4,28},{6,30},{8,16},{10,18},{12,20},{14,22},{16,8},... | collective-permute-start | bytes 417800 | tf_op jit(solution)/shard_map/ppermute | solution.py:52
  48.7 10.6 %collective-permute-start.9 = (f32[136,256]{1,0:T(8,128)S(1)}, f32[136,256]{1,0:T(8,128)S(1)}, u32[]{:S(2)}, u32[]{:S(2)}) collective-permute-start(f32[136,256]{1,0:T(8,128)S(1)} %shard_map.53.refs_0_), channel_id=1, source_target_pairs={{0,2},{2,4},{4,6},{6,8},{8,10},{10,12},{12,14},{14,0},{1,3},{3,5},... | collective-permute-start | bytes 417800 | tf_op jit(solution)/shard_map/ppermute | solution.py:43
  48.8 10.6 %collective-permute-start.8 = (f32[136,256]{1,0:T(8,128)S(1)}, f32[136,256]{1,0:T(8,128)S(1)}, u32[]{:S(2)}, u32[]{:S(2)}) collective-permute-start(f32[136,256]{1,0:T(8,128)S(1)} %shard_map.53.refs_0_), channel_id=1, source_target_pairs={{0,14},{2,0},{4,2},{6,4},{8,6},{10,8},{12,10},{14,12},{1,15},{3,1}... | collective-permute-start | bytes 417800 | tf_op jit(solution)/shard_map/ppermute | solution.py:43
  51.5 10.8 %collective-permute-start.13 = (f32[136,256]{1,0:T(8,128)S(1)}, f32[136,256]{1,0:T(8,128)S(1)}, u32[]{:S(2)}, u32[]{:S(2)}) collective-permute-start(f32[136,256]{1,0:T(8,128)S(1)} %shard_map.53.refs_0_), channel_id=1, source_target_pairs={{0,16},{16,0},{1,17},{17,1},{2,18},{18,2},{3,19},{19,3},{4,20},{20... | collective-permute-start | bytes 417800 | tf_op jit(solution)/shard_map/ppermute | solution.py:47
  54.6 9.3 %collective-permute-start.11 = (f32[136,256]{1,0:T(8,128)S(1)}, f32[136,256]{1,0:T(8,128)S(1)}, u32[]{:S(2)}, u32[]{:S(2)}) collective-permute-start(f32[136,256]{1,0:T(8,128)S(1)} %shard_map.53.refs_0_), channel_id=1, source_target_pairs={{0,4},{2,6},{4,8},{6,10},{8,12},{10,14},{12,0},{14,2},{1,5},{3,7},... | collective-permute-start | bytes 417800 | tf_op jit(solution)/shard_map/ppermute | solution.py:43
  59.3 7.6 %collective-permute-start.10 = (f32[136,256]{1,0:T(8,128)S(1)}, f32[136,256]{1,0:T(8,128)S(1)}, u32[]{:S(2)}, u32[]{:S(2)}) collective-permute-start(f32[136,256]{1,0:T(8,128)S(1)} %shard_map.53.refs_0_), channel_id=1, source_target_pairs={{0,12},{2,14},{4,0},{6,2},{8,4},{10,6},{12,8},{14,10},{1,13},{3,15... | collective-permute-start | bytes 417800 | tf_op jit(solution)/shard_map/ppermute | solution.py:43
  59.3 7.6 %collective-permute-start.12 = (f32[136,256]{1,0:T(8,128)S(1)}, f32[136,256]{1,0:T(8,128)S(1)}, u32[]{:S(2)}, u32[]{:S(2)}) collective-permute-start(f32[136,256]{1,0:T(8,128)S(1)} %collective-permute-done.9.refs_2_), channel_id=1, source_target_pairs={{0,16},{16,0},{1,17},{17,1},{2,18},{18,2},{3,19},{19,3},{4,20},{20... | collective-permute-start | bytes 417800 | tf_op jit(solution)/shard_map/ppermute | solution.py:47
  59.4 7.5 %collective-permute-start.14 = (f32[136,256]{1,0:T(8,128)S(1)}, f32[136,256]{1,0:T(8,128)S(1)}, u32[]{:S(2)}, u32[]{:S(2)}) collective-permute-start(f32[136,256]{1,0:T(8,128)S(1)} %collective-permute-done.8.refs_1_), channel_id=1, source_target_pairs={{0,16},{16,0},{1,17},{17,1},{2,18},{18,2},{3,19},{19,3},{4,20},{20... | collective-permute-start | bytes 417800 | tf_op jit(solution)/shard_map/ppermute | solution.py:47
  69.4 9.8 %copy-start.1 = (f32[3072,128]{1,0:T(8,128)S(1)}, f32[3072,128]{1,0:T(8,128)}, u32[]{:S(2)}) copy-start(f32[3072,128]{1,0:T(8,128)} %grad_ref.1) | copy-start | bytes 4718596
  69.4 9.8 %copy-start.2 = (s32[8,12]{1,0:T(8,128)S(1)}, s32[8,12]{1,0:T(8,128)}, u32[]{:S(2)}) copy-start(s32[8,12]{1,0:T(8,128)} %owner_ref.1) | copy-start | bytes 1156
  69.4 4.4 %collective-permute-start.15 = (f32[6,8,256]{2,1,0:T(8,128)S(1)}, f32[6,8,256]{2,1,0:T(8,128)S(1)}, u32[]{:S(2)}, u32[]{:S(2)}) collective-permute-start(f32[6,8,256]{2,1,0:T(8,128)S(1)} %get-tuple-element.25), channel_id=1, source_target_pairs={{0,1},{1,0},{2,3},{3,2},{4,5},{5,4},{6,7},{7,6},{8,9},{9,8},{10,11... | collective-permute-start | bytes 147464 | tf_op jit(solution)/shard_map/ppermute | solution.py:56
  74.8 4.5 %collective-permute-start.16 = (f32[6,256,256]{2,1,0:T(8,128)}, f32[6,256,256]{2,1,0:T(8,128)}, u32[]{:S(2)}, u32[]{:S(2)}) collective-permute-start(f32[6,256,256]{2,1,0:T(8,128)} %get-tuple-element.26.own_ref), channel_id=1, source_target_pairs={{0,1},{1,0},{2,3},{3,2},{4,5},{5,4},{6,7},{7,6},{8,9},{9,8},{10,11... | collective-permute-start | bytes 4718600 | tf_op jit(solution)/shard_map/ppermute | solution.py:56
  75.1 16.7 %all-to-all-start = ((f32[8,12,8,256]{3,2,1,0:T(8,128)}), f32[8,12,8,256]{3,2,1,0:T(8,128)S(1)}, u32[]{:S(2)}, u32[]{:S(2)}) async-start(f32[8,12,8,256]{3,2,1,0:T(8,128)} %broadcast_in_dim.4), calls=%async_computation | async-start | bytes 1572864 | tf_op jit(solution)/shard_map/all_to_all | solution.py:345

commit v5 on v4

--- a/solution.py
+++ b/solution.py
@@ -132,57 +132,55 @@
     return terms[0]
 
 
-def take_out(tiles, t):
-    first = SUB * t
-    lane = lax.broadcasted_iota(jnp.int32, (SUB, HALF), 1)
-    line = lax.broadcasted_iota(jnp.int32, (SUB, HALF), 0)
-    inside = (lane >= first) & (lane < first + SUB)
-    pivot = tiles[t]
-
-    def spread(v):
-        return jnp.broadcast_to(v, (SUB, HALF))
-
-    minus = small_inverse(
-        {
-            (i, j): spread(pivot[i : i + 1, first + j : first + j + 1])
-            for i in range(SUB)
-            for j in range(i + 1)
-        }
-    )
-    rows = [
-        jnp.where(lane == first + j, 1.0, jnp.where(inside, 0.0, spread(pivot[j : j + 1, :])))
-        for j in range(SUB)
-    ]
-    new = [
-        summed([minus[(max(i, j), min(i, j))] * rows[j] for j in range(SUB)]) for i in range(SUB)
-    ]
-    result = []
-    for v, tile in enumerate(tiles):
-        if v == t:
-            own = jnp.zeros((SUB, HALF), f32)
-            for j in range(SUB):
-                own = jnp.where(line == j, -new[j], own)
-            result.append(own)
-        else:
-            update = summed([spread(tile[:, first + j : first + j + 1]) * new[j] for j in range(SUB)])
-            result.append(jnp.where(inside, 0.0, tile) + update)
-    return result
-
-
-def half_inverse(value):
-    tiles = [value[SUB * v : SUB * v + SUB] for v in range(HALF // SUB)]
-    for t in range(len(tiles)):
-        tiles = take_out(tiles, t)
-    return jnp.concatenate(tiles, axis=0)
-
-
 def dot(a, b, dims=((1,), (0,))):
     return lax.dot_general(
         a, b, (dims, ((), ())), precision=lax.Precision.HIGHEST, preferred_element_type=f32
     )
 
 
-def invert_kernel(here_ref, a_ref, b_ref, out_ref, *, all_tokens):
+def half_inverse(value, rows_ref):
+    count = HALF // SUB
+    tiles = [value[SUB * v : SUB * v + SUB] for v in range(count)]
+    lane = lax.broadcasted_iota(jnp.int32, (SUB, HALF), 1)
+    line = lax.broadcasted_iota(jnp.int32, (SUB, HALF), 0)
+    lower, scaled = [], []
+
+    def spread(v):
+        return jnp.broadcast_to(v, (SUB, HALF))
+
+    for t, pivot in enumerate(tiles):
+        first = SUB * t
+        inside = (lane >= first) & (lane < first + SUB)
+        rows_ref[first : first + SUB, :] = pivot
+        each = [rows_ref[pl.ds(first + j, SUB, stride=0), :] for j in range(SUB)]
+        minus = small_inverse(
+            {
+                (i, j): spread(each[i][:, first + j : first + j + 1])
+                for i in range(SUB)
+                for j in range(i + 1)
+            }
+        )
+        rows = [
+            jnp.where(lane == first + j, 1.0, jnp.where(inside, 0.0, each[j])) for j in range(SUB)
+        ]
+        new = [
+            summed([minus[(max(i, j), min(i, j))] * rows[j] for j in range(SUB)])
+            for i in range(SUB)
+        ]
+        own = jnp.zeros((SUB, HALF), f32)
+        for j in range(SUB):
+            own = jnp.where(line == j, -new[j], own)
+        scaled.append(jnp.where(lane < first + SUB, own, 0.0))
+        lower.append(jnp.where(lane < first, pivot, jnp.where(lane == line + first, 1.0, 0.0)))
+        for v in range(t + 1, count):
+            update = summed(
+                [spread(tiles[v][:, first + j : first + j + 1]) * new[j] for j in range(SUB)]
+            )
+            tiles[v] = jnp.where(inside, 0.0, tiles[v]) + update
+    return dot(jnp.concatenate(lower, axis=0), jnp.concatenate(scaled, axis=0), ((0,), (0,)))
+
+
+def invert_kernel(here_ref, a_ref, b_ref, out_ref, rows_ref, *, all_tokens):
     @pl.when(holds(own_slot(here_ref), here_ref[2]))
     def _():
         upper, cross, lower = unpacked((a_ref[...] + b_ref[...]) * (1.0 / all_tokens))
@@ -193,20 +191,23 @@
         )
         damping = damping_ratio * trace / BLK
         shift = jnp.where(same, damping, 0.0)
-        first = half_inverse(upper + shift)
+        first = half_inverse(upper + shift, rows_ref.at[0])
         w = dot(cross, first)
-        second = half_inverse(lower + shift - dot(w, cross, ((1,), (1,))))
+        second = half_inverse(lower + shift - dot(w, cross, ((1,), (1,))), rows_ref.at[1])
         x = dot(second, w)
         store_packed(out_ref, first + dot(w, x, ((0,), (0,))), -x, second)
 
 
 def unpack_kernel(here_ref, *refs):
-    in_refs, (full_ref, mine_ref, theirs_ref) = refs[:N_Z], refs[N_Z:]
+    in_refs, (full_ref, mine_ref, theirs_ref, block_ref, done) = refs[:N_Z], refs[N_Z:]
     c, own = here_ref[2], own_slot(here_ref)
     start = (here_ref[0] * N_Z + here_ref[1]) * 2
 
     def rows(k, core):
-        return full_ref[k, pl.ds(pl.multiple_of((start + core) * SUB, SUB), SUB), :]
+        return block_ref[k, pl.ds(pl.multiple_of((start + core) * SUB, SUB), SUB), :]
+
+    def leave(k):
+        return pltpu.make_async_copy(block_ref.at[k], full_ref.at[k], done.at[k])
 
     for offset, ref in zip(OFFSETS, in_refs):
         slot = (own + N_Z + offset) % N_Z
@@ -215,12 +216,16 @@
         @pl.when(holds(slot, c))
         def _():
             upper, cross, lower = unpacked(ref[...])
-            full_ref[k, 0:HALF, 0:HALF] = upper
-            full_ref[k, 0:HALF, HALF:BLK] = cross.T
-            full_ref[k, HALF:BLK, 0:HALF] = cross
-            full_ref[k, HALF:BLK, HALF:BLK] = lower
+            block_ref[k, 0:HALF, 0:HALF] = upper
+            block_ref[k, 0:HALF, HALF:BLK] = cross.T
+            block_ref[k, HALF:BLK, 0:HALF] = cross
+            block_ref[k, HALF:BLK, HALF:BLK] = lower
+            leave(k).start()
             mine_ref[k] = rows(k, c)
             theirs_ref[k] = rows(k, 1 - c)
+
+    for k in range(PER_CORE):
+        leave(k).wait()
 
 
 def precond_kernel(here_ref, owner_ref, own_ref, other_ref, grad_ref, out_ref, table_ref):
@@ -264,7 +269,7 @@
         out_ref[j] = jnp.where(source >= 0, rows, 0.0)
 
 
-def call(kernel, out_shape, n_smem, n_vmem):
+def call(kernel, out_shape, n_smem, n_vmem, scratch=()):
     out_specs = jax.tree.map(lambda _: pl.BlockSpec(memory_space=VMEM), out_shape)
     return pl.pallas_call(
         kernel,
@@ -272,6 +277,7 @@
         in_specs=[pl.BlockSpec(memory_space=pltpu.SMEM)] * n_smem
         + [pl.BlockSpec(memory_space=VMEM)] * n_vmem,
         out_specs=out_specs,
+        scratch_shapes=scratch,
         compiler_params=pltpu.CompilerParams(vmem_limit_bytes=LIMIT),
     )
 
@@ -282,6 +288,17 @@
 
 IN_VMEM = pl.BlockSpec(memory_space=VMEM)
 IN_SMEM = pl.BlockSpec(memory_space=pltpu.SMEM)
+
+
+def unpack(here, values):
+    return pl.pallas_call(
+        unpack_kernel,
+        out_shape=[shape(PER_CORE, BLK, BLK)] + [shape(PER_CORE, SUB, BLK)] * 2,
+        in_specs=[IN_SMEM] + [IN_VMEM] * N_Z,
+        out_specs=[pl.BlockSpec(memory_space=pltpu.HBM), IN_VMEM, IN_VMEM],
+        scratch_shapes=[VMEM((PER_CORE, BLK, BLK), f32), pltpu.SemaphoreType.DMA((PER_CORE,))],
+        compiler_params=pltpu.CompilerParams(vmem_limit_bytes=LIMIT),
+    )(here, *values)
 
 
 def preconditioned(here, owner_of, own, other, grad):
@@ -327,16 +344,14 @@
     near = [along_z(part[1] + pair[0], 1), along_z(part[-1] + pair[1], -1)]
     half = part[0] + across + far[0] + far[1] + near[0] + near[1]
     other_half = to_twin(half)
-    inverse = call(functools.partial(invert_kernel, all_tokens=all_tokens), one, 1, 2)(
-        here, half, other_half
-    )
+    invert = functools.partial(invert_kernel, all_tokens=all_tokens)
+    inverse = call(invert, one, 1, 2, [VMEM((2, HALF, HALF), f32)])(here, half, other_half)
 
     held = {0: inverse, -1: along_z(inverse, 1), 1: along_z(inverse, -1)}
     held[4] = across_x(inverse)
     held[-2], held[2] = along_z(inverse, 2), along_z(inverse, -2)
     held[3], held[5] = across_x(held[-1]), across_x(held[1])
-    opened = [shape(PER_CORE, BLK, BLK)] + [shape(PER_CORE, SUB, BLK)] * 2
-    own, own_rows, their_rows = call(unpack_kernel, opened, 1, N_Z)(here, *[held[k] for k in OFFSETS])
+    own, own_rows, their_rows = unpack(here, [held[k] for k in OFFSETS])
     other_rows = across_cores(their_rows)
     rows = jnp.concatenate([own_rows, other_rows])
     sent = jnp.broadcast_to(rows[None], (section_count, *rows.shape))

time: 93.6 us -> 92.4 us (0.987)
  Pallas kernels: 27.7 us -> 26.3 us
    pallas_call x2, Pallas kernels: 13.7 us -> 12.4 us  [the longest x1 10.1 us: shards(): call(invert, one, 1, 2, [VMEM((2, HALF, HALF), f32)])]
where the time goes in v5:
time: 92.4 us; the launch traced here: 92 us
  starting transfers between devices  41.5 us (45%)
  Pallas kernels  26.3 us (28%)
  waiting for transfers between devices  20.7 us (22%)
  local copies, waits for them, and re-layouts  2.38 us (3%)
    ppermute x8, starting transfers between devices, along_z(): return lax.ppermute(value, 'z', [(z, (z + step) % N_Z) for z in range(N_Z)])  15.8 us
    pallas_call x1, Pallas kernels, shards(): call(invert, one, 1, 2, [VMEM((2, HALF, HALF), f32)])  10.1 us
    pallas_call x1, Pallas kernels, preconditioned(): pl.pallas_call(precond_kernel, grid_spec=pltpu.PrefetchScalarGridSpec(num...  9.84 us
    ppermute x5, starting transfers between devices, across_x(): return lax.ppermute(value, 'x', [(0, 1), (1, 0)])  9.1 us
    ppermute x8, waiting for transfers between devices, along_z(): return lax.ppermute(value, 'z', [(z, (z + step) % N_Z) for z in range(N_Z)])  8.86 us
    ppermute x3, starting transfers between devices, across_cores(): return lax.ppermute(value, 'c', [(0, 1), (1, 0)])  7.28 us
    ppermute x1, starting transfers between devices, to_twin(): return lax.ppermute(value, ('x', 'z'), pairs)  5.25 us
    ppermute x1, waiting for transfers between devices, to_twin(): return lax.ppermute(value, ('x', 'z'), pairs)  5.15 us
  transfers between devices with their start and end apart: 18, of which 10 were waited for; matrix products, arithmetic and copies ran while one was open for 0% of the time, Pallas kernels for 12%

profile of v5, /device:TPU:1, one launch (start us, length us, event | category | flops | bytes accessed | tf_op | source)
XLA Modules:
  0.0 92.0 jit_solution(16701646150151678866)
XLA Ops:
  0.6 0.1 pad_add_fusion.here_ref
  0.7 1.4 %copy-done = bf16[1,256,3072]{2,1,0:T(8,128)(2,1)S(1)} copy-done((bf16[1,256,3072]{2,1,0:T(8,128)(2,1)S(1)}, bf16[1,256,3072]{2,1,0:T(8,128)(2,1)}, u32[]{:S(2)}) %copy-start) | copy-done | bytes 1572888
  2.1 1.0 %shard_map.51 = f32[6,136,256]{2,1,0:T(8,128)S(1)} custom-call(s32[4]{0:T(128)S(1)} %pad_add_fusion.here_ref, bf16[256,3072]{1,0:T(8,128)(2,1)S(1)} %bitcast.14), custom_call_target="tpu_custom_call" | custom-call | tf_op jit(solution)/shard_map/pallas_call | solution.py:335
  3.1 3.3 %collective-permute-start = (f32[6,136,256]{2,1,0:T(8,128)S(1)}, f32[6,136,256]{2,1,0:T(8,128)S(1)}, u32[]{:S(2)}, u32[]{:S(2)}) collective-permute-start(f32[6,136,256]{2,1,0:T(8,128)S(1)} %shard_map.51), channel_id=1, source_target_pairs={{0,1},{1,0},{2,3},{3,2},{4,5},{5,4},{6,7},{7,6},{8,9},{9,8},{10,11... | collective-permute-start | bytes 2506760 | tf_op jit(solution)/shard_map/ppermute | solution.py:56
  6.4 1.0 %shard_map.50.mine_ref = f32[6,136,256]{2,1,0:T(8,128)S(1)} custom-call(s32[4]{0:T(128)S(1)} %pad_add_fusion.here_ref, bf16[256,3072]{1,0:T(8,128)(2,1)S(1)} %bitcast.15), custom_call_target="tpu_custom_call" | custom-call | tf_op jit(solution)/shard_map/pallas_call | solution.py:336
  7.4 1.0 %collective-permute-done.got_ref = f32[6,136,256]{2,1,0:T(8,128)S(1)} collective-permute-done((f32[6,136,256]{2,1,0:T(8,128)S(1)}, f32[6,136,256]{2,1,0:T(8,128)S(1)}, u32[]{:S(2)}, u32[]{:S(2)}) %collective-permute-start) | collective-permute-done | bytes 835616 | tf_op jit(solution)/shard_map/ppermute | solution.py:56
  8.4 0.8 shard_map.52
  9.2 1.1 %collective-permute-start.4 = (f32[2,136,256]{2,1,0:T(8,128)S(1)}, f32[2,136,256]{2,1,0:T(8,128)S(1)}, u32[]{:S(2)}, u32[]{:S(2)}) collective-permute-start(f32[2,136,256]{2,1,0:T(8,128)S(1)} %get-tuple-element.21), channel_id=1, source_target_pairs={{0,16},{16,0},{1,17},{17,1},{2,18},{18,2},{3,19},{19,3},{4,20},{20... | collective-permute-start | bytes 835592 | tf_op jit(solution)/shard_map/ppermute | solution.py:47
  10.3 2.0 %collective-permute-start.1 = (f32[136,256]{1,0:T(8,128)S(1)}, f32[136,256]{1,0:T(8,128)S(1)}, u32[]{:S(2)}, u32[]{:S(2)}) collective-permute-start(f32[136,256]{1,0:T(8,128)S(1)} %get-tuple-element.17), channel_id=1, source_target_pairs={{0,16},{16,0},{1,17},{17,1},{2,18},{18,2},{3,19},{19,3},{4,20},{20... | collective-permute-start | bytes 417800 | tf_op jit(solution)/shard_map/ppermute | solution.py:47
  12.3 1.3 %collective-permute-start.2 = (f32[136,256]{1,0:T(8,128)S(1)}, f32[136,256]{1,0:T(8,128)S(1)}, u32[]{:S(2)}, u32[]{:S(2)}) collective-permute-start(f32[136,256]{1,0:T(8,128)S(1)} %get-tuple-element.18), channel_id=1, source_target_pairs={{0,4},{2,6},{4,8},{6,10},{8,12},{10,14},{12,0},{14,2},{1,5},{3,7},... | collective-permute-start | bytes 417800 | tf_op jit(solution)/shard_map/ppermute | solution.py:43
  13.5 3.0 %collective-permute-start.3 = (f32[136,256]{1,0:T(8,128)S(1)}, f32[136,256]{1,0:T(8,128)S(1)}, u32[]{:S(2)}, u32[]{:S(2)}) collective-permute-start(f32[136,256]{1,0:T(8,128)S(1)} %get-tuple-element.19), channel_id=1, source_target_pairs={{0,12},{2,14},{4,0},{6,2},{8,4},{10,6},{12,8},{14,10},{1,13},{3,15... | collective-permute-start | bytes 417800 | tf_op jit(solution)/shard_map/ppermute | solution.py:43
  16.6 2.1 %collective-permute-done.4 = f32[2,136,256]{2,1,0:T(8,128)S(1)} collective-permute-done((f32[2,136,256]{2,1,0:T(8,128)S(1)}, f32[2,136,256]{2,1,0:T(8,128)S(1)}, u32[]{:S(2)}, u32[]{:S(2)}) %collective-permute-start.4) | collective-permute-done | bytes 278560 | tf_op jit(solution)/shard_map/ppermute | solution.py:47
  18.7 0.1 collective-permute-start.5
  18.8 3.9 %collective-permute-start.6 = (f32[136,256]{1,0:T(8,128)S(1)}, f32[136,256]{1,0:T(8,128)S(1)}, u32[]{:S(2)}, u32[]{:S(2)}) collective-permute-start(f32[136,256]{1,0:T(8,128)S(1)} %get-tuple-element.31), channel_id=1, source_target_pairs={{0,14},{2,0},{4,2},{6,4},{8,6},{10,8},{12,10},{14,12},{1,15},{3,1}... | collective-permute-start | bytes 417800 | tf_op jit(solution)/shard_map/ppermute | solution.py:43
  22.7 0.0 collective-permute-done.1
  22.7 0.0 collective-permute-done.2
  22.7 1.6 %collective-permute-done.3 = f32[136,256]{1,0:T(8,128)S(1)} collective-permute-done((f32[136,256]{1,0:T(8,128)S(1)}, f32[136,256]{1,0:T(8,128)S(1)}, u32[]{:S(2)}, u32[]{:S(2)}) %collective-permute-start.3) | collective-permute-done | bytes 139296 | tf_op jit(solution)/shard_map/ppermute | solution.py:43
  24.3 0.9 collective-permute-done.5
  25.2 1.7 %collective-permute-done.6 = f32[136,256]{1,0:T(8,128)S(1)} collective-permute-done((f32[136,256]{1,0:T(8,128)S(1)}, f32[136,256]{1,0:T(8,128)S(1)}, u32[]{:S(2)}, u32[]{:S(2)}) %collective-permute-start.6) | collective-permute-done | bytes 139296 | tf_op jit(solution)/shard_map/ppermute | solution.py:43
  26.9 0.1 add_add_fusion.a_ref
  27.0 5.3 %collective-permute-start.7 = (f32[136,256]{1,0:T(8,128)S(1)}, f32[136,256]{1,0:T(8,128)S(1)}, u32[]{:S(2)}, u32[]{:S(2)}) collective-permute-start(f32[136,256]{1,0:T(8,128)S(1)} %add_add_fusion.a_ref), channel_id=1, source_target_pairs={{0,24},{2,26},{4,28},{6,30},{8,16},{10,18},{12,20},{14,22},{16,8},... | collective-permute-start | bytes 417800 | tf_op jit(solution)/shard_map/ppermute | solution.py:52
  32.3 5.1 %collective-permute-done.7.b_ref = f32[136,256]{1,0:T(8,128)S(1)} collective-permute-done((f32[136,256]{1,0:T(8,128)S(1)}, f32[136,256]{1,0:T(8,128)S(1)}, u32[]{:S(2)}, u32[]{:S(2)}) %collective-permute-start.7) | collective-permute-done | bytes 139296 | tf_op jit(solution)/shard_map/ppermute | solution.py:52
  37.4 10.1 %shard_map.53.refs_0_ = f32[136,256]{1,0:T(8,128)S(1)} custom-call(s32[4]{0:T(128)S(1)} %pad_add_fusion.here_ref, f32[136,256]{1,0:T(8,128)S(1)} %add_add_fusion.a_ref, f32[136,256]{1,0:T(8,128)S(1)} %collective-permute-done.7.b_ref), custom_call_target="tpu_custom_call" | custom-call | tf_op jit(solution)/shard_map/pallas_call | solution.py:348
  47.5 0.1 collective-permute-start.9
  47.6 2.7 %collective-permute-start.8 = (f32[136,256]{1,0:T(8,128)S(1)}, f32[136,256]{1,0:T(8,128)S(1)}, u32[]{:S(2)}, u32[]{:S(2)}) collective-permute-start(f32[136,256]{1,0:T(8,128)S(1)} %shard_map.53.refs_0_), channel_id=1, source_target_pairs={{0,14},{2,0},{4,2},{6,4},{8,6},{10,8},{12,10},{14,12},{1,15},{3,1}... | collective-permute-start | bytes 417800 | tf_op jit(solution)/shard_map/ppermute | solution.py:43
  50.3 3.1 %collective-permute-start.13 = (f32[136,256]{1,0:T(8,128)S(1)}, f32[136,256]{1,0:T(8,128)S(1)}, u32[]{:S(2)}, u32[]{:S(2)}) collective-permute-start(f32[136,256]{1,0:T(8,128)S(1)} %shard_map.53.refs_0_), channel_id=1, source_target_pairs={{0,16},{16,0},{1,17},{17,1},{2,18},{18,2},{3,19},{19,3},{4,20},{20... | collective-permute-start | bytes 417800 | tf_op jit(solution)/shard_map/ppermute | solution.py:47
  53.4 4.8 %collective-permute-start.11 = (f32[136,256]{1,0:T(8,128)S(1)}, f32[136,256]{1,0:T(8,128)S(1)}, u32[]{:S(2)}, u32[]{:S(2)}) collective-permute-start(f32[136,256]{1,0:T(8,128)S(1)} %shard_map.53.refs_0_), channel_id=1, source_target_pairs={{0,4},{2,6},{4,8},{6,10},{8,12},{10,14},{12,0},{14,2},{1,5},{3,7},... | collective-permute-start | bytes 417800 | tf_op jit(solution)/shard_map/ppermute | solution.py:43
  58.1 0.0 collective-permute-start.10
  58.1 0.0 collective-permute-done.9.refs_2_
  58.1 0.1 collective-permute-start.12
  58.2 0.0 collective-permute-done.8.refs_1_
  58.2 2.9 %collective-permute-start.14 = (f32[136,256]{1,0:T(8,128)S(1)}, f32[136,256]{1,0:T(8,128)S(1)}, u32[]{:S(2)}, u32[]{:S(2)}) collective-permute-start(f32[136,256]{1,0:T(8,128)S(1)} %collective-permute-done.8.refs_1_), channel_id=1, source_target_pairs={{0,16},{16,0},{1,17},{17,1},{2,18},{18,2},{3,19},{19,3},{4,20},{20... | collective-permute-start | bytes 417800 | tf_op jit(solution)/shard_map/ppermute | solution.py:47
  61.1 0.0 collective-permute-done.13.refs_6_
  61.1 1.5 %collective-permute-done.11.refs_4_ = f32[136,256]{1,0:T(8,128)S(1)} collective-permute-done((f32[136,256]{1,0:T(8,128)S(1)}, f32[136,256]{1,0:T(8,128)S(1)}, u32[]{:S(2)}, u32[]{:S(2)}) %collective-permute-start.11) | collective-permute-done | bytes 139296 | tf_op jit(solution)/shard_map/ppermute | solution.py:43
  62.6 3.1 %collective-permute-done.10.refs_3_ = f32[136,256]{1,0:T(8,128)S(1)} collective-permute-done((f32[136,256]{1,0:T(8,128)S(1)}, f32[136,256]{1,0:T(8,128)S(1)}, u32[]{:S(2)}, u32[]{:S(2)}) %collective-permute-start.10) | collective-permute-done | bytes 139296 | tf_op jit(solution)/shard_map/ppermute | solution.py:43
  65.8 0.0 collective-permute-done.12.refs_5_
  65.8 2.2 %shard_map.54 = (f32[6,256,256]{2,1,0:T(8,128)}, f32[6,8,256]{2,1,0:T(8,128)S(1)}, f32[6,8,256]{2,1,0:T(8,128)S(1)}) custom-call(s32[4]{0:T(128)S(1)} %pad_add_fusion.here_ref, f32[136,256]{1,0:T(8,128)S(1)} %shard_map.53.refs_0_, f32[136,256]{1,0:T(8,128)S(1)} %collective-permute-done.8.refs_1_, f32[136,256]{1,0:T(8,128)S(1)} %collective-permute-done.9.refs_2_, ...), custom_call_target="tpu_custom_call" | custom-call | tf_op jit(solution)/shard_map/pallas_call | solution.py:294
  68.0 0.0 copy-start.1
  68.0 0.0 copy-start.2
  68.0 3.6 %collective-permute-start.15 = (f32[6,8,256]{2,1,0:T(8,128)S(1)}, f32[6,8,256]{2,1,0:T(8,128)S(1)}, u32[]{:S(2)}, u32[]{:S(2)}) collective-permute-start(f32[6,8,256]{2,1,0:T(8,128)S(1)} %get-tuple-element.25), channel_id=1, source_target_pairs={{0,1},{1,0},{2,3},{3,2},{4,5},{5,4},{6,7},{7,6},{8,9},{9,8},{10,11... | collective-permute-start | bytes 147464 | tf_op jit(solution)/shard_map/ppermute | solution.py:56
  71.6 0.9 collective-permute-done.15
  72.5 1.0 %broadcast_in_dim.4 = f32[8,12,8,256]{3,2,1,0:T(8,128)} broadcast(f32[12,8,256]{2,1,0:T(8,128)S(1)} %pad_maximum_fusion), dimensions={1,2,3} | broadcast | bytes 884736 | tf_op jit(solution)/shard_map/broadcast_in_dim | solution.py:357
  73.5 0.4 collective-permute-start.16
  73.8 4.1 %all-to-all-start = ((f32[8,12,8,256]{3,2,1,0:T(8,128)}), f32[8,12,8,256]{3,2,1,0:T(8,128)S(1)}, u32[]{:S(2)}, u32[]{:S(2)}) async-start(f32[8,12,8,256]{3,2,1,0:T(8,128)} %broadcast_in_dim.4), calls=%async_computation | async-start | bytes 1572864 | tf_op jit(solution)/shard_map/all_to_all | solution.py:360
  78.0 0.0 collective-permute-done.16.other_ref
  78.0 9.8 %shard_map.55 = (f32[3072,128]{1,0:T(8,128)}, s32[24]{0:T(128)S(1)}) custom-call(s32[4]{0:T(128)S(1)} %pad_add_fusion.here_ref, s32[8,12]{1,0:T(8,128)S(1)} %copy-done.2, f32[6,256,256]{2,1,0:T(8,128)} %get-tuple-element.26.own_ref, f32[6,256,256]{2,1,0:T(8,128)} %collective-permute-done.16.other_ref, f32[3072,128]{1,0:T(8,128)S(1)} %copy-done.1), custom_call_target="tpu_custom_call" | custom-call | flops 1207959552 | bytes 6291456 | tf_op jit(solution)/shard_map/pallas_call | solution.py:312
  87.8 2.7 %all-to-all-done.rows_ref = f32[8,12,8,256]{3,2,1,0:T(8,128)S(1)} async-done(((f32[8,12,8,256]{3,2,1,0:T(8,128)}), f32[8,12,8,256]{3,2,1,0:T(8,128)S(1)}, u32[]{:S(2)}, u32[]{:S(2)}) %all-to-all-start) | async-done | bytes 786464 | tf_op jit(solution)/shard_map/all_to_all | solution.py:360
  90.6 1.4 %shard_map.56 = f32[24,8,256]{2,1,0:T(8,128)} custom-call(s32[24]{0:T(128)S(1)} %get-tuple-element.28.table_ref, f32[8,12,8,256]{3,2,1,0:T(8,128)S(1)} %all-to-all-done.rows_ref), custom_call_target="tpu_custom_call" | custom-call | tf_op jit(solution)/shard_map/pallas_call | solution.py:362
  (6 shorter events, 0.1 us)
Async XLA Ops:
  0.7 1.4 %copy-start = (bf16[1,256,3072]{2,1,0:T(8,128)(2,1)S(1)}, bf16[1,256,3072]{2,1,0:T(8,128)(2,1)}, u32[]{:S(2)}) copy-start(bf16[1,256,3072]{2,1,0:T(8,128)(2,1)} %param.3) | copy-start | bytes 4718596
  3.1 5.3 %collective-permute-start = (f32[6,136,256]{2,1,0:T(8,128)S(1)}, f32[6,136,256]{2,1,0:T(8,128)S(1)}, u32[]{:S(2)}, u32[]{:S(2)}) collective-permute-start(f32[6,136,256]{2,1,0:T(8,128)S(1)} %shard_map.51), channel_id=1, source_target_pairs={{0,1},{1,0},{2,3},{3,2},{4,5},{5,4},{6,7},{7,6},{8,9},{9,8},{10,11... | collective-permute-start | bytes 2506760 | tf_op jit(solution)/shard_map/ppermute | solution.py:56
  9.2 9.5 %collective-permute-start.4 = (f32[2,136,256]{2,1,0:T(8,128)S(1)}, f32[2,136,256]{2,1,0:T(8,128)S(1)}, u32[]{:S(2)}, u32[]{:S(2)}) collective-permute-start(f32[2,136,256]{2,1,0:T(8,128)S(1)} %get-tuple-element.21), channel_id=1, source_target_pairs={{0,16},{16,0},{1,17},{17,1},{2,18},{18,2},{3,19},{19,3},{4,20},{20... | collective-permute-start | bytes 835592 | tf_op jit(solution)/shard_map/ppermute | solution.py:47
  10.3 12.4 %collective-permute-start.1 = (f32[136,256]{1,0:T(8,128)S(1)}, f32[136,256]{1,0:T(8,128)S(1)}, u32[]{:S(2)}, u32[]{:S(2)}) collective-permute-start(f32[136,256]{1,0:T(8,128)S(1)} %get-tuple-element.17), channel_id=1, source_target_pairs={{0,16},{16,0},{1,17},{17,1},{2,18},{18,2},{3,19},{19,3},{4,20},{20... | collective-permute-start | bytes 417800 | tf_op jit(solution)/shard_map/ppermute | solution.py:47
  12.3 10.5 %collective-permute-start.2 = (f32[136,256]{1,0:T(8,128)S(1)}, f32[136,256]{1,0:T(8,128)S(1)}, u32[]{:S(2)}, u32[]{:S(2)}) collective-permute-start(f32[136,256]{1,0:T(8,128)S(1)} %get-tuple-element.18), channel_id=1, source_target_pairs={{0,4},{2,6},{4,8},{6,10},{8,12},{10,14},{12,0},{14,2},{1,5},{3,7},... | collective-permute-start | bytes 417800 | tf_op jit(solution)/shard_map/ppermute | solution.py:43
  13.5 10.8 %collective-permute-start.3 = (f32[136,256]{1,0:T(8,128)S(1)}, f32[136,256]{1,0:T(8,128)S(1)}, u32[]{:S(2)}, u32[]{:S(2)}) collective-permute-start(f32[136,256]{1,0:T(8,128)S(1)} %get-tuple-element.19), channel_id=1, source_target_pairs={{0,12},{2,14},{4,0},{6,2},{8,4},{10,6},{12,8},{14,10},{1,13},{3,15... | collective-permute-start | bytes 417800 | tf_op jit(solution)/shard_map/ppermute | solution.py:43
  18.7 6.5 %collective-permute-start.5 = (f32[136,256]{1,0:T(8,128)S(1)}, f32[136,256]{1,0:T(8,128)S(1)}, u32[]{:S(2)}, u32[]{:S(2)}) collective-permute-start(f32[136,256]{1,0:T(8,128)S(1)} %get-tuple-element.30), channel_id=1, source_target_pairs={{0,2},{2,4},{4,6},{6,8},{8,10},{10,12},{12,14},{14,0},{1,3},{3,5},... | collective-permute-start | bytes 417800 | tf_op jit(solution)/shard_map/ppermute | solution.py:43
  18.8 8.1 %collective-permute-start.6 = (f32[136,256]{1,0:T(8,128)S(1)}, f32[136,256]{1,0:T(8,128)S(1)}, u32[]{:S(2)}, u32[]{:S(2)}) collective-permute-start(f32[136,256]{1,0:T(8,128)S(1)} %get-tuple-element.31), channel_id=1, source_target_pairs={{0,14},{2,0},{4,2},{6,4},{8,6},{10,8},{12,10},{14,12},{1,15},{3,1}... | collective-permute-start | bytes 417800 | tf_op jit(solution)/shard_map/ppermute | solution.py:43
  27.0 10.4 %collective-permute-start.7 = (f32[136,256]{1,0:T(8,128)S(1)}, f32[136,256]{1,0:T(8,128)S(1)}, u32[]{:S(2)}, u32[]{:S(2)}) collective-permute-start(f32[136,256]{1,0:T(8,128)S(1)} %add_add_fusion.a_ref), channel_id=1, source_target_pairs={{0,24},{2,26},{4,28},{6,30},{8,16},{10,18},{12,20},{14,22},{16,8},... | collective-permute-start | bytes 417800 | tf_op jit(solution)/shard_map/ppermute | solution.py:52
  47.5 10.6 %collective-permute-start.9 = (f32[136,256]{1,0:T(8,128)S(1)}, f32[136,256]{1,0:T(8,128)S(1)}, u32[]{:S(2)}, u32[]{:S(2)}) collective-permute-start(f32[136,256]{1,0:T(8,128)S(1)} %shard_map.53.refs_0_), channel_id=1, source_target_pairs={{0,2},{2,4},{4,6},{6,8},{8,10},{10,12},{12,14},{14,0},{1,3},{3,5},... | collective-permute-start | bytes 417800 | tf_op jit(solution)/shard_map/ppermute | solution.py:43
  47.6 10.6 %collective-permute-start.8 = (f32[136,256]{1,0:T(8,128)S(1)}, f32[136,256]{1,0:T(8,128)S(1)}, u32[]{:S(2)}, u32[]{:S(2)}) collective-permute-start(f32[136,256]{1,0:T(8,128)S(1)} %shard_map.53.refs_0_), channel_id=1, source_target_pairs={{0,14},{2,0},{4,2},{6,4},{8,6},{10,8},{12,10},{14,12},{1,15},{3,1}... | collective-permute-start | bytes 417800 | tf_op jit(solution)/shard_map/ppermute | solution.py:43
  50.3 10.8 %collective-permute-start.13 = (f32[136,256]{1,0:T(8,128)S(1)}, f32[136,256]{1,0:T(8,128)S(1)}, u32[]{:S(2)}, u32[]{:S(2)}) collective-permute-start(f32[136,256]{1,0:T(8,128)S(1)} %shard_map.53.refs_0_), channel_id=1, source_target_pairs={{0,16},{16,0},{1,17},{17,1},{2,18},{18,2},{3,19},{19,3},{4,20},{20... | collective-permute-start | bytes 417800 | tf_op jit(solution)/shard_map/ppermute | solution.py:47
  53.4 9.3 %collective-permute-start.11 = (f32[136,256]{1,0:T(8,128)S(1)}, f32[136,256]{1,0:T(8,128)S(1)}, u32[]{:S(2)}, u32[]{:S(2)}) collective-permute-start(f32[136,256]{1,0:T(8,128)S(1)} %shard_map.53.refs_0_), channel_id=1, source_target_pairs={{0,4},{2,6},{4,8},{6,10},{8,12},{10,14},{12,0},{14,2},{1,5},{3,7},... | collective-permute-start | bytes 417800 | tf_op jit(solution)/shard_map/ppermute | solution.py:43
  58.1 7.6 %collective-permute-start.10 = (f32[136,256]{1,0:T(8,128)S(1)}, f32[136,256]{1,0:T(8,128)S(1)}, u32[]{:S(2)}, u32[]{:S(2)}) collective-permute-start(f32[136,256]{1,0:T(8,128)S(1)} %shard_map.53.refs_0_), channel_id=1, source_target_pairs={{0,12},{2,14},{4,0},{6,2},{8,4},{10,6},{12,8},{14,10},{1,13},{3,15... | collective-permute-start | bytes 417800 | tf_op jit(solution)/shard_map/ppermute | solution.py:43
  58.1 7.6 %collective-permute-start.12 = (f32[136,256]{1,0:T(8,128)S(1)}, f32[136,256]{1,0:T(8,128)S(1)}, u32[]{:S(2)}, u32[]{:S(2)}) collective-permute-start(f32[136,256]{1,0:T(8,128)S(1)} %collective-permute-done.9.refs_2_), channel_id=1, source_target_pairs={{0,16},{16,0},{1,17},{17,1},{2,18},{18,2},{3,19},{19,3},{4,20},{20... | collective-permute-start | bytes 417800 | tf_op jit(solution)/shard_map/ppermute | solution.py:47
  58.2 7.5 %collective-permute-start.14 = (f32[136,256]{1,0:T(8,128)S(1)}, f32[136,256]{1,0:T(8,128)S(1)}, u32[]{:S(2)}, u32[]{:S(2)}) collective-permute-start(f32[136,256]{1,0:T(8,128)S(1)} %collective-permute-done.8.refs_1_), channel_id=1, source_target_pairs={{0,16},{16,0},{1,17},{17,1},{2,18},{18,2},{3,19},{19,3},{4,20},{20... | collective-permute-start | bytes 417800 | tf_op jit(solution)/shard_map/ppermute | solution.py:47
  68.0 9.9 %copy-start.1 = (f32[3072,128]{1,0:T(8,128)S(1)}, f32[3072,128]{1,0:T(8,128)}, u32[]{:S(2)}) copy-start(f32[3072,128]{1,0:T(8,128)} %grad_ref.1) | copy-start | bytes 4718596
  68.0 9.9 %copy-start.2 = (s32[8,12]{1,0:T(8,128)S(1)}, s32[8,12]{1,0:T(8,128)}, u32[]{:S(2)}) copy-start(s32[8,12]{1,0:T(8,128)} %owner_ref.1) | copy-start | bytes 1156
  68.0 4.5 %collective-permute-start.15 = (f32[6,8,256]{2,1,0:T(8,128)S(1)}, f32[6,8,256]{2,1,0:T(8,128)S(1)}, u32[]{:S(2)}, u32[]{:S(2)}) collective-permute-start(f32[6,8,256]{2,1,0:T(8,128)S(1)} %get-tuple-element.25), channel_id=1, source_target_pairs={{0,1},{1,0},{2,3},{3,2},{4,5},{5,4},{6,7},{7,6},{8,9},{9,8},{10,11... | collective-permute-start | bytes 147464 | tf_op jit(solution)/shard_map/ppermute | solution.py:56
  73.5 4.5 %collective-permute-start.16 = (f32[6,256,256]{2,1,0:T(8,128)}, f32[6,256,256]{2,1,0:T(8,128)}, u32[]{:S(2)}, u32[]{:S(2)}) collective-permute-start(f32[6,256,256]{2,1,0:T(8,128)} %get-tuple-element.26.own_ref), channel_id=1, source_target_pairs={{0,1},{1,0},{2,3},{3,2},{4,5},{5,4},{6,7},{7,6},{8,9},{9,8},{10,11... | collective-permute-start | bytes 4718600 | tf_op jit(solution)/shard_map/ppermute | solution.py:56
  73.8 16.7 %all-to-all-start = ((f32[8,12,8,256]{3,2,1,0:T(8,128)}), f32[8,12,8,256]{3,2,1,0:T(8,128)S(1)}, u32[]{:S(2)}, u32[]{:S(2)}) async-start(f32[8,12,8,256]{3,2,1,0:T(8,128)} %broadcast_in_dim.4), calls=%async_computation | async-start | bytes 1572864 | tf_op jit(solution)/shard_map/all_to_all | solution.py:360

commit v6 on v5

--- a/solution.py
+++ b/solution.py
@@ -24,7 +24,13 @@
 
 
 def own_slot(here_ref):
-    return (here_ref[1] + 4 * here_ref[0]) % N_Z
+    x, z, c = here_ref[0], here_ref[1], here_ref[2]
+    return (z + N_Z - 2 * (1 - 2 * c) * x) % N_Z
+
+
+def slot_at(here_ref, offset):
+    way = jnp.where(here_ref[0] == here_ref[2], 1, -1)
+    return (own_slot(here_ref) + N_Z + way * offset) % N_Z
 
 
 def holds(slot, c):
@@ -35,12 +41,22 @@
     return (slot // 4) * 3 + jnp.where(c == 0, slot % 4, (slot % 4 + 1) // 2)
 
 
-OFFSETS = (0, 1, -1, 2, -2, 3, 4, 5)
-PAIR = (5, 3)
+OFFSETS = (0, 1, -1, 2, -2, 3, -3, -4)
+PAIR = (-3, -4)
+
+
+def number(x, z, c):
+    return (x * N_Z + z % N_Z) * 2 + c
+
+
+PLACES = [(x, z, c) for x in range(2) for z in range(N_Z) for c in range(2)]
 
 
 def along_z(value, step):
-    return lax.ppermute(value, "z", [(z, (z + step) % N_Z) for z in range(N_Z)])
+    pairs = [
+        (number(x, z, c), number(x, z + (step if x == c else -step), c)) for x, z, c in PLACES
+    ]
+    return lax.ppermute(value, DP, pairs)
 
 
 def across_x(value):
@@ -48,8 +64,10 @@
 
 
 def to_twin(value):
-    pairs = [(x * N_Z + z, (1 - x) * N_Z + (z + 4) % N_Z) for x in range(2) for z in range(N_Z)]
-    return lax.ppermute(value, ("x", "z"), pairs)
+    pairs = [
+        (number(x, z, c), number(1 - x, z + (2 if x == c else -2), c)) for x, z, c in PLACES
+    ]
+    return lax.ppermute(value, DP, pairs)
 
 
 def across_cores(value):
@@ -95,11 +113,11 @@
 
 
 def parts_kernel(here_ref, mine_ref, got_ref, pair_ref, *out_refs):
-    c, own = here_ref[2], own_slot(here_ref)
+    c = here_ref[2]
     single = [offset for offset in OFFSETS if offset not in PAIR]
     targets = [(offset, pair_ref.at[n]) for n, offset in enumerate(PAIR)] + list(zip(single, out_refs))
     for offset, out_ref in targets:
-        slot = (own + N_Z + offset) % N_Z
+        slot = slot_at(here_ref, offset)
         k = rank(slot, c)
 
         @pl.when(holds(slot, c))
@@ -200,7 +218,7 @@
 
 def unpack_kernel(here_ref, *refs):
     in_refs, (full_ref, mine_ref, theirs_ref, block_ref, done) = refs[:N_Z], refs[N_Z:]
-    c, own = here_ref[2], own_slot(here_ref)
+    c = here_ref[2]
     start = (here_ref[0] * N_Z + here_ref[1]) * 2
 
     def rows(k, core):
@@ -210,7 +228,7 @@
         return pltpu.make_async_copy(block_ref.at[k], full_ref.at[k], done.at[k])
 
     for offset, ref in zip(OFFSETS, in_refs):
-        slot = (own + N_Z + offset) % N_Z
+        slot = slot_at(here_ref, offset)
         k = rank(slot, c)
 
         @pl.when(holds(slot, c))
@@ -339,23 +357,22 @@
     part = dict(zip(single, parts[1:]))
 
     pair = across_x(parts[0])
-    far = [along_z(part[2], 2), along_z(part[-2], -2)]
-    across = across_x(part[4])
-    near = [along_z(part[1] + pair[0], 1), along_z(part[-1] + pair[1], -1)]
-    half = part[0] + across + far[0] + far[1] + near[0] + near[1]
+    far = [along_z(part[offset], offset) for offset in (3, -2, -1)]
+    near = [along_z(part[1] + pair[0], 1), along_z(part[2] + pair[1], 2)]
+    half = part[0] + far[0] + far[1] + far[2] + near[0] + near[1]
     other_half = to_twin(half)
     invert = functools.partial(invert_kernel, all_tokens=all_tokens)
     inverse = call(invert, one, 1, 2, [VMEM((2, HALF, HALF), f32)])(here, half, other_half)
 
-    held = {0: inverse, -1: along_z(inverse, 1), 1: along_z(inverse, -1)}
-    held[4] = across_x(inverse)
-    held[-2], held[2] = along_z(inverse, 2), along_z(inverse, -2)
-    held[3], held[5] = across_x(held[-1]), across_x(held[1])
+    held = {0: inverse}
+    for offset in (1, 2, 3, -2, -1):
+        held[offset] = along_z(inverse, -offset)
+    held[-3], held[-4] = across_x(held[1]), across_x(held[2])
     own, own_rows, their_rows = unpack(here, [held[k] for k in OFFSETS])
     other_rows = across_cores(their_rows)
     rows = jnp.concatenate([own_rows, other_rows])
     sent = jnp.broadcast_to(rows[None], (section_count, *rows.shape))
-    own, sent = lax.optimization_barrier((own, sent))
+    own, sent, grad = lax.optimization_barrier((own, sent, grad))
     other = across_cores(own)
     everyone = lax.all_to_all(sent, "pipe", 0, 0, tiled=True)
     precond, table = preconditioned(here, owner_of, own, other, grad)

time: 92.4 us -> 93.8 us (1.015)
  waiting for transfers between devices: 20.7 us -> 29.4 us
  starting transfers between devices: 41.5 us -> 34.7 us
    ppermute x9 -> x11, waiting for transfers between devices: 14 us -> 24 us  [the longest x10 15 us: along_z(): return lax.ppermute(value, DP, pairs)]
    ppermute x5 -> x3, starting transfers between devices: 9.1 us -> 4.07 us  [across_x(): return lax.ppermute(value, 'x', [(0, 1), (1, 0)])]
    ppermute x3, starting transfers between devices: 7.28 us -> 5.16 us  [across_cores(): return lax.ppermute(value, 'c', [(0, 1), (1, 0)])]
    ppermute x5 -> x3, waiting for transfers between devices: 2.12 us -> 0.71 us  [across_x(): return lax.ppermute(value, 'x', [(0, 1), (1, 0)])]
    ppermute x9 -> x11, starting transfers between devices: 21.1 us -> 20.8 us  [the longest x10 19.2 us: along_z(): return lax.ppermute(value, DP, pairs)]
where the time goes in v6:
time: 93.8 us; the launch traced here: 93.6 us
  starting transfers between devices  34.7 us (37%)
  waiting for transfers between devices  29.4 us (31%)
  Pallas kernels  26.3 us (28%)
  local copies, waits for them, and re-layouts  2.38 us (3%)
    ppermute x10, starting transfers between devices, along_z(): return lax.ppermute(value, DP, pairs)  19.2 us
    ppermute x10, waiting for transfers between devices, along_z(): return lax.ppermute(value, DP, pairs)  15 us
    pallas_call x1, Pallas kernels, shards(): call(invert, one, 1, 2, [VMEM((2, HALF, HALF), f32)])  10.1 us
    pallas_call x1, Pallas kernels, preconditioned(): pl.pallas_call(precond_kernel, grid_spec=pltpu.PrefetchScalarGridSpec(num...  9.84 us
    ppermute x1, waiting for transfers between devices, to_twin(): return lax.ppermute(value, DP, pairs)  9.03 us
    ppermute x3, starting transfers between devices, across_cores(): return lax.ppermute(value, 'c', [(0, 1), (1, 0)])  5.16 us
    all_to_all x1, starting transfers between devices, shards(): everyone = lax.all_to_all(sent, 'pipe', 0, 0, tiled=True)  4.62 us
    ppermute x3, starting transfers between devices, across_x(): return lax.ppermute(value, 'x', [(0, 1), (1, 0)])  4.07 us
  transfers between devices with their start and end apart: 18, of which 10 were waited for; matrix products, arithmetic and copies ran while one was open for 0% of the time, Pallas kernels for 12%

profile of v6, /device:TPU:1, one launch (start us, length us, event | category | flops | bytes accessed | tf_op | source)
XLA Modules:
  0.0 93.6 jit_solution(18370194556065995053)
XLA Ops:
  0.6 0.1 pad_add_fusion.here_ref
  0.7 1.4 %copy-done = bf16[1,256,3072]{2,1,0:T(8,128)(2,1)S(1)} copy-done((bf16[1,256,3072]{2,1,0:T(8,128)(2,1)S(1)}, bf16[1,256,3072]{2,1,0:T(8,128)(2,1)}, u32[]{:S(2)}) %copy-start) | copy-done | bytes 1572888
  2.1 1.0 %shard_map.51 = f32[6,136,256]{2,1,0:T(8,128)S(1)} custom-call(s32[4]{0:T(128)S(1)} %pad_add_fusion.here_ref, bf16[256,3072]{1,0:T(8,128)(2,1)S(1)} %bitcast.14), custom_call_target="tpu_custom_call" | custom-call | tf_op jit(solution)/shard_map/pallas_call | solution.py:353
  3.1 3.3 %collective-permute-start = (f32[6,136,256]{2,1,0:T(8,128)S(1)}, f32[6,136,256]{2,1,0:T(8,128)S(1)}, u32[]{:S(2)}, u32[]{:S(2)}) collective-permute-start(f32[6,136,256]{2,1,0:T(8,128)S(1)} %shard_map.51), channel_id=1, source_target_pairs={{0,1},{1,0},{2,3},{3,2},{4,5},{5,4},{6,7},{7,6},{8,9},{9,8},{10,11... | collective-permute-start | bytes 2506760 | tf_op jit(solution)/shard_map/ppermute | solution.py:74
  6.4 1.0 %shard_map.50.mine_ref = f32[6,136,256]{2,1,0:T(8,128)S(1)} custom-call(s32[4]{0:T(128)S(1)} %pad_add_fusion.here_ref, bf16[256,3072]{1,0:T(8,128)(2,1)S(1)} %bitcast.15), custom_call_target="tpu_custom_call" | custom-call | tf_op jit(solution)/shard_map/pallas_call | solution.py:354
  7.4 1.0 %collective-permute-done.got_ref = f32[6,136,256]{2,1,0:T(8,128)S(1)} collective-permute-done((f32[6,136,256]{2,1,0:T(8,128)S(1)}, f32[6,136,256]{2,1,0:T(8,128)S(1)}, u32[]{:S(2)}, u32[]{:S(2)}) %collective-permute-start) | collective-permute-done | bytes 835616 | tf_op jit(solution)/shard_map/ppermute | solution.py:74
  8.4 0.9 shard_map.52
  9.3 1.1 %collective-permute-start.4 = (f32[2,136,256]{2,1,0:T(8,128)S(1)}, f32[2,136,256]{2,1,0:T(8,128)S(1)}, u32[]{:S(2)}, u32[]{:S(2)}) collective-permute-start(f32[2,136,256]{2,1,0:T(8,128)S(1)} %get-tuple-element.22), channel_id=1, source_target_pairs={{0,16},{16,0},{1,17},{17,1},{2,18},{18,2},{3,19},{19,3},{4,20},{20... | collective-permute-start | bytes 835592 | tf_op jit(solution)/shard_map/ppermute | solution.py:63
  10.4 6.5 %collective-permute-start.1 = (f32[136,256]{1,0:T(8,128)S(1)}, f32[136,256]{1,0:T(8,128)S(1)}, u32[]{:S(2)}, u32[]{:S(2)}) collective-permute-start(f32[136,256]{1,0:T(8,128)S(1)} %get-tuple-element.18), channel_id=1, source_target_pairs={{0,6},{1,11},{2,8},{3,13},{4,10},{5,15},{6,12},{7,1},{8,14},{9,3},... | collective-permute-start | bytes 417800 | tf_op jit(solution)/shard_map/ppermute | solution.py:59
  16.9 1.2 %collective-permute-start.2 = (f32[136,256]{1,0:T(8,128)S(1)}, f32[136,256]{1,0:T(8,128)S(1)}, u32[]{:S(2)}, u32[]{:S(2)}) collective-permute-start(f32[136,256]{1,0:T(8,128)S(1)} %get-tuple-element.19), channel_id=1, source_target_pairs={{0,12},{1,5},{2,14},{3,7},{4,0},{5,9},{6,2},{7,11},{8,4},{9,13},{1... | collective-permute-start | bytes 417800 | tf_op jit(solution)/shard_map/ppermute | solution.py:59
  18.1 0.0 collective-permute-start.3
  18.1 0.7 collective-permute-done.4
  18.8 3.9 %collective-permute-start.5 = (f32[136,256]{1,0:T(8,128)S(1)}, f32[136,256]{1,0:T(8,128)S(1)}, u32[]{:S(2)}, u32[]{:S(2)}) collective-permute-start(f32[136,256]{1,0:T(8,128)S(1)} %get-tuple-element.32), channel_id=1, source_target_pairs={{0,2},{1,15},{2,4},{3,1},{4,6},{5,3},{6,8},{7,5},{8,10},{9,7},{10,... | collective-permute-start | bytes 417800 | tf_op jit(solution)/shard_map/ppermute | solution.py:59
  22.7 1.2 %collective-permute-start.6 = (f32[136,256]{1,0:T(8,128)S(1)}, f32[136,256]{1,0:T(8,128)S(1)}, u32[]{:S(2)}, u32[]{:S(2)}) collective-permute-start(f32[136,256]{1,0:T(8,128)S(1)} %get-tuple-element.33), channel_id=1, source_target_pairs={{0,4},{1,13},{2,6},{3,15},{4,8},{5,1},{6,10},{7,3},{8,12},{9,5},{1... | collective-permute-start | bytes 417800 | tf_op jit(solution)/shard_map/ppermute | solution.py:59
  23.9 0.0 collective-permute-done.1
  23.9 1.1 %collective-permute-done.2 = f32[136,256]{1,0:T(8,128)S(1)} collective-permute-done((f32[136,256]{1,0:T(8,128)S(1)}, f32[136,256]{1,0:T(8,128)S(1)}, u32[]{:S(2)}, u32[]{:S(2)}) %collective-permute-start.2) | collective-permute-done | bytes 139296 | tf_op jit(solution)/shard_map/ppermute | solution.py:59
  25.0 3.5 %collective-permute-done.3 = f32[136,256]{1,0:T(8,128)S(1)} collective-permute-done((f32[136,256]{1,0:T(8,128)S(1)}, f32[136,256]{1,0:T(8,128)S(1)}, u32[]{:S(2)}, u32[]{:S(2)}) %collective-permute-start.3) | collective-permute-done | bytes 139296 | tf_op jit(solution)/shard_map/ppermute | solution.py:59
  28.5 0.0 collective-permute-done.5
  28.5 2.3 %collective-permute-done.6 = f32[136,256]{1,0:T(8,128)S(1)} collective-permute-done((f32[136,256]{1,0:T(8,128)S(1)}, f32[136,256]{1,0:T(8,128)S(1)}, u32[]{:S(2)}, u32[]{:S(2)}) %collective-permute-start.6) | collective-permute-done | bytes 139296 | tf_op jit(solution)/shard_map/ppermute | solution.py:59
  30.8 0.1 add_add_fusion.a_ref
  30.9 1.6 %collective-permute-start.7 = (f32[136,256]{1,0:T(8,128)S(1)}, f32[136,256]{1,0:T(8,128)S(1)}, u32[]{:S(2)}, u32[]{:S(2)}) collective-permute-start(f32[136,256]{1,0:T(8,128)S(1)} %add_add_fusion.a_ref), channel_id=1, source_target_pairs={{0,20},{1,29},{2,22},{3,31},{4,24},{5,17},{6,26},{7,19},{8,28},{9,... | collective-permute-start | bytes 417800 | tf_op jit(solution)/shard_map/ppermute | solution.py:70
  32.5 9.0 %collective-permute-done.7.b_ref = f32[136,256]{1,0:T(8,128)S(1)} collective-permute-done((f32[136,256]{1,0:T(8,128)S(1)}, f32[136,256]{1,0:T(8,128)S(1)}, u32[]{:S(2)}, u32[]{:S(2)}) %collective-permute-start.7) | collective-permute-done | bytes 139296 | tf_op jit(solution)/shard_map/ppermute | solution.py:70
  41.5 10.1 %shard_map.53.refs_0_ = f32[136,256]{1,0:T(8,128)S(1)} custom-call(s32[4]{0:T(128)S(1)} %pad_add_fusion.here_ref, f32[136,256]{1,0:T(8,128)S(1)} %add_add_fusion.a_ref, f32[136,256]{1,0:T(8,128)S(1)} %collective-permute-done.7.b_ref), custom_call_target="tpu_custom_call" | custom-call | tf_op jit(solution)/shard_map/pallas_call | solution.py:365
  51.6 0.1 collective-permute-start.10
  51.7 0.8 collective-permute-start.8
  52.5 3.4 %collective-permute-start.12 = (f32[136,256]{1,0:T(8,128)S(1)}, f32[136,256]{1,0:T(8,128)S(1)}, u32[]{:S(2)}, u32[]{:S(2)}) collective-permute-start(f32[136,256]{1,0:T(8,128)S(1)} %shard_map.53.refs_0_), channel_id=1, source_target_pairs={{0,10},{1,7},{2,12},{3,9},{4,14},{5,11},{6,0},{7,13},{8,2},{9,15},... | collective-permute-start | bytes 417800 | tf_op jit(solution)/shard_map/ppermute | solution.py:59
  55.9 2.2 %collective-permute-start.11 = (f32[136,256]{1,0:T(8,128)S(1)}, f32[136,256]{1,0:T(8,128)S(1)}, u32[]{:S(2)}, u32[]{:S(2)}) collective-permute-start(f32[136,256]{1,0:T(8,128)S(1)} %shard_map.53.refs_0_), channel_id=1, source_target_pairs={{0,4},{1,13},{2,6},{3,15},{4,8},{5,1},{6,10},{7,3},{8,12},{9,5},{1... | collective-permute-start | bytes 417800 | tf_op jit(solution)/shard_map/ppermute | solution.py:59
  58.1 0.0 collective-permute-start.9
  58.1 0.0 collective-permute-done.10.refs_3_
  58.1 0.7 collective-permute-start.14
  58.9 0.0 collective-permute-done.8.refs_1_
  58.9 2.2 %collective-permute-start.13 = (f32[136,256]{1,0:T(8,128)S(1)}, f32[136,256]{1,0:T(8,128)S(1)}, u32[]{:S(2)}, u32[]{:S(2)}) collective-permute-start(f32[136,256]{1,0:T(8,128)S(1)} %collective-permute-done.8.refs_1_), channel_id=1, source_target_pairs={{0,16},{16,0},{1,17},{17,1},{2,18},{18,2},{3,19},{19,3},{4,20},{20... | collective-permute-start | bytes 417800 | tf_op jit(solution)/shard_map/ppermute | solution.py:63
  61.1 5.4 %collective-permute-done.12.refs_5_ = f32[136,256]{1,0:T(8,128)S(1)} collective-permute-done((f32[136,256]{1,0:T(8,128)S(1)}, f32[136,256]{1,0:T(8,128)S(1)}, u32[]{:S(2)}, u32[]{:S(2)}) %collective-permute-start.12) | collective-permute-done | bytes 139296 | tf_op jit(solution)/shard_map/ppermute | solution.py:59
  66.5 0.0 collective-permute-done.11.refs_4_
  66.5 2.7 %collective-permute-done.9.refs_2_ = f32[136,256]{1,0:T(8,128)S(1)} collective-permute-done((f32[136,256]{1,0:T(8,128)S(1)}, f32[136,256]{1,0:T(8,128)S(1)}, u32[]{:S(2)}, u32[]{:S(2)}) %collective-permute-start.9) | collective-permute-done | bytes 139296 | tf_op jit(solution)/shard_map/ppermute | solution.py:59
  69.2 0.0 collective-permute-done.14.refs_7_
  69.2 0.0 collective-permute-done.13.refs_6_
  69.2 2.1 %shard_map.54 = (f32[6,256,256]{2,1,0:T(8,128)}, f32[6,8,256]{2,1,0:T(8,128)S(1)}, f32[6,8,256]{2,1,0:T(8,128)S(1)}) custom-call(s32[4]{0:T(128)S(1)} %pad_add_fusion.here_ref, f32[136,256]{1,0:T(8,128)S(1)} %shard_map.53.refs_0_, f32[136,256]{1,0:T(8,128)S(1)} %collective-permute-done.8.refs_1_, f32[136,256]{1,0:T(8,128)S(1)} %collective-permute-done.9.refs_2_, ...), custom_call_target="tpu_custom_call" | custom-call | tf_op jit(solution)/shard_map/pallas_call | solution.py:312
  71.3 0.0 copy-start.1
  71.3 0.0 copy-start.2
  71.3 1.5 %collective-permute-start.15 = (f32[6,8,256]{2,1,0:T(8,128)S(1)}, f32[6,8,256]{2,1,0:T(8,128)S(1)}, u32[]{:S(2)}, u32[]{:S(2)}) collective-permute-start(f32[6,8,256]{2,1,0:T(8,128)S(1)} %get-tuple-element.26), channel_id=1, source_target_pairs={{0,1},{1,0},{2,3},{3,2},{4,5},{5,4},{6,7},{7,6},{8,9},{9,8},{10,11... | collective-permute-start | bytes 147464 | tf_op jit(solution)/shard_map/ppermute | solution.py:74
  72.8 0.9 collective-permute-done.15
  73.7 1.0 %broadcast_in_dim.4 = f32[8,12,8,256]{3,2,1,0:T(8,128)} broadcast(f32[12,8,256]{2,1,0:T(8,128)S(1)} %pad_maximum_fusion), dimensions={1,2,3} | broadcast | bytes 884736 | tf_op jit(solution)/shard_map/broadcast_in_dim | solution.py:374
  74.7 0.4 collective-permute-start.16
  75.0 4.6 %all-to-all-start = ((f32[8,12,8,256]{3,2,1,0:T(8,128)}), f32[8,12,8,256]{3,2,1,0:T(8,128)S(1)}, u32[]{:S(2)}, u32[]{:S(2)}) async-start(f32[8,12,8,256]{3,2,1,0:T(8,128)} %broadcast_in_dim.4), calls=%async_computation | async-start | bytes 1572864 | tf_op jit(solution)/shard_map/all_to_all | solution.py:377
  79.7 9.8 %shard_map.55 = (f32[3072,128]{1,0:T(8,128)}, s32[24]{0:T(128)S(1)}) custom-call(s32[4]{0:T(128)S(1)} %pad_add_fusion.here_ref, s32[8,12]{1,0:T(8,128)S(1)} %copy-done.2, f32[6,256,256]{2,1,0:T(8,128)} %get-tuple-element.27.own_ref, f32[6,256,256]{2,1,0:T(8,128)} %collective-permute-done.16.other_ref, f32[3072,128]{1,0:T(8,128)S(1)} %copy-done.1), custom_call_target="tpu_custom_call" | custom-call | flops 1207959552 | bytes 6291456 | tf_op jit(solution)/shard_map/pallas_call | solution.py:330
  89.5 2.7 %all-to-all-done.rows_ref = f32[8,12,8,256]{3,2,1,0:T(8,128)S(1)} async-done(((f32[8,12,8,256]{3,2,1,0:T(8,128)}), f32[8,12,8,256]{3,2,1,0:T(8,128)S(1)}, u32[]{:S(2)}, u32[]{:S(2)}) %all-to-all-start) | async-done | bytes 786464 | tf_op jit(solution)/shard_map/all_to_all | solution.py:377
  92.2 1.4 %shard_map.56 = f32[24,8,256]{2,1,0:T(8,128)} custom-call(s32[24]{0:T(128)S(1)} %get-tuple-element.30.table_ref, f32[8,12,8,256]{3,2,1,0:T(8,128)S(1)} %all-to-all-done.rows_ref), custom_call_target="tpu_custom_call" | custom-call | tf_op jit(solution)/shard_map/pallas_call | solution.py:379
  (6 shorter events, 0.1 us)
Async XLA Ops:
  0.7 1.4 %copy-start = (bf16[1,256,3072]{2,1,0:T(8,128)(2,1)S(1)}, bf16[1,256,3072]{2,1,0:T(8,128)(2,1)}, u32[]{:S(2)}) copy-start(bf16[1,256,3072]{2,1,0:T(8,128)(2,1)} %param.3) | copy-start | bytes 4718596
  3.1 5.3 %collective-permute-start = (f32[6,136,256]{2,1,0:T(8,128)S(1)}, f32[6,136,256]{2,1,0:T(8,128)S(1)}, u32[]{:S(2)}, u32[]{:S(2)}) collective-permute-start(f32[6,136,256]{2,1,0:T(8,128)S(1)} %shard_map.51), channel_id=1, source_target_pairs={{0,1},{1,0},{2,3},{3,2},{4,5},{5,4},{6,7},{7,6},{8,9},{9,8},{10,11... | collective-permute-start | bytes 2506760 | tf_op jit(solution)/shard_map/ppermute | solution.py:74
  9.3 9.5 %collective-permute-start.4 = (f32[2,136,256]{2,1,0:T(8,128)S(1)}, f32[2,136,256]{2,1,0:T(8,128)S(1)}, u32[]{:S(2)}, u32[]{:S(2)}) collective-permute-start(f32[2,136,256]{2,1,0:T(8,128)S(1)} %get-tuple-element.22), channel_id=1, source_target_pairs={{0,16},{16,0},{1,17},{17,1},{2,18},{18,2},{3,19},{19,3},{4,20},{20... | collective-permute-start | bytes 835592 | tf_op jit(solution)/shard_map/ppermute | solution.py:63
  10.4 13.5 %collective-permute-start.1 = (f32[136,256]{1,0:T(8,128)S(1)}, f32[136,256]{1,0:T(8,128)S(1)}, u32[]{:S(2)}, u32[]{:S(2)}) collective-permute-start(f32[136,256]{1,0:T(8,128)S(1)} %get-tuple-element.18), channel_id=1, source_target_pairs={{0,6},{1,11},{2,8},{3,13},{4,10},{5,15},{6,12},{7,1},{8,14},{9,3},... | collective-permute-start | bytes 417800 | tf_op jit(solution)/shard_map/ppermute | solution.py:59
  16.9 8.1 %collective-permute-start.2 = (f32[136,256]{1,0:T(8,128)S(1)}, f32[136,256]{1,0:T(8,128)S(1)}, u32[]{:S(2)}, u32[]{:S(2)}) collective-permute-start(f32[136,256]{1,0:T(8,128)S(1)} %get-tuple-element.19), channel_id=1, source_target_pairs={{0,12},{1,5},{2,14},{3,7},{4,0},{5,9},{6,2},{7,11},{8,4},{9,13},{1... | collective-permute-start | bytes 417800 | tf_op jit(solution)/shard_map/ppermute | solution.py:59
  18.1 10.5 %collective-permute-start.3 = (f32[136,256]{1,0:T(8,128)S(1)}, f32[136,256]{1,0:T(8,128)S(1)}, u32[]{:S(2)}, u32[]{:S(2)}) collective-permute-start(f32[136,256]{1,0:T(8,128)S(1)} %get-tuple-element.20), channel_id=1, source_target_pairs={{0,14},{1,3},{2,0},{3,5},{4,2},{5,7},{6,4},{7,9},{8,6},{9,11},{10,... | collective-permute-start | bytes 417800 | tf_op jit(solution)/shard_map/ppermute | solution.py:59
  18.8 9.7 %collective-permute-start.5 = (f32[136,256]{1,0:T(8,128)S(1)}, f32[136,256]{1,0:T(8,128)S(1)}, u32[]{:S(2)}, u32[]{:S(2)}) collective-permute-start(f32[136,256]{1,0:T(8,128)S(1)} %get-tuple-element.32), channel_id=1, source_target_pairs={{0,2},{1,15},{2,4},{3,1},{4,6},{5,3},{6,8},{7,5},{8,10},{9,7},{10,... | collective-permute-start | bytes 417800 | tf_op jit(solution)/shard_map/ppermute | solution.py:59
  22.7 8.1 %collective-permute-start.6 = (f32[136,256]{1,0:T(8,128)S(1)}, f32[136,256]{1,0:T(8,128)S(1)}, u32[]{:S(2)}, u32[]{:S(2)}) collective-permute-start(f32[136,256]{1,0:T(8,128)S(1)} %get-tuple-element.33), channel_id=1, source_target_pairs={{0,4},{1,13},{2,6},{3,15},{4,8},{5,1},{6,10},{7,3},{8,12},{9,5},{1... | collective-permute-start | bytes 417800 | tf_op jit(solution)/shard_map/ppermute | solution.py:59
  30.9 10.6 %collective-permute-start.7 = (f32[136,256]{1,0:T(8,128)S(1)}, f32[136,256]{1,0:T(8,128)S(1)}, u32[]{:S(2)}, u32[]{:S(2)}) collective-permute-start(f32[136,256]{1,0:T(8,128)S(1)} %add_add_fusion.a_ref), channel_id=1, source_target_pairs={{0,20},{1,29},{2,22},{3,31},{4,24},{5,17},{6,26},{7,19},{8,28},{9,... | collective-permute-start | bytes 417800 | tf_op jit(solution)/shard_map/ppermute | solution.py:70
  51.6 6.5 %collective-permute-start.10 = (f32[136,256]{1,0:T(8,128)S(1)}, f32[136,256]{1,0:T(8,128)S(1)}, u32[]{:S(2)}, u32[]{:S(2)}) collective-permute-start(f32[136,256]{1,0:T(8,128)S(1)} %shard_map.53.refs_0_), channel_id=1, source_target_pairs={{0,12},{1,5},{2,14},{3,7},{4,0},{5,9},{6,2},{7,11},{8,4},{9,13},{1... | collective-permute-start | bytes 417800 | tf_op jit(solution)/shard_map/ppermute | solution.py:59
  51.7 7.1 %collective-permute-start.8 = (f32[136,256]{1,0:T(8,128)S(1)}, f32[136,256]{1,0:T(8,128)S(1)}, u32[]{:S(2)}, u32[]{:S(2)}) collective-permute-start(f32[136,256]{1,0:T(8,128)S(1)} %shard_map.53.refs_0_), channel_id=1, source_target_pairs={{0,14},{1,3},{2,0},{3,5},{4,2},{5,7},{6,4},{7,9},{8,6},{9,11},{10,... | collective-permute-start | bytes 417800 | tf_op jit(solution)/shard_map/ppermute | solution.py:59
  52.5 14.0 %collective-permute-start.12 = (f32[136,256]{1,0:T(8,128)S(1)}, f32[136,256]{1,0:T(8,128)S(1)}, u32[]{:S(2)}, u32[]{:S(2)}) collective-permute-start(f32[136,256]{1,0:T(8,128)S(1)} %shard_map.53.refs_0_), channel_id=1, source_target_pairs={{0,10},{1,7},{2,12},{3,9},{4,14},{5,11},{6,0},{7,13},{8,2},{9,15},... | collective-permute-start | bytes 417800 | tf_op jit(solution)/shard_map/ppermute | solution.py:59
  55.9 10.6 %collective-permute-start.11 = (f32[136,256]{1,0:T(8,128)S(1)}, f32[136,256]{1,0:T(8,128)S(1)}, u32[]{:S(2)}, u32[]{:S(2)}) collective-permute-start(f32[136,256]{1,0:T(8,128)S(1)} %shard_map.53.refs_0_), channel_id=1, source_target_pairs={{0,4},{1,13},{2,6},{3,15},{4,8},{5,1},{6,10},{7,3},{8,12},{9,5},{1... | collective-permute-start | bytes 417800 | tf_op jit(solution)/shard_map/ppermute | solution.py:59
  58.1 11.1 %collective-permute-start.9 = (f32[136,256]{1,0:T(8,128)S(1)}, f32[136,256]{1,0:T(8,128)S(1)}, u32[]{:S(2)}, u32[]{:S(2)}) collective-permute-start(f32[136,256]{1,0:T(8,128)S(1)} %shard_map.53.refs_0_), channel_id=1, source_target_pairs={{0,2},{1,15},{2,4},{3,1},{4,6},{5,3},{6,8},{7,5},{8,10},{9,7},{10,... | collective-permute-start | bytes 417800 | tf_op jit(solution)/shard_map/ppermute | solution.py:59
  58.1 11.1 %collective-permute-start.14 = (f32[136,256]{1,0:T(8,128)S(1)}, f32[136,256]{1,0:T(8,128)S(1)}, u32[]{:S(2)}, u32[]{:S(2)}) collective-permute-start(f32[136,256]{1,0:T(8,128)S(1)} %collective-permute-done.10.refs_3_), channel_id=1, source_target_pairs={{0,16},{16,0},{1,17},{17,1},{2,18},{18,2},{3,19},{19,3},{4,20},{20... | collective-permute-start | bytes 417800 | tf_op jit(solution)/shard_map/ppermute | solution.py:63
  58.9 10.3 %collective-permute-start.13 = (f32[136,256]{1,0:T(8,128)S(1)}, f32[136,256]{1,0:T(8,128)S(1)}, u32[]{:S(2)}, u32[]{:S(2)}) collective-permute-start(f32[136,256]{1,0:T(8,128)S(1)} %collective-permute-done.8.refs_1_), channel_id=1, source_target_pairs={{0,16},{16,0},{1,17},{17,1},{2,18},{18,2},{3,19},{19,3},{4,20},{20... | collective-permute-start | bytes 417800 | tf_op jit(solution)/shard_map/ppermute | solution.py:63
  71.3 8.3 %copy-start.1 = (f32[3072,128]{1,0:T(8,128)S(1)}, f32[3072,128]{1,0:T(8,128)}, u32[]{:S(2)}) copy-start(f32[3072,128]{1,0:T(8,128)} %grad_ref) | copy-start | bytes 4718596
  71.3 8.3 %copy-start.2 = (s32[8,12]{1,0:T(8,128)S(1)}, s32[8,12]{1,0:T(8,128)}, u32[]{:S(2)}) copy-start(s32[8,12]{1,0:T(8,128)} %owner_ref.1) | copy-start | bytes 1156
  71.3 2.4 %collective-permute-start.15 = (f32[6,8,256]{2,1,0:T(8,128)S(1)}, f32[6,8,256]{2,1,0:T(8,128)S(1)}, u32[]{:S(2)}, u32[]{:S(2)}) collective-permute-start(f32[6,8,256]{2,1,0:T(8,128)S(1)} %get-tuple-element.26), channel_id=1, source_target_pairs={{0,1},{1,0},{2,3},{3,2},{4,5},{5,4},{6,7},{7,6},{8,9},{9,8},{10,11... | collective-permute-start | bytes 147464 | tf_op jit(solution)/shard_map/ppermute | solution.py:74
  74.7 5.0 %collective-permute-start.16 = (f32[6,256,256]{2,1,0:T(8,128)}, f32[6,256,256]{2,1,0:T(8,128)}, u32[]{:S(2)}, u32[]{:S(2)}) collective-permute-start(f32[6,256,256]{2,1,0:T(8,128)} %get-tuple-element.27.own_ref), channel_id=1, source_target_pairs={{0,1},{1,0},{2,3},{3,2},{4,5},{5,4},{6,7},{7,6},{8,9},{9,8},{10,11... | collective-permute-start | bytes 4718600 | tf_op jit(solution)/shard_map/ppermute | solution.py:74
  75.0 17.2 %all-to-all-start = ((f32[8,12,8,256]{3,2,1,0:T(8,128)}), f32[8,12,8,256]{3,2,1,0:T(8,128)S(1)}, u32[]{:S(2)}, u32[]{:S(2)}) async-start(f32[8,12,8,256]{3,2,1,0:T(8,128)} %broadcast_in_dim.4), calls=%async_computation | async-start | bytes 1572864 | tf_op jit(solution)/shard_map/all_to_all | solution.py:377

commit v7 on v6

--- a/solution.py
+++ b/solution.py
@@ -357,16 +357,18 @@
     part = dict(zip(single, parts[1:]))
 
     pair = across_x(parts[0])
-    far = [along_z(part[offset], offset) for offset in (3, -2, -1)]
-    near = [along_z(part[1] + pair[0], 1), along_z(part[2] + pair[1], 2)]
-    half = part[0] + far[0] + far[1] + far[2] + near[0] + near[1]
+    step = along_z(part[3], 1)
+    far = [along_z(part[-2], -2), along_z(part[-1], -1)]
+    near = [along_z(part[1] + pair[0], 1), along_z(part[2] + step + pair[1], 2)]
+    half = part[0] + far[0] + far[1] + near[0] + near[1]
     other_half = to_twin(half)
     invert = functools.partial(invert_kernel, all_tokens=all_tokens)
     inverse = call(invert, one, 1, 2, [VMEM((2, HALF, HALF), f32)])(here, half, other_half)
 
     held = {0: inverse}
-    for offset in (1, 2, 3, -2, -1):
+    for offset in (2, 1, -2, -1):
         held[offset] = along_z(inverse, -offset)
+    held[3] = along_z(held[2], -1)
     held[-3], held[-4] = across_x(held[1]), across_x(held[2])
     own, own_rows, their_rows = unpack(here, [held[k] for k in OFFSETS])
     other_rows = across_cores(their_rows)

time: 93.8 us -> 95.6 us (1.019)
  starting transfers between devices: 34.7 us -> 40.4 us
  waiting for transfers between devices: 29.4 us -> 25.5 us
    ppermute x3, starting transfers between devices: 5.16 us -> 13.4 us  [across_cores(): return lax.ppermute(value, 'c', [(0, 1), (1, 0)])]
    ppermute x10, starting transfers between devices: 19.2 us -> 16.8 us  [along_z(): return lax.ppermute(value, DP, pairs)]
    ppermute x10, waiting for transfers between devices: 15 us -> 13 us  [along_z(): return lax.ppermute(value, DP, pairs)]
    ppermute x1, waiting for transfers between devices: 9.03 us -> 7.08 us  [to_twin(): return lax.ppermute(value, DP, pairs)]
    ppermute x1, starting transfers between devices: 1.61 us -> 2.92 us  [to_twin(): return lax.ppermute(value, DP, pairs)]
    ppermute x3, starting transfers between devices: 4.07 us -> 3.07 us  [across_x(): return lax.ppermute(value, 'x', [(0, 1), (1, 0)])]
  transfers between devices with their start and end apart: 18 -> 18, of which waited for: 10 -> 11; matrix products, arithmetic and copies ran while one was open for 0% -> 0% of each run, Pallas kernels for 12% -> 11%
where the time goes in v7:
time: 95.6 us; the launch traced here: 95.4 us
  starting transfers between devices  40.4 us (42%)
  Pallas kernels  26.3 us (28%)
  waiting for transfers between devices  25.5 us (27%)
  local copies, waits for them, and re-layouts  2.38 us (2%)
    ppermute x10, starting transfers between devices, along_z(): return lax.ppermute(value, DP, pairs)  16.8 us
    ppermute x3, starting transfers between devices, across_cores(): return lax.ppermute(value, 'c', [(0, 1), (1, 0)])  13.4 us
    ppermute x10, waiting for transfers between devices, along_z(): return lax.ppermute(value, DP, pairs)  13 us
    pallas_call x1, Pallas kernels, shards(): call(invert, one, 1, 2, [VMEM((2, HALF, HALF), f32)])  10.1 us
    pallas_call x1, Pallas kernels, preconditioned(): pl.pallas_call(precond_kernel, grid_spec=pltpu.PrefetchScalarGridSpec(num...  9.84 us
    ppermute x1, waiting for transfers between devices, to_twin(): return lax.ppermute(value, DP, pairs)  7.08 us
    all_to_all x1, starting transfers between devices, shards(): everyone = lax.all_to_all(sent, 'pipe', 0, 0, tiled=True)  4.23 us
    ppermute x3, starting transfers between devices, across_x(): return lax.ppermute(value, 'x', [(0, 1), (1, 0)])  3.07 us
  transfers between devices with their start and end apart: 18, of which 11 were waited for; matrix products, arithmetic and copies ran while one was open for 0% of the time, Pallas kernels for 11%

profile of v7, /device:TPU:1, one launch (start us, length us, event | category | flops | bytes accessed | tf_op | source)
XLA Modules:
  0.0 95.4 jit_solution(7415647192669584140)
XLA Ops:
  0.6 0.1 pad_add_fusion.here_ref
  0.7 1.4 %copy-done = bf16[1,256,3072]{2,1,0:T(8,128)(2,1)S(1)} copy-done((bf16[1,256,3072]{2,1,0:T(8,128)(2,1)S(1)}, bf16[1,256,3072]{2,1,0:T(8,128)(2,1)}, u32[]{:S(2)}) %copy-start) | copy-done | bytes 1572888
  2.1 1.0 %shard_map.51 = f32[6,136,256]{2,1,0:T(8,128)S(1)} custom-call(s32[4]{0:T(128)S(1)} %pad_add_fusion.here_ref, bf16[256,3072]{1,0:T(8,128)(2,1)S(1)} %bitcast.14), custom_call_target="tpu_custom_call" | custom-call | tf_op jit(solution)/shard_map/pallas_call | solution.py:353
  3.1 3.3 %collective-permute-start = (f32[6,136,256]{2,1,0:T(8,128)S(1)}, f32[6,136,256]{2,1,0:T(8,128)S(1)}, u32[]{:S(2)}, u32[]{:S(2)}) collective-permute-start(f32[6,136,256]{2,1,0:T(8,128)S(1)} %shard_map.51), channel_id=1, source_target_pairs={{0,1},{1,0},{2,3},{3,2},{4,5},{5,4},{6,7},{7,6},{8,9},{9,8},{10,11... | collective-permute-start | bytes 2506760 | tf_op jit(solution)/shard_map/ppermute | solution.py:74
  6.4 1.0 %shard_map.50.mine_ref = f32[6,136,256]{2,1,0:T(8,128)S(1)} custom-call(s32[4]{0:T(128)S(1)} %pad_add_fusion.here_ref, bf16[256,3072]{1,0:T(8,128)(2,1)S(1)} %bitcast.15), custom_call_target="tpu_custom_call" | custom-call | tf_op jit(solution)/shard_map/pallas_call | solution.py:354
  7.4 1.0 %collective-permute-done.got_ref = f32[6,136,256]{2,1,0:T(8,128)S(1)} collective-permute-done((f32[6,136,256]{2,1,0:T(8,128)S(1)}, f32[6,136,256]{2,1,0:T(8,128)S(1)}, u32[]{:S(2)}, u32[]{:S(2)}) %collective-permute-start) | collective-permute-done | bytes 835616 | tf_op jit(solution)/shard_map/ppermute | solution.py:74
  8.4 0.9 shard_map.52
  9.3 1.1 %collective-permute-start.3 = (f32[2,136,256]{2,1,0:T(8,128)S(1)}, f32[2,136,256]{2,1,0:T(8,128)S(1)}, u32[]{:S(2)}, u32[]{:S(2)}) collective-permute-start(f32[2,136,256]{2,1,0:T(8,128)S(1)} %get-tuple-element.21), channel_id=1, source_target_pairs={{0,16},{16,0},{1,17},{17,1},{2,18},{18,2},{3,19},{19,3},{4,20},{20... | collective-permute-start | bytes 835592 | tf_op jit(solution)/shard_map/ppermute | solution.py:63
  10.4 5.6 %collective-permute-start.5 = (f32[136,256]{1,0:T(8,128)S(1)}, f32[136,256]{1,0:T(8,128)S(1)}, u32[]{:S(2)}, u32[]{:S(2)}) collective-permute-start(f32[136,256]{1,0:T(8,128)S(1)} %get-tuple-element.23), channel_id=1, source_target_pairs={{0,2},{1,15},{2,4},{3,1},{4,6},{5,3},{6,8},{7,5},{8,10},{9,7},{10,... | collective-permute-start | bytes 417800 | tf_op jit(solution)/shard_map/ppermute | solution.py:59
  16.0 0.0 collective-permute-start.1
  16.0 0.0 collective-permute-start.2
  16.0 2.0 %collective-permute-done.5 = f32[136,256]{1,0:T(8,128)S(1)} collective-permute-done((f32[136,256]{1,0:T(8,128)S(1)}, f32[136,256]{1,0:T(8,128)S(1)}, u32[]{:S(2)}, u32[]{:S(2)}) %collective-permute-start.5) | collective-permute-done | bytes 139296 | tf_op jit(solution)/shard_map/ppermute | solution.py:59
  18.0 0.8 collective-permute-done.3
  18.8 0.1 fusion.1
  18.8 3.9 %collective-permute-start.4 = (f32[136,256]{1,0:T(8,128)S(1)}, f32[136,256]{1,0:T(8,128)S(1)}, u32[]{:S(2)}, u32[]{:S(2)}) collective-permute-start(f32[136,256]{1,0:T(8,128)S(1)} %get-tuple-element.32), channel_id=1, source_target_pairs={{0,2},{1,15},{2,4},{3,1},{4,6},{5,3},{6,8},{7,5},{8,10},{9,7},{10,... | collective-permute-start | bytes 417800 | tf_op jit(solution)/shard_map/ppermute | solution.py:59
  22.7 1.2 %collective-permute-start.6 = (f32[136,256]{1,0:T(8,128)S(1)}, f32[136,256]{1,0:T(8,128)S(1)}, u32[]{:S(2)}, u32[]{:S(2)}) collective-permute-start(f32[136,256]{1,0:T(8,128)S(1)} %get-tuple-element.33), channel_id=1, source_target_pairs={{0,4},{1,13},{2,6},{3,15},{4,8},{5,1},{6,10},{7,3},{8,12},{9,5},{1... | collective-permute-start | bytes 417800 | tf_op jit(solution)/shard_map/ppermute | solution.py:59
  23.9 0.0 collective-permute-done.1
  23.9 0.0 collective-permute-done.2
  23.9 0.8 collective-permute-done.4
  24.8 4.0 %collective-permute-done.6 = f32[136,256]{1,0:T(8,128)S(1)} collective-permute-done((f32[136,256]{1,0:T(8,128)S(1)}, f32[136,256]{1,0:T(8,128)S(1)}, u32[]{:S(2)}, u32[]{:S(2)}) %collective-permute-start.6) | collective-permute-done | bytes 139296 | tf_op jit(solution)/shard_map/ppermute | solution.py:59
  28.8 0.1 add_add_fusion.a_ref
  28.8 2.9 %collective-permute-start.7 = (f32[136,256]{1,0:T(8,128)S(1)}, f32[136,256]{1,0:T(8,128)S(1)}, u32[]{:S(2)}, u32[]{:S(2)}) collective-permute-start(f32[136,256]{1,0:T(8,128)S(1)} %add_add_fusion.a_ref), channel_id=1, source_target_pairs={{0,20},{1,29},{2,22},{3,31},{4,24},{5,17},{6,26},{7,19},{8,28},{9,... | collective-permute-start | bytes 417800 | tf_op jit(solution)/shard_map/ppermute | solution.py:70
  31.7 7.1 %collective-permute-done.7.b_ref = f32[136,256]{1,0:T(8,128)S(1)} collective-permute-done((f32[136,256]{1,0:T(8,128)S(1)}, f32[136,256]{1,0:T(8,128)S(1)}, u32[]{:S(2)}, u32[]{:S(2)}) %collective-permute-start.7) | collective-permute-done | bytes 139296 | tf_op jit(solution)/shard_map/ppermute | solution.py:70
  38.8 10.1 %shard_map.53.refs_0_ = f32[136,256]{1,0:T(8,128)S(1)} custom-call(s32[4]{0:T(128)S(1)} %pad_add_fusion.here_ref, f32[136,256]{1,0:T(8,128)S(1)} %add_add_fusion.a_ref, f32[136,256]{1,0:T(8,128)S(1)} %collective-permute-done.7.b_ref), custom_call_target="tpu_custom_call" | custom-call | tf_op jit(solution)/shard_map/pallas_call | solution.py:366
  48.9 0.1 collective-permute-start.10
  49.0 0.9 collective-permute-start.8
  49.9 2.7 %collective-permute-start.11 = (f32[136,256]{1,0:T(8,128)S(1)}, f32[136,256]{1,0:T(8,128)S(1)}, u32[]{:S(2)}, u32[]{:S(2)}) collective-permute-start(f32[136,256]{1,0:T(8,128)S(1)} %shard_map.53.refs_0_), channel_id=1, source_target_pairs={{0,4},{1,13},{2,6},{3,15},{4,8},{5,1},{6,10},{7,3},{8,12},{9,5},{1... | collective-permute-start | bytes 417800 | tf_op jit(solution)/shard_map/ppermute | solution.py:59
  52.6 1.5 %collective-permute-start.9 = (f32[136,256]{1,0:T(8,128)S(1)}, f32[136,256]{1,0:T(8,128)S(1)}, u32[]{:S(2)}, u32[]{:S(2)}) collective-permute-start(f32[136,256]{1,0:T(8,128)S(1)} %shard_map.53.refs_0_), channel_id=1, source_target_pairs={{0,2},{1,15},{2,4},{3,1},{4,6},{5,3},{6,8},{7,5},{8,10},{9,7},{10,... | collective-permute-start | bytes 417800 | tf_op jit(solution)/shard_map/ppermute | solution.py:59
  54.1 1.1 %collective-permute-done.10.refs_3_ = f32[136,256]{1,0:T(8,128)S(1)} collective-permute-done((f32[136,256]{1,0:T(8,128)S(1)}, f32[136,256]{1,0:T(8,128)S(1)}, u32[]{:S(2)}, u32[]{:S(2)}) %collective-permute-start.10) | collective-permute-done | bytes 139296 | tf_op jit(solution)/shard_map/ppermute | solution.py:59
  55.1 0.0 collective-permute-start.14
  55.1 1.0 %collective-permute-start.12 = (f32[136,256]{1,0:T(8,128)S(1)}, f32[136,256]{1,0:T(8,128)S(1)}, u32[]{:S(2)}, u32[]{:S(2)}) collective-permute-start(f32[136,256]{1,0:T(8,128)S(1)} %collective-permute-done.10.refs_3_), channel_id=1, source_target_pairs={{0,14},{1,3},{2,0},{3,5},{4,2},{5,7},{6,4},{7,9},{8,6},{9,11},{10,... | collective-permute-start | bytes 417800 | tf_op jit(solution)/shard_map/ppermute | solution.py:59
  56.1 2.0 %collective-permute-start.13 = (f32[136,256]{1,0:T(8,128)S(1)}, f32[136,256]{1,0:T(8,128)S(1)}, u32[]{:S(2)}, u32[]{:S(2)}) collective-permute-start(f32[136,256]{1,0:T(8,128)S(1)} %collective-permute-done.8.refs_1_), channel_id=1, source_target_pairs={{0,16},{16,0},{1,17},{17,1},{2,18},{18,2},{3,19},{19,3},{4,20},{20... | collective-permute-start | bytes 417800 | tf_op jit(solution)/shard_map/ppermute | solution.py:63
  58.1 0.0 collective-permute-done.11.refs_4_
  58.1 4.4 %collective-permute-done.9.refs_2_ = f32[136,256]{1,0:T(8,128)S(1)} collective-permute-done((f32[136,256]{1,0:T(8,128)S(1)}, f32[136,256]{1,0:T(8,128)S(1)}, u32[]{:S(2)}, u32[]{:S(2)}) %collective-permute-start.9) | collective-permute-done | bytes 139296 | tf_op jit(solution)/shard_map/ppermute | solution.py:59
  62.5 0.0 collective-permute-done.14.refs_7_
  62.5 0.7 collective-permute-done.12.refs_5_
  63.2 2.1 %shard_map.54 = (f32[6,256,256]{2,1,0:T(8,128)}, f32[6,8,256]{2,1,0:T(8,128)S(1)}, f32[6,8,256]{2,1,0:T(8,128)S(1)}) custom-call(s32[4]{0:T(128)S(1)} %pad_add_fusion.here_ref, f32[136,256]{1,0:T(8,128)S(1)} %shard_map.53.refs_0_, f32[136,256]{1,0:T(8,128)S(1)} %collective-permute-done.8.refs_1_, f32[136,256]{1,0:T(8,128)S(1)} %collective-permute-done.9.refs_2_, ...), custom_call_target="tpu_custom_call" | custom-call | tf_op jit(solution)/shard_map/pallas_call | solution.py:312
  65.3 0.0 copy-start.1
  65.3 0.0 copy-start.2
  65.3 9.7 %collective-permute-start.15 = (f32[6,8,256]{2,1,0:T(8,128)S(1)}, f32[6,8,256]{2,1,0:T(8,128)S(1)}, u32[]{:S(2)}, u32[]{:S(2)}) collective-permute-start(f32[6,8,256]{2,1,0:T(8,128)S(1)} %get-tuple-element.26), channel_id=1, source_target_pairs={{0,1},{1,0},{2,3},{3,2},{4,5},{5,4},{6,7},{7,6},{8,9},{9,8},{10,11... | collective-permute-start | bytes 147464 | tf_op jit(solution)/shard_map/ppermute | solution.py:74
  75.0 0.9 collective-permute-done.15
  75.9 1.0 %broadcast_in_dim.4 = f32[8,12,8,256]{3,2,1,0:T(8,128)} broadcast(f32[12,8,256]{2,1,0:T(8,128)S(1)} %pad_maximum_fusion), dimensions={1,2,3} | broadcast | bytes 884736 | tf_op jit(solution)/shard_map/broadcast_in_dim | solution.py:376
  76.8 0.4 collective-permute-start.16
  77.2 4.2 %all-to-all-start = ((f32[8,12,8,256]{3,2,1,0:T(8,128)}), f32[8,12,8,256]{3,2,1,0:T(8,128)S(1)}, u32[]{:S(2)}, u32[]{:S(2)}) async-start(f32[8,12,8,256]{3,2,1,0:T(8,128)} %broadcast_in_dim.4), calls=%async_computation | async-start | bytes 1572864 | tf_op jit(solution)/shard_map/all_to_all | solution.py:379
  81.4 0.0 collective-permute-done.16.other_ref
  81.4 9.8 %shard_map.55 = (f32[3072,128]{1,0:T(8,128)}, s32[24]{0:T(128)S(1)}) custom-call(s32[4]{0:T(128)S(1)} %pad_add_fusion.here_ref, s32[8,12]{1,0:T(8,128)S(1)} %copy-done.2, f32[6,256,256]{2,1,0:T(8,128)} %get-tuple-element.27.own_ref, f32[6,256,256]{2,1,0:T(8,128)} %collective-permute-done.16.other_ref, f32[3072,128]{1,0:T(8,128)S(1)} %copy-done.1), custom_call_target="tpu_custom_call" | custom-call | flops 1207959552 | bytes 6291456 | tf_op jit(solution)/shard_map/pallas_call | solution.py:330
  91.3 2.7 %all-to-all-done.rows_ref = f32[8,12,8,256]{3,2,1,0:T(8,128)S(1)} async-done(((f32[8,12,8,256]{3,2,1,0:T(8,128)}), f32[8,12,8,256]{3,2,1,0:T(8,128)S(1)}, u32[]{:S(2)}, u32[]{:S(2)}) %all-to-all-start) | async-done | bytes 786464 | tf_op jit(solution)/shard_map/all_to_all | solution.py:379
  94.0 1.4 %shard_map.56 = f32[24,8,256]{2,1,0:T(8,128)} custom-call(s32[24]{0:T(128)S(1)} %get-tuple-element.30.table_ref, f32[8,12,8,256]{3,2,1,0:T(8,128)S(1)} %all-to-all-done.rows_ref), custom_call_target="tpu_custom_call" | custom-call | tf_op jit(solution)/shard_map/pallas_call | solution.py:381
  (6 shorter events, 0.0 us)
Async XLA Ops:
  0.7 1.4 %copy-start = (bf16[1,256,3072]{2,1,0:T(8,128)(2,1)S(1)}, bf16[1,256,3072]{2,1,0:T(8,128)(2,1)}, u32[]{:S(2)}) copy-start(bf16[1,256,3072]{2,1,0:T(8,128)(2,1)} %param.3) | copy-start | bytes 4718596
  3.1 5.3 %collective-permute-start = (f32[6,136,256]{2,1,0:T(8,128)S(1)}, f32[6,136,256]{2,1,0:T(8,128)S(1)}, u32[]{:S(2)}, u32[]{:S(2)}) collective-permute-start(f32[6,136,256]{2,1,0:T(8,128)S(1)} %shard_map.51), channel_id=1, source_target_pairs={{0,1},{1,0},{2,3},{3,2},{4,5},{5,4},{6,7},{7,6},{8,9},{9,8},{10,11... | collective-permute-start | bytes 2506760 | tf_op jit(solution)/shard_map/ppermute | solution.py:74
  9.3 9.5 %collective-permute-start.3 = (f32[2,136,256]{2,1,0:T(8,128)S(1)}, f32[2,136,256]{2,1,0:T(8,128)S(1)}, u32[]{:S(2)}, u32[]{:S(2)}) collective-permute-start(f32[2,136,256]{2,1,0:T(8,128)S(1)} %get-tuple-element.21), channel_id=1, source_target_pairs={{0,16},{16,0},{1,17},{17,1},{2,18},{18,2},{3,19},{19,3},{4,20},{20... | collective-permute-start | bytes 835592 | tf_op jit(solution)/shard_map/ppermute | solution.py:63
  10.4 7.6 %collective-permute-start.5 = (f32[136,256]{1,0:T(8,128)S(1)}, f32[136,256]{1,0:T(8,128)S(1)}, u32[]{:S(2)}, u32[]{:S(2)}) collective-permute-start(f32[136,256]{1,0:T(8,128)S(1)} %get-tuple-element.23), channel_id=1, source_target_pairs={{0,2},{1,15},{2,4},{3,1},{4,6},{5,3},{6,8},{7,5},{8,10},{9,7},{10,... | collective-permute-start | bytes 417800 | tf_op jit(solution)/shard_map/ppermute | solution.py:59
  16.0 7.9 %collective-permute-start.1 = (f32[136,256]{1,0:T(8,128)S(1)}, f32[136,256]{1,0:T(8,128)S(1)}, u32[]{:S(2)}, u32[]{:S(2)}) collective-permute-start(f32[136,256]{1,0:T(8,128)S(1)} %get-tuple-element.18), channel_id=1, source_target_pairs={{0,12},{1,5},{2,14},{3,7},{4,0},{5,9},{6,2},{7,11},{8,4},{9,13},{1... | collective-permute-start | bytes 417800 | tf_op jit(solution)/shard_map/ppermute | solution.py:59
  16.0 7.9 %collective-permute-start.2 = (f32[136,256]{1,0:T(8,128)S(1)}, f32[136,256]{1,0:T(8,128)S(1)}, u32[]{:S(2)}, u32[]{:S(2)}) collective-permute-start(f32[136,256]{1,0:T(8,128)S(1)} %get-tuple-element.19), channel_id=1, source_target_pairs={{0,14},{1,3},{2,0},{3,5},{4,2},{5,7},{6,4},{7,9},{8,6},{9,11},{10,... | collective-permute-start | bytes 417800 | tf_op jit(solution)/shard_map/ppermute | solution.py:59
  18.8 5.9 %collective-permute-start.4 = (f32[136,256]{1,0:T(8,128)S(1)}, f32[136,256]{1,0:T(8,128)S(1)}, u32[]{:S(2)}, u32[]{:S(2)}) collective-permute-start(f32[136,256]{1,0:T(8,128)S(1)} %get-tuple-element.32), channel_id=1, source_target_pairs={{0,2},{1,15},{2,4},{3,1},{4,6},{5,3},{6,8},{7,5},{8,10},{9,7},{10,... | collective-permute-start | bytes 417800 | tf_op jit(solution)/shard_map/ppermute | solution.py:59
  22.7 6.0 %collective-permute-start.6 = (f32[136,256]{1,0:T(8,128)S(1)}, f32[136,256]{1,0:T(8,128)S(1)}, u32[]{:S(2)}, u32[]{:S(2)}) collective-permute-start(f32[136,256]{1,0:T(8,128)S(1)} %get-tuple-element.33), channel_id=1, source_target_pairs={{0,4},{1,13},{2,6},{3,15},{4,8},{5,1},{6,10},{7,3},{8,12},{9,5},{1... | collective-permute-start | bytes 417800 | tf_op jit(solution)/shard_map/ppermute | solution.py:59
  28.8 10.0 %collective-permute-start.7 = (f32[136,256]{1,0:T(8,128)S(1)}, f32[136,256]{1,0:T(8,128)S(1)}, u32[]{:S(2)}, u32[]{:S(2)}) collective-permute-start(f32[136,256]{1,0:T(8,128)S(1)} %add_add_fusion.a_ref), channel_id=1, source_target_pairs={{0,20},{1,29},{2,22},{3,31},{4,24},{5,17},{6,26},{7,19},{8,28},{9,... | collective-permute-start | bytes 417800 | tf_op jit(solution)/shard_map/ppermute | solution.py:70
  48.9 6.2 %collective-permute-start.10 = (f32[136,256]{1,0:T(8,128)S(1)}, f32[136,256]{1,0:T(8,128)S(1)}, u32[]{:S(2)}, u32[]{:S(2)}) collective-permute-start(f32[136,256]{1,0:T(8,128)S(1)} %shard_map.53.refs_0_), channel_id=1, source_target_pairs={{0,12},{1,5},{2,14},{3,7},{4,0},{5,9},{6,2},{7,11},{8,4},{9,13},{1... | collective-permute-start | bytes 417800 | tf_op jit(solution)/shard_map/ppermute | solution.py:59
  49.0 7.1 %collective-permute-start.8 = (f32[136,256]{1,0:T(8,128)S(1)}, f32[136,256]{1,0:T(8,128)S(1)}, u32[]{:S(2)}, u32[]{:S(2)}) collective-permute-start(f32[136,256]{1,0:T(8,128)S(1)} %shard_map.53.refs_0_), channel_id=1, source_target_pairs={{0,14},{1,3},{2,0},{3,5},{4,2},{5,7},{6,4},{7,9},{8,6},{9,11},{10,... | collective-permute-start | bytes 417800 | tf_op jit(solution)/shard_map/ppermute | solution.py:59
  49.9 8.2 %collective-permute-start.11 = (f32[136,256]{1,0:T(8,128)S(1)}, f32[136,256]{1,0:T(8,128)S(1)}, u32[]{:S(2)}, u32[]{:S(2)}) collective-permute-start(f32[136,256]{1,0:T(8,128)S(1)} %shard_map.53.refs_0_), channel_id=1, source_target_pairs={{0,4},{1,13},{2,6},{3,15},{4,8},{5,1},{6,10},{7,3},{8,12},{9,5},{1... | collective-permute-start | bytes 417800 | tf_op jit(solution)/shard_map/ppermute | solution.py:59
  52.6 9.9 %collective-permute-start.9 = (f32[136,256]{1,0:T(8,128)S(1)}, f32[136,256]{1,0:T(8,128)S(1)}, u32[]{:S(2)}, u32[]{:S(2)}) collective-permute-start(f32[136,256]{1,0:T(8,128)S(1)} %shard_map.53.refs_0_), channel_id=1, source_target_pairs={{0,2},{1,15},{2,4},{3,1},{4,6},{5,3},{6,8},{7,5},{8,10},{9,7},{10,... | collective-permute-start | bytes 417800 | tf_op jit(solution)/shard_map/ppermute | solution.py:59
  55.1 7.4 %collective-permute-start.14 = (f32[136,256]{1,0:T(8,128)S(1)}, f32[136,256]{1,0:T(8,128)S(1)}, u32[]{:S(2)}, u32[]{:S(2)}) collective-permute-start(f32[136,256]{1,0:T(8,128)S(1)} %collective-permute-done.10.refs_3_), channel_id=1, source_target_pairs={{0,16},{16,0},{1,17},{17,1},{2,18},{18,2},{3,19},{19,3},{4,20},{20... | collective-permute-start | bytes 417800 | tf_op jit(solution)/shard_map/ppermute | solution.py:63
  55.1 8.0 %collective-permute-start.12 = (f32[136,256]{1,0:T(8,128)S(1)}, f32[136,256]{1,0:T(8,128)S(1)}, u32[]{:S(2)}, u32[]{:S(2)}) collective-permute-start(f32[136,256]{1,0:T(8,128)S(1)} %collective-permute-done.10.refs_3_), channel_id=1, source_target_pairs={{0,14},{1,3},{2,0},{3,5},{4,2},{5,7},{6,4},{7,9},{8,6},{9,11},{10,... | collective-permute-start | bytes 417800 | tf_op jit(solution)/shard_map/ppermute | solution.py:59
  56.1 7.0 %collective-permute-start.13 = (f32[136,256]{1,0:T(8,128)S(1)}, f32[136,256]{1,0:T(8,128)S(1)}, u32[]{:S(2)}, u32[]{:S(2)}) collective-permute-start(f32[136,256]{1,0:T(8,128)S(1)} %collective-permute-done.8.refs_1_), channel_id=1, source_target_pairs={{0,16},{16,0},{1,17},{17,1},{2,18},{18,2},{3,19},{19,3},{4,20},{20... | collective-permute-start | bytes 417800 | tf_op jit(solution)/shard_map/ppermute | solution.py:63
  65.3 16.1 %copy-start.1 = (f32[3072,128]{1,0:T(8,128)S(1)}, f32[3072,128]{1,0:T(8,128)}, u32[]{:S(2)}) copy-start(f32[3072,128]{1,0:T(8,128)} %grad_ref) | copy-start | bytes 4718596
  65.3 16.1 %copy-start.2 = (s32[8,12]{1,0:T(8,128)S(1)}, s32[8,12]{1,0:T(8,128)}, u32[]{:S(2)}) copy-start(s32[8,12]{1,0:T(8,128)} %owner_ref.1) | copy-start | bytes 1156
  65.3 10.6 %collective-permute-start.15 = (f32[6,8,256]{2,1,0:T(8,128)S(1)}, f32[6,8,256]{2,1,0:T(8,128)S(1)}, u32[]{:S(2)}, u32[]{:S(2)}) collective-permute-start(f32[6,8,256]{2,1,0:T(8,128)S(1)} %get-tuple-element.26), channel_id=1, source_target_pairs={{0,1},{1,0},{2,3},{3,2},{4,5},{5,4},{6,7},{7,6},{8,9},{9,8},{10,11... | collective-permute-start | bytes 147464 | tf_op jit(solution)/shard_map/ppermute | solution.py:74
  76.8 4.6 %collective-permute-start.16 = (f32[6,256,256]{2,1,0:T(8,128)}, f32[6,256,256]{2,1,0:T(8,128)}, u32[]{:S(2)}, u32[]{:S(2)}) collective-permute-start(f32[6,256,256]{2,1,0:T(8,128)} %get-tuple-element.27.own_ref), channel_id=1, source_target_pairs={{0,1},{1,0},{2,3},{3,2},{4,5},{5,4},{6,7},{7,6},{8,9},{9,8},{10,11... | collective-permute-start | bytes 4718600 | tf_op jit(solution)/shard_map/ppermute | solution.py:74
  77.2 16.8 %all-to-all-start = ((f32[8,12,8,256]{3,2,1,0:T(8,128)}), f32[8,12,8,256]{3,2,1,0:T(8,128)S(1)}, u32[]{:S(2)}, u32[]{:S(2)}) async-start(f32[8,12,8,256]{3,2,1,0:T(8,128)} %broadcast_in_dim.4), calls=%async_computation | async-start | bytes 1572864 | tf_op jit(solution)/shard_map/all_to_all | solution.py:379

commit v8 on v5

--- a/solution.py
+++ b/solution.py
@@ -14,7 +14,7 @@
 NB = 12
 PER_CORE = NB // 2
 HOST = 24
-TALL = HALF + SUB
+TALL = 2 * HALF + SUB
 N_Z = 8
 DP = ("x", "z", "c")
 damping_ratio = 0.1
@@ -65,17 +65,16 @@
 
 def store_packed(ref, upper, cross, lower):
     i, j = grids()
-    ref[0:HALF, 0:HALF] = cross
-    ref[0:HALF, HALF:BLK] = jnp.where(i >= j, upper, lower)
-    ref[HALF:TALL, 0:HALF] = jnp.broadcast_to(
+    ref[0:HALF, :] = cross
+    ref[HALF:BLK, :] = jnp.where(i >= j, upper, lower)
+    ref[BLK:TALL, :] = jnp.broadcast_to(
         jnp.sum(jnp.where(i == j, lower, 0.0), axis=0, keepdims=True), (SUB, HALF)
     )
-    ref[HALF:TALL, HALF:BLK] = jnp.zeros((SUB, HALF), f32)
 
 
 def unpacked(value):
     i, j = grids()
-    cross, mixed, diagonal = value[0:HALF, 0:HALF], value[0:HALF, HALF:BLK], value[HALF : HALF + 1, 0:HALF]
+    cross, mixed, diagonal = value[0:HALF], value[HALF:BLK], value[BLK : BLK + 1]
     turned = mixed.T
     upper = jnp.where(i >= j, mixed, turned)
     lower = jnp.where(i < j, mixed, jnp.where(i > j, turned, diagonal))
@@ -330,12 +329,12 @@
     all_tokens = acts.shape[1] * lax.axis_size(DP)
     here = jnp.stack([lax.axis_index(a) for a in ("x", "z", "c", "pipe")]).astype(jnp.int32)
     features = acts[0]
-    one = shape(TALL, BLK)
-    packed = shape(PER_CORE, TALL, BLK)
+    one = shape(TALL, HALF)
+    packed = shape(PER_CORE, TALL, HALF)
     got = across_cores(call(functools.partial(gram_kernel, other=True), packed, 1, 1)(here, features))
     mine = call(functools.partial(gram_kernel, other=False), packed, 1, 1)(here, features)
     single = [offset for offset in OFFSETS if offset not in PAIR]
-    parts = call(parts_kernel, [shape(2, TALL, BLK)] + [one] * len(single), 1, 2)(here, mine, got)
+    parts = call(parts_kernel, [shape(2, TALL, HALF)] + [one] * len(single), 1, 2)(here, mine, got)
     part = dict(zip(single, parts[1:]))
 
     pair = across_x(parts[0])

time: 92.4 us -> 91.7 us (level)
  no operation moved by 1% of the time
where the time goes in v8:
time: 91.7 us; the launch traced here: 91.5 us
  starting transfers between devices  42.1 us (46%)
  Pallas kernels  26.3 us (29%)
  waiting for transfers between devices  19.9 us (22%)
  local copies, waits for them, and re-layouts  2.38 us (3%)
    ppermute x8, starting transfers between devices, along_z(): return lax.ppermute(value, 'z', [(z, (z + step) % N_Z) for z in range(N_Z)])  15.8 us
    pallas_call x1, Pallas kernels, shards(): call(invert, one, 1, 2, [VMEM((2, HALF, HALF), f32)])  10.1 us
    pallas_call x1, Pallas kernels, preconditioned(): pl.pallas_call(precond_kernel, grid_spec=pltpu.PrefetchScalarGridSpec(num...  9.84 us
    ppermute x5, starting transfers between devices, across_x(): return lax.ppermute(value, 'x', [(0, 1), (1, 0)])  8.82 us
    ppermute x8, waiting for transfers between devices, along_z(): return lax.ppermute(value, 'z', [(z, (z + step) % N_Z) for z in range(N_Z)])  8.3 us
    ppermute x3, starting transfers between devices, across_cores(): return lax.ppermute(value, 'c', [(0, 1), (1, 0)])  7.88 us
    ppermute x1, starting transfers between devices, to_twin(): return lax.ppermute(value, ('x', 'z'), pairs)  5.34 us
    ppermute x1, waiting for transfers between devices, to_twin(): return lax.ppermute(value, ('x', 'z'), pairs)  5.02 us
  transfers between devices with their start and end apart: 18, of which 10 were waited for; matrix products, arithmetic and copies ran while one was open for 0% of the time, Pallas kernels for 12%

profile of v8, /device:TPU:1, one launch (start us, length us, event | category | flops | bytes accessed | tf_op | source)
XLA Modules:
  0.0 91.5 jit_solution(8182559125133726748)
XLA Ops:
  0.6 0.1 pad_add_fusion.here_ref
  0.7 1.4 %copy-done = bf16[1,256,3072]{2,1,0:T(8,128)(2,1)S(1)} copy-done((bf16[1,256,3072]{2,1,0:T(8,128)(2,1)S(1)}, bf16[1,256,3072]{2,1,0:T(8,128)(2,1)}, u32[]{:S(2)}) %copy-start) | copy-done | bytes 1572888
  2.1 1.0 %shard_map.51 = f32[6,264,128]{2,1,0:T(8,128)S(1)} custom-call(s32[4]{0:T(128)S(1)} %pad_add_fusion.here_ref, bf16[256,3072]{1,0:T(8,128)(2,1)S(1)} %bitcast.14), custom_call_target="tpu_custom_call" | custom-call | tf_op jit(solution)/shard_map/pallas_call | solution.py:334
  3.1 3.3 %collective-permute-start = (f32[6,264,128]{2,1,0:T(8,128)S(1)}, f32[6,264,128]{2,1,0:T(8,128)S(1)}, u32[]{:S(2)}, u32[]{:S(2)}) collective-permute-start(f32[6,264,128]{2,1,0:T(8,128)S(1)} %shard_map.51), channel_id=1, source_target_pairs={{0,1},{1,0},{2,3},{3,2},{4,5},{5,4},{6,7},{7,6},{8,9},{9,8},{10,11... | collective-permute-start | bytes 2433032 | tf_op jit(solution)/shard_map/ppermute | solution.py:56
  6.4 1.0 %shard_map.50.mine_ref = f32[6,264,128]{2,1,0:T(8,128)S(1)} custom-call(s32[4]{0:T(128)S(1)} %pad_add_fusion.here_ref, bf16[256,3072]{1,0:T(8,128)(2,1)S(1)} %bitcast.15), custom_call_target="tpu_custom_call" | custom-call | tf_op jit(solution)/shard_map/pallas_call | solution.py:335
  7.4 1.0 %collective-permute-done.got_ref = f32[6,264,128]{2,1,0:T(8,128)S(1)} collective-permute-done((f32[6,264,128]{2,1,0:T(8,128)S(1)}, f32[6,264,128]{2,1,0:T(8,128)S(1)}, u32[]{:S(2)}, u32[]{:S(2)}) %collective-permute-start) | collective-permute-done | bytes 811040 | tf_op jit(solution)/shard_map/ppermute | solution.py:56
  8.4 0.8 shard_map.52
  9.2 1.1 %collective-permute-start.4 = (f32[2,264,128]{2,1,0:T(8,128)S(1)}, f32[2,264,128]{2,1,0:T(8,128)S(1)}, u32[]{:S(2)}, u32[]{:S(2)}) collective-permute-start(f32[2,264,128]{2,1,0:T(8,128)S(1)} %get-tuple-element.21), channel_id=1, source_target_pairs={{0,16},{16,0},{1,17},{17,1},{2,18},{18,2},{3,19},{19,3},{4,20},{20... | collective-permute-start | bytes 811016 | tf_op jit(solution)/shard_map/ppermute | solution.py:47
  10.3 2.0 %collective-permute-start.1 = (f32[264,128]{1,0:T(8,128)S(1)}, f32[264,128]{1,0:T(8,128)S(1)}, u32[]{:S(2)}, u32[]{:S(2)}) collective-permute-start(f32[264,128]{1,0:T(8,128)S(1)} %get-tuple-element.17), channel_id=1, source_target_pairs={{0,16},{16,0},{1,17},{17,1},{2,18},{18,2},{3,19},{19,3},{4,20},{20... | collective-permute-start | bytes 405512 | tf_op jit(solution)/shard_map/ppermute | solution.py:47
  12.2 1.3 %collective-permute-start.2 = (f32[264,128]{1,0:T(8,128)S(1)}, f32[264,128]{1,0:T(8,128)S(1)}, u32[]{:S(2)}, u32[]{:S(2)}) collective-permute-start(f32[264,128]{1,0:T(8,128)S(1)} %get-tuple-element.18), channel_id=1, source_target_pairs={{0,4},{2,6},{4,8},{6,10},{8,12},{10,14},{12,0},{14,2},{1,5},{3,7},... | collective-permute-start | bytes 405512 | tf_op jit(solution)/shard_map/ppermute | solution.py:43
  13.5 3.0 %collective-permute-start.3 = (f32[264,128]{1,0:T(8,128)S(1)}, f32[264,128]{1,0:T(8,128)S(1)}, u32[]{:S(2)}, u32[]{:S(2)}) collective-permute-start(f32[264,128]{1,0:T(8,128)S(1)} %get-tuple-element.19), channel_id=1, source_target_pairs={{0,12},{2,14},{4,0},{6,2},{8,4},{10,6},{12,8},{14,10},{1,13},{3,15... | collective-permute-start | bytes 405512 | tf_op jit(solution)/shard_map/ppermute | solution.py:43
  16.5 1.9 %collective-permute-done.4 = f32[2,264,128]{2,1,0:T(8,128)S(1)} collective-permute-done((f32[2,264,128]{2,1,0:T(8,128)S(1)}, f32[2,264,128]{2,1,0:T(8,128)S(1)}, u32[]{:S(2)}, u32[]{:S(2)}) %collective-permute-start.4) | collective-permute-done | bytes 270368 | tf_op jit(solution)/shard_map/ppermute | solution.py:47
  18.5 0.1 collective-permute-start.5
  18.6 3.9 %collective-permute-start.6 = (f32[264,128]{1,0:T(8,128)S(1)}, f32[264,128]{1,0:T(8,128)S(1)}, u32[]{:S(2)}, u32[]{:S(2)}) collective-permute-start(f32[264,128]{1,0:T(8,128)S(1)} %get-tuple-element.31), channel_id=1, source_target_pairs={{0,14},{2,0},{4,2},{6,4},{8,6},{10,8},{12,10},{14,12},{1,15},{3,1}... | collective-permute-start | bytes 405512 | tf_op jit(solution)/shard_map/ppermute | solution.py:43
  22.5 0.0 collective-permute-done.1
  22.5 0.0 collective-permute-done.2
  22.5 1.6 %collective-permute-done.3 = f32[264,128]{1,0:T(8,128)S(1)} collective-permute-done((f32[264,128]{1,0:T(8,128)S(1)}, f32[264,128]{1,0:T(8,128)S(1)}, u32[]{:S(2)}, u32[]{:S(2)}) %collective-permute-start.3) | collective-permute-done | bytes 135200 | tf_op jit(solution)/shard_map/ppermute | solution.py:43
  24.2 0.8 collective-permute-done.5
  25.0 1.6 %collective-permute-done.6 = f32[264,128]{1,0:T(8,128)S(1)} collective-permute-done((f32[264,128]{1,0:T(8,128)S(1)}, f32[264,128]{1,0:T(8,128)S(1)}, u32[]{:S(2)}, u32[]{:S(2)}) %collective-permute-start.6) | collective-permute-done | bytes 135200 | tf_op jit(solution)/shard_map/ppermute | solution.py:43
  26.6 0.1 add_add_fusion.a_ref
  26.7 5.3 %collective-permute-start.7 = (f32[264,128]{1,0:T(8,128)S(1)}, f32[264,128]{1,0:T(8,128)S(1)}, u32[]{:S(2)}, u32[]{:S(2)}) collective-permute-start(f32[264,128]{1,0:T(8,128)S(1)} %add_add_fusion.a_ref), channel_id=1, source_target_pairs={{0,24},{2,26},{4,28},{6,30},{8,16},{10,18},{12,20},{14,22},{16,8},... | collective-permute-start | bytes 405512 | tf_op jit(solution)/shard_map/ppermute | solution.py:52
  32.0 5.0 %collective-permute-done.7.b_ref = f32[264,128]{1,0:T(8,128)S(1)} collective-permute-done((f32[264,128]{1,0:T(8,128)S(1)}, f32[264,128]{1,0:T(8,128)S(1)}, u32[]{:S(2)}, u32[]{:S(2)}) %collective-permute-start.7) | collective-permute-done | bytes 135200 | tf_op jit(solution)/shard_map/ppermute | solution.py:52
  37.0 10.1 %shard_map.53.refs_0_ = f32[264,128]{1,0:T(8,128)S(1)} custom-call(s32[4]{0:T(128)S(1)} %pad_add_fusion.here_ref, f32[264,128]{1,0:T(8,128)S(1)} %add_add_fusion.a_ref, f32[264,128]{1,0:T(8,128)S(1)} %collective-permute-done.7.b_ref), custom_call_target="tpu_custom_call" | custom-call | tf_op jit(solution)/shard_map/pallas_call | solution.py:347
  47.1 0.1 collective-permute-start.9
  47.2 2.7 %collective-permute-start.8 = (f32[264,128]{1,0:T(8,128)S(1)}, f32[264,128]{1,0:T(8,128)S(1)}, u32[]{:S(2)}, u32[]{:S(2)}) collective-permute-start(f32[264,128]{1,0:T(8,128)S(1)} %shard_map.53.refs_0_), channel_id=1, source_target_pairs={{0,14},{2,0},{4,2},{6,4},{8,6},{10,8},{12,10},{14,12},{1,15},{3,1}... | collective-permute-start | bytes 405512 | tf_op jit(solution)/shard_map/ppermute | solution.py:43
  49.9 2.8 %collective-permute-start.13 = (f32[264,128]{1,0:T(8,128)S(1)}, f32[264,128]{1,0:T(8,128)S(1)}, u32[]{:S(2)}, u32[]{:S(2)}) collective-permute-start(f32[264,128]{1,0:T(8,128)S(1)} %shard_map.53.refs_0_), channel_id=1, source_target_pairs={{0,16},{16,0},{1,17},{17,1},{2,18},{18,2},{3,19},{19,3},{4,20},{20... | collective-permute-start | bytes 405512 | tf_op jit(solution)/shard_map/ppermute | solution.py:47
  52.7 4.8 %collective-permute-start.11 = (f32[264,128]{1,0:T(8,128)S(1)}, f32[264,128]{1,0:T(8,128)S(1)}, u32[]{:S(2)}, u32[]{:S(2)}) collective-permute-start(f32[264,128]{1,0:T(8,128)S(1)} %shard_map.53.refs_0_), channel_id=1, source_target_pairs={{0,4},{2,6},{4,8},{6,10},{8,12},{10,14},{12,0},{14,2},{1,5},{3,7},... | collective-permute-start | bytes 405512 | tf_op jit(solution)/shard_map/ppermute | solution.py:43
  57.5 0.0 collective-permute-start.10
  57.5 0.0 collective-permute-done.9.refs_2_
  57.5 0.2 collective-permute-start.12
  57.7 0.0 collective-permute-done.8.refs_1_
  57.7 2.7 %collective-permute-start.14 = (f32[264,128]{1,0:T(8,128)S(1)}, f32[264,128]{1,0:T(8,128)S(1)}, u32[]{:S(2)}, u32[]{:S(2)}) collective-permute-start(f32[264,128]{1,0:T(8,128)S(1)} %collective-permute-done.8.refs_1_), channel_id=1, source_target_pairs={{0,16},{16,0},{1,17},{17,1},{2,18},{18,2},{3,19},{19,3},{4,20},{20... | collective-permute-start | bytes 405512 | tf_op jit(solution)/shard_map/ppermute | solution.py:47
  60.5 0.0 collective-permute-done.13.refs_6_
  60.5 0.6 collective-permute-done.11.refs_4_
  61.1 3.6 %collective-permute-done.10.refs_3_ = f32[264,128]{1,0:T(8,128)S(1)} collective-permute-done((f32[264,128]{1,0:T(8,128)S(1)}, f32[264,128]{1,0:T(8,128)S(1)}, u32[]{:S(2)}, u32[]{:S(2)}) %collective-permute-start.10) | collective-permute-done | bytes 135200 | tf_op jit(solution)/shard_map/ppermute | solution.py:43
  64.7 0.0 collective-permute-done.12.refs_5_
  64.7 0.0 collective-permute-done.14.refs_7_
  64.7 2.2 %shard_map.54 = (f32[6,256,256]{2,1,0:T(8,128)}, f32[6,8,256]{2,1,0:T(8,128)S(1)}, f32[6,8,256]{2,1,0:T(8,128)S(1)}) custom-call(s32[4]{0:T(128)S(1)} %pad_add_fusion.here_ref, f32[264,128]{1,0:T(8,128)S(1)} %shard_map.53.refs_0_, f32[264,128]{1,0:T(8,128)S(1)} %collective-permute-done.8.refs_1_, f32[264,128]{1,0:T(8,128)S(1)} %collective-permute-done.9.refs_2_, ...), custom_call_target="tpu_custom_call" | custom-call | tf_op jit(solution)/shard_map/pallas_call | solution.py:293
  66.9 0.0 copy-start.1
  66.9 0.0 copy-start.2
  67.0 4.2 %collective-permute-start.15 = (f32[6,8,256]{2,1,0:T(8,128)S(1)}, f32[6,8,256]{2,1,0:T(8,128)S(1)}, u32[]{:S(2)}, u32[]{:S(2)}) collective-permute-start(f32[6,8,256]{2,1,0:T(8,128)S(1)} %get-tuple-element.25), channel_id=1, source_target_pairs={{0,1},{1,0},{2,3},{3,2},{4,5},{5,4},{6,7},{7,6},{8,9},{9,8},{10,11... | collective-permute-start | bytes 147464 | tf_op jit(solution)/shard_map/ppermute | solution.py:56
  71.2 0.9 collective-permute-done.15
  72.0 1.0 %broadcast_in_dim.4 = f32[8,12,8,256]{3,2,1,0:T(8,128)} broadcast(f32[12,8,256]{2,1,0:T(8,128)S(1)} %pad_maximum_fusion), dimensions={1,2,3} | broadcast | bytes 884736 | tf_op jit(solution)/shard_map/broadcast_in_dim | solution.py:356
  73.0 0.4 collective-permute-start.16
  73.4 4.2 %all-to-all-start = ((f32[8,12,8,256]{3,2,1,0:T(8,128)}), f32[8,12,8,256]{3,2,1,0:T(8,128)S(1)}, u32[]{:S(2)}, u32[]{:S(2)}) async-start(f32[8,12,8,256]{3,2,1,0:T(8,128)} %broadcast_in_dim.4), calls=%async_computation | async-start | bytes 1572864 | tf_op jit(solution)/shard_map/all_to_all | solution.py:359
  77.6 9.8 %shard_map.55 = (f32[3072,128]{1,0:T(8,128)}, s32[24]{0:T(128)S(1)}) custom-call(s32[4]{0:T(128)S(1)} %pad_add_fusion.here_ref, s32[8,12]{1,0:T(8,128)S(1)} %copy-done.2, f32[6,256,256]{2,1,0:T(8,128)} %get-tuple-element.26.own_ref, f32[6,256,256]{2,1,0:T(8,128)} %collective-permute-done.16.other_ref, f32[3072,128]{1,0:T(8,128)S(1)} %copy-done.1), custom_call_target="tpu_custom_call" | custom-call | flops 1207959552 | bytes 6291456 | tf_op jit(solution)/shard_map/pallas_call | solution.py:311
  87.4 2.7 %all-to-all-done.rows_ref = f32[8,12,8,256]{3,2,1,0:T(8,128)S(1)} async-done(((f32[8,12,8,256]{3,2,1,0:T(8,128)}), f32[8,12,8,256]{3,2,1,0:T(8,128)S(1)}, u32[]{:S(2)}, u32[]{:S(2)}) %all-to-all-start) | async-done | bytes 786464 | tf_op jit(solution)/shard_map/all_to_all | solution.py:359
  90.2 1.4 %shard_map.56 = f32[24,8,256]{2,1,0:T(8,128)} custom-call(s32[24]{0:T(128)S(1)} %get-tuple-element.28.table_ref, f32[8,12,8,256]{3,2,1,0:T(8,128)S(1)} %all-to-all-done.rows_ref), custom_call_target="tpu_custom_call" | custom-call | tf_op jit(solution)/shard_map/pallas_call | solution.py:361
  (6 shorter events, 0.1 us)
Async XLA Ops:
  0.7 1.4 %copy-start = (bf16[1,256,3072]{2,1,0:T(8,128)(2,1)S(1)}, bf16[1,256,3072]{2,1,0:T(8,128)(2,1)}, u32[]{:S(2)}) copy-start(bf16[1,256,3072]{2,1,0:T(8,128)(2,1)} %param.3) | copy-start | bytes 4718596
  3.1 5.3 %collective-permute-start = (f32[6,264,128]{2,1,0:T(8,128)S(1)}, f32[6,264,128]{2,1,0:T(8,128)S(1)}, u32[]{:S(2)}, u32[]{:S(2)}) collective-permute-start(f32[6,264,128]{2,1,0:T(8,128)S(1)} %shard_map.51), channel_id=1, source_target_pairs={{0,1},{1,0},{2,3},{3,2},{4,5},{5,4},{6,7},{7,6},{8,9},{9,8},{10,11... | collective-permute-start | bytes 2433032 | tf_op jit(solution)/shard_map/ppermute | solution.py:56
  9.2 9.3 %collective-permute-start.4 = (f32[2,264,128]{2,1,0:T(8,128)S(1)}, f32[2,264,128]{2,1,0:T(8,128)S(1)}, u32[]{:S(2)}, u32[]{:S(2)}) collective-permute-start(f32[2,264,128]{2,1,0:T(8,128)S(1)} %get-tuple-element.21), channel_id=1, source_target_pairs={{0,16},{16,0},{1,17},{17,1},{2,18},{18,2},{3,19},{19,3},{4,20},{20... | collective-permute-start | bytes 811016 | tf_op jit(solution)/shard_map/ppermute | solution.py:47
  10.3 12.2 %collective-permute-start.1 = (f32[264,128]{1,0:T(8,128)S(1)}, f32[264,128]{1,0:T(8,128)S(1)}, u32[]{:S(2)}, u32[]{:S(2)}) collective-permute-start(f32[264,128]{1,0:T(8,128)S(1)} %get-tuple-element.17), channel_id=1, source_target_pairs={{0,16},{16,0},{1,17},{17,1},{2,18},{18,2},{3,19},{19,3},{4,20},{20... | collective-permute-start | bytes 405512 | tf_op jit(solution)/shard_map/ppermute | solution.py:47
  12.2 10.3 %collective-permute-start.2 = (f32[264,128]{1,0:T(8,128)S(1)}, f32[264,128]{1,0:T(8,128)S(1)}, u32[]{:S(2)}, u32[]{:S(2)}) collective-permute-start(f32[264,128]{1,0:T(8,128)S(1)} %get-tuple-element.18), channel_id=1, source_target_pairs={{0,4},{2,6},{4,8},{6,10},{8,12},{10,14},{12,0},{14,2},{1,5},{3,7},... | collective-permute-start | bytes 405512 | tf_op jit(solution)/shard_map/ppermute | solution.py:43
  13.5 10.7 %collective-permute-start.3 = (f32[264,128]{1,0:T(8,128)S(1)}, f32[264,128]{1,0:T(8,128)S(1)}, u32[]{:S(2)}, u32[]{:S(2)}) collective-permute-start(f32[264,128]{1,0:T(8,128)S(1)} %get-tuple-element.19), channel_id=1, source_target_pairs={{0,12},{2,14},{4,0},{6,2},{8,4},{10,6},{12,8},{14,10},{1,13},{3,15... | collective-permute-start | bytes 405512 | tf_op jit(solution)/shard_map/ppermute | solution.py:43
  18.5 6.5 %collective-permute-start.5 = (f32[264,128]{1,0:T(8,128)S(1)}, f32[264,128]{1,0:T(8,128)S(1)}, u32[]{:S(2)}, u32[]{:S(2)}) collective-permute-start(f32[264,128]{1,0:T(8,128)S(1)} %get-tuple-element.30), channel_id=1, source_target_pairs={{0,2},{2,4},{4,6},{6,8},{8,10},{10,12},{12,14},{14,0},{1,3},{3,5},... | collective-permute-start | bytes 405512 | tf_op jit(solution)/shard_map/ppermute | solution.py:43
  18.6 8.0 %collective-permute-start.6 = (f32[264,128]{1,0:T(8,128)S(1)}, f32[264,128]{1,0:T(8,128)S(1)}, u32[]{:S(2)}, u32[]{:S(2)}) collective-permute-start(f32[264,128]{1,0:T(8,128)S(1)} %get-tuple-element.31), channel_id=1, source_target_pairs={{0,14},{2,0},{4,2},{6,4},{8,6},{10,8},{12,10},{14,12},{1,15},{3,1}... | collective-permute-start | bytes 405512 | tf_op jit(solution)/shard_map/ppermute | solution.py:43
  26.7 10.4 %collective-permute-start.7 = (f32[264,128]{1,0:T(8,128)S(1)}, f32[264,128]{1,0:T(8,128)S(1)}, u32[]{:S(2)}, u32[]{:S(2)}) collective-permute-start(f32[264,128]{1,0:T(8,128)S(1)} %add_add_fusion.a_ref), channel_id=1, source_target_pairs={{0,24},{2,26},{4,28},{6,30},{8,16},{10,18},{12,20},{14,22},{16,8},... | collective-permute-start | bytes 405512 | tf_op jit(solution)/shard_map/ppermute | solution.py:52
  47.1 10.3 %collective-permute-start.9 = (f32[264,128]{1,0:T(8,128)S(1)}, f32[264,128]{1,0:T(8,128)S(1)}, u32[]{:S(2)}, u32[]{:S(2)}) collective-permute-start(f32[264,128]{1,0:T(8,128)S(1)} %shard_map.53.refs_0_), channel_id=1, source_target_pairs={{0,2},{2,4},{4,6},{6,8},{8,10},{10,12},{12,14},{14,0},{1,3},{3,5},... | collective-permute-start | bytes 405512 | tf_op jit(solution)/shard_map/ppermute | solution.py:43
  47.2 10.5 %collective-permute-start.8 = (f32[264,128]{1,0:T(8,128)S(1)}, f32[264,128]{1,0:T(8,128)S(1)}, u32[]{:S(2)}, u32[]{:S(2)}) collective-permute-start(f32[264,128]{1,0:T(8,128)S(1)} %shard_map.53.refs_0_), channel_id=1, source_target_pairs={{0,14},{2,0},{4,2},{6,4},{8,6},{10,8},{12,10},{14,12},{1,15},{3,1}... | collective-permute-start | bytes 405512 | tf_op jit(solution)/shard_map/ppermute | solution.py:43
  49.9 10.6 %collective-permute-start.13 = (f32[264,128]{1,0:T(8,128)S(1)}, f32[264,128]{1,0:T(8,128)S(1)}, u32[]{:S(2)}, u32[]{:S(2)}) collective-permute-start(f32[264,128]{1,0:T(8,128)S(1)} %shard_map.53.refs_0_), channel_id=1, source_target_pairs={{0,16},{16,0},{1,17},{17,1},{2,18},{18,2},{3,19},{19,3},{4,20},{20... | collective-permute-start | bytes 405512 | tf_op jit(solution)/shard_map/ppermute | solution.py:47
  52.7 8.4 %collective-permute-start.11 = (f32[264,128]{1,0:T(8,128)S(1)}, f32[264,128]{1,0:T(8,128)S(1)}, u32[]{:S(2)}, u32[]{:S(2)}) collective-permute-start(f32[264,128]{1,0:T(8,128)S(1)} %shard_map.53.refs_0_), channel_id=1, source_target_pairs={{0,4},{2,6},{4,8},{6,10},{8,12},{10,14},{12,0},{14,2},{1,5},{3,7},... | collective-permute-start | bytes 405512 | tf_op jit(solution)/shard_map/ppermute | solution.py:43
  57.5 7.2 %collective-permute-start.10 = (f32[264,128]{1,0:T(8,128)S(1)}, f32[264,128]{1,0:T(8,128)S(1)}, u32[]{:S(2)}, u32[]{:S(2)}) collective-permute-start(f32[264,128]{1,0:T(8,128)S(1)} %shard_map.53.refs_0_), channel_id=1, source_target_pairs={{0,12},{2,14},{4,0},{6,2},{8,4},{10,6},{12,8},{14,10},{1,13},{3,15... | collective-permute-start | bytes 405512 | tf_op jit(solution)/shard_map/ppermute | solution.py:43
  57.5 7.2 %collective-permute-start.12 = (f32[264,128]{1,0:T(8,128)S(1)}, f32[264,128]{1,0:T(8,128)S(1)}, u32[]{:S(2)}, u32[]{:S(2)}) collective-permute-start(f32[264,128]{1,0:T(8,128)S(1)} %collective-permute-done.9.refs_2_), channel_id=1, source_target_pairs={{0,16},{16,0},{1,17},{17,1},{2,18},{18,2},{3,19},{19,3},{4,20},{20... | collective-permute-start | bytes 405512 | tf_op jit(solution)/shard_map/ppermute | solution.py:47
  57.7 7.0 %collective-permute-start.14 = (f32[264,128]{1,0:T(8,128)S(1)}, f32[264,128]{1,0:T(8,128)S(1)}, u32[]{:S(2)}, u32[]{:S(2)}) collective-permute-start(f32[264,128]{1,0:T(8,128)S(1)} %collective-permute-done.8.refs_1_), channel_id=1, source_target_pairs={{0,16},{16,0},{1,17},{17,1},{2,18},{18,2},{3,19},{19,3},{4,20},{20... | collective-permute-start | bytes 405512 | tf_op jit(solution)/shard_map/ppermute | solution.py:47
  66.9 10.6 %copy-start.1 = (f32[3072,128]{1,0:T(8,128)S(1)}, f32[3072,128]{1,0:T(8,128)}, u32[]{:S(2)}) copy-start(f32[3072,128]{1,0:T(8,128)} %grad_ref.1) | copy-start | bytes 4718596
  66.9 10.6 %copy-start.2 = (s32[8,12]{1,0:T(8,128)S(1)}, s32[8,12]{1,0:T(8,128)}, u32[]{:S(2)}) copy-start(s32[8,12]{1,0:T(8,128)} %owner_ref.1) | copy-start | bytes 1156
  67.0 5.1 %collective-permute-start.15 = (f32[6,8,256]{2,1,0:T(8,128)S(1)}, f32[6,8,256]{2,1,0:T(8,128)S(1)}, u32[]{:S(2)}, u32[]{:S(2)}) collective-permute-start(f32[6,8,256]{2,1,0:T(8,128)S(1)} %get-tuple-element.25), channel_id=1, source_target_pairs={{0,1},{1,0},{2,3},{3,2},{4,5},{5,4},{6,7},{7,6},{8,9},{9,8},{10,11... | collective-permute-start | bytes 147464 | tf_op jit(solution)/shard_map/ppermute | solution.py:56
  73.0 4.5 %collective-permute-start.16 = (f32[6,256,256]{2,1,0:T(8,128)}, f32[6,256,256]{2,1,0:T(8,128)}, u32[]{:S(2)}, u32[]{:S(2)}) collective-permute-start(f32[6,256,256]{2,1,0:T(8,128)} %get-tuple-element.26.own_ref), channel_id=1, source_target_pairs={{0,1},{1,0},{2,3},{3,2},{4,5},{5,4},{6,7},{7,6},{8,9},{9,8},{10,11... | collective-permute-start | bytes 4718600 | tf_op jit(solution)/shard_map/ppermute | solution.py:56
  73.4 16.8 %all-to-all-start = ((f32[8,12,8,256]{3,2,1,0:T(8,128)}), f32[8,12,8,256]{3,2,1,0:T(8,128)S(1)}, u32[]{:S(2)}, u32[]{:S(2)}) async-start(f32[8,12,8,256]{3,2,1,0:T(8,128)} %broadcast_in_dim.4), calls=%async_computation | async-start | bytes 1572864 | tf_op jit(solution)/shard_map/all_to_all | solution.py:359

commit v9 on v8

--- a/solution.py
+++ b/solution.py
@@ -137,7 +137,7 @@
     )
 
 
-def half_inverse(value, rows_ref):
+def half_factors(value, rows_ref):
     count = HALF // SUB
     tiles = [value[SUB * v : SUB * v + SUB] for v in range(count)]
     lane = lax.broadcasted_iota(jnp.int32, (SUB, HALF), 1)
@@ -176,7 +176,7 @@
                 [spread(tiles[v][:, first + j : first + j + 1]) * new[j] for j in range(SUB)]
             )
             tiles[v] = jnp.where(inside, 0.0, tiles[v]) + update
-    return dot(jnp.concatenate(lower, axis=0), jnp.concatenate(scaled, axis=0), ((0,), (0,)))
+    return jnp.concatenate(lower, axis=0), jnp.concatenate(scaled, axis=0)
 
 
 def invert_kernel(here_ref, a_ref, b_ref, out_ref, rows_ref, *, all_tokens):
@@ -190,11 +190,14 @@
         )
         damping = damping_ratio * trace / BLK
         shift = jnp.where(same, damping, 0.0)
-        first = half_inverse(upper + shift, rows_ref.at[0])
+        turned = ((0,), (0,))
+        first = dot(*half_factors(upper + shift, rows_ref.at[0]), turned)
         w = dot(cross, first)
-        second = half_inverse(lower + shift - dot(w, cross, ((1,), (1,))), rows_ref.at[1])
-        x = dot(second, w)
-        store_packed(out_ref, first + dot(w, x, ((0,), (0,))), -x, second)
+        below, scaled = half_factors(lower + shift - dot(w, cross, ((1,), (1,))), rows_ref.at[1])
+        left, right = dot(below, w), dot(scaled, w)
+        store_packed(
+            out_ref, first + dot(left, right, turned), -dot(below, right, turned), dot(below, scaled, turned)
+        )
 
 
 def unpack_kernel(here_ref, *refs):

time: 91.7 us -> 91.5 us (level)
  no operation moved by 1% of the time
where the time goes in v9:
time: 91.5 us; the launch traced here: 91.3 us
  starting transfers between devices  42.1 us (46%)
  Pallas kernels  26.1 us (29%)
  waiting for transfers between devices  19.9 us (22%)
  local copies, waits for them, and re-layouts  2.38 us (3%)
    ppermute x8, starting transfers between devices, along_z(): return lax.ppermute(value, 'z', [(z, (z + step) % N_Z) for z in range(N_Z)])  15.8 us
    pallas_call x1, Pallas kernels, shards(): call(invert, one, 1, 2, [VMEM((2, HALF, HALF), f32)])  10.1 us
    pallas_call x1, Pallas kernels, preconditioned(): pl.pallas_call(precond_kernel, grid_spec=pltpu.PrefetchScalarGridSpec(num...  9.84 us
    ppermute x5, starting transfers between devices, across_x(): return lax.ppermute(value, 'x', [(0, 1), (1, 0)])  8.82 us
    ppermute x8, waiting for transfers between devices, along_z(): return lax.ppermute(value, 'z', [(z, (z + step) % N_Z) for z in range(N_Z)])  8.3 us
    ppermute x3, starting transfers between devices, across_cores(): return lax.ppermute(value, 'c', [(0, 1), (1, 0)])  7.88 us
    ppermute x1, starting transfers between devices, to_twin(): return lax.ppermute(value, ('x', 'z'), pairs)  5.34 us
    ppermute x1, waiting for transfers between devices, to_twin(): return lax.ppermute(value, ('x', 'z'), pairs)  5.02 us
  transfers between devices with their start and end apart: 18, of which 10 were waited for; matrix products, arithmetic and copies ran while one was open for 0% of the time, Pallas kernels for 12%

profile of v9, /device:TPU:1, one launch (start us, length us, event | category | flops | bytes accessed | tf_op | source)
XLA Modules:
  0.0 91.3 jit_solution(4001772304742002450)
XLA Ops:
  0.6 0.1 pad_add_fusion.here_ref
  0.7 1.4 %copy-done = bf16[1,256,3072]{2,1,0:T(8,128)(2,1)S(1)} copy-done((bf16[1,256,3072]{2,1,0:T(8,128)(2,1)S(1)}, bf16[1,256,3072]{2,1,0:T(8,128)(2,1)}, u32[]{:S(2)}) %copy-start) | copy-done | bytes 1572888
  2.1 1.0 %shard_map.51 = f32[6,264,128]{2,1,0:T(8,128)S(1)} custom-call(s32[4]{0:T(128)S(1)} %pad_add_fusion.here_ref, bf16[256,3072]{1,0:T(8,128)(2,1)S(1)} %bitcast.14), custom_call_target="tpu_custom_call" | custom-call | tf_op jit(solution)/shard_map/pallas_call | solution.py:337
  3.1 3.3 %collective-permute-start = (f32[6,264,128]{2,1,0:T(8,128)S(1)}, f32[6,264,128]{2,1,0:T(8,128)S(1)}, u32[]{:S(2)}, u32[]{:S(2)}) collective-permute-start(f32[6,264,128]{2,1,0:T(8,128)S(1)} %shard_map.51), channel_id=1, source_target_pairs={{0,1},{1,0},{2,3},{3,2},{4,5},{5,4},{6,7},{7,6},{8,9},{9,8},{10,11... | collective-permute-start | bytes 2433032 | tf_op jit(solution)/shard_map/ppermute | solution.py:56
  6.4 1.0 %shard_map.50.mine_ref = f32[6,264,128]{2,1,0:T(8,128)S(1)} custom-call(s32[4]{0:T(128)S(1)} %pad_add_fusion.here_ref, bf16[256,3072]{1,0:T(8,128)(2,1)S(1)} %bitcast.15), custom_call_target="tpu_custom_call" | custom-call | tf_op jit(solution)/shard_map/pallas_call | solution.py:338
  7.4 1.0 %collective-permute-done.got_ref = f32[6,264,128]{2,1,0:T(8,128)S(1)} collective-permute-done((f32[6,264,128]{2,1,0:T(8,128)S(1)}, f32[6,264,128]{2,1,0:T(8,128)S(1)}, u32[]{:S(2)}, u32[]{:S(2)}) %collective-permute-start) | collective-permute-done | bytes 811040 | tf_op jit(solution)/shard_map/ppermute | solution.py:56
  8.4 0.8 shard_map.52
  9.2 1.1 %collective-permute-start.4 = (f32[2,264,128]{2,1,0:T(8,128)S(1)}, f32[2,264,128]{2,1,0:T(8,128)S(1)}, u32[]{:S(2)}, u32[]{:S(2)}) collective-permute-start(f32[2,264,128]{2,1,0:T(8,128)S(1)} %get-tuple-element.21), channel_id=1, source_target_pairs={{0,16},{16,0},{1,17},{17,1},{2,18},{18,2},{3,19},{19,3},{4,20},{20... | collective-permute-start | bytes 811016 | tf_op jit(solution)/shard_map/ppermute | solution.py:47
  10.3 2.0 %collective-permute-start.1 = (f32[264,128]{1,0:T(8,128)S(1)}, f32[264,128]{1,0:T(8,128)S(1)}, u32[]{:S(2)}, u32[]{:S(2)}) collective-permute-start(f32[264,128]{1,0:T(8,128)S(1)} %get-tuple-element.17), channel_id=1, source_target_pairs={{0,16},{16,0},{1,17},{17,1},{2,18},{18,2},{3,19},{19,3},{4,20},{20... | collective-permute-start | bytes 405512 | tf_op jit(solution)/shard_map/ppermute | solution.py:47
  12.2 1.3 %collective-permute-start.2 = (f32[264,128]{1,0:T(8,128)S(1)}, f32[264,128]{1,0:T(8,128)S(1)}, u32[]{:S(2)}, u32[]{:S(2)}) collective-permute-start(f32[264,128]{1,0:T(8,128)S(1)} %get-tuple-element.18), channel_id=1, source_target_pairs={{0,4},{2,6},{4,8},{6,10},{8,12},{10,14},{12,0},{14,2},{1,5},{3,7},... | collective-permute-start | bytes 405512 | tf_op jit(solution)/shard_map/ppermute | solution.py:43
  13.5 3.0 %collective-permute-start.3 = (f32[264,128]{1,0:T(8,128)S(1)}, f32[264,128]{1,0:T(8,128)S(1)}, u32[]{:S(2)}, u32[]{:S(2)}) collective-permute-start(f32[264,128]{1,0:T(8,128)S(1)} %get-tuple-element.19), channel_id=1, source_target_pairs={{0,12},{2,14},{4,0},{6,2},{8,4},{10,6},{12,8},{14,10},{1,13},{3,15... | collective-permute-start | bytes 405512 | tf_op jit(solution)/shard_map/ppermute | solution.py:43
  16.5 1.9 %collective-permute-done.4 = f32[2,264,128]{2,1,0:T(8,128)S(1)} collective-permute-done((f32[2,264,128]{2,1,0:T(8,128)S(1)}, f32[2,264,128]{2,1,0:T(8,128)S(1)}, u32[]{:S(2)}, u32[]{:S(2)}) %collective-permute-start.4) | collective-permute-done | bytes 270368 | tf_op jit(solution)/shard_map/ppermute | solution.py:47
  18.5 0.1 collective-permute-start.5
  18.6 3.9 %collective-permute-start.6 = (f32[264,128]{1,0:T(8,128)S(1)}, f32[264,128]{1,0:T(8,128)S(1)}, u32[]{:S(2)}, u32[]{:S(2)}) collective-permute-start(f32[264,128]{1,0:T(8,128)S(1)} %get-tuple-element.31), channel_id=1, source_target_pairs={{0,14},{2,0},{4,2},{6,4},{8,6},{10,8},{12,10},{14,12},{1,15},{3,1}... | collective-permute-start | bytes 405512 | tf_op jit(solution)/shard_map/ppermute | solution.py:43
  22.5 0.0 collective-permute-done.1
  22.5 0.0 collective-permute-done.2
  22.5 1.6 %collective-permute-done.3 = f32[264,128]{1,0:T(8,128)S(1)} collective-permute-done((f32[264,128]{1,0:T(8,128)S(1)}, f32[264,128]{1,0:T(8,128)S(1)}, u32[]{:S(2)}, u32[]{:S(2)}) %collective-permute-start.3) | collective-permute-done | bytes 135200 | tf_op jit(solution)/shard_map/ppermute | solution.py:43
  24.2 0.8 collective-permute-done.5
  25.0 1.6 %collective-permute-done.6 = f32[264,128]{1,0:T(8,128)S(1)} collective-permute-done((f32[264,128]{1,0:T(8,128)S(1)}, f32[264,128]{1,0:T(8,128)S(1)}, u32[]{:S(2)}, u32[]{:S(2)}) %collective-permute-start.6) | collective-permute-done | bytes 135200 | tf_op jit(solution)/shard_map/ppermute | solution.py:43
  26.6 0.1 add_add_fusion.a_ref
  26.7 5.3 %collective-permute-start.7 = (f32[264,128]{1,0:T(8,128)S(1)}, f32[264,128]{1,0:T(8,128)S(1)}, u32[]{:S(2)}, u32[]{:S(2)}) collective-permute-start(f32[264,128]{1,0:T(8,128)S(1)} %add_add_fusion.a_ref), channel_id=1, source_target_pairs={{0,24},{2,26},{4,28},{6,30},{8,16},{10,18},{12,20},{14,22},{16,8},... | collective-permute-start | bytes 405512 | tf_op jit(solution)/shard_map/ppermute | solution.py:52
  32.0 5.0 %collective-permute-done.7.b_ref = f32[264,128]{1,0:T(8,128)S(1)} collective-permute-done((f32[264,128]{1,0:T(8,128)S(1)}, f32[264,128]{1,0:T(8,128)S(1)}, u32[]{:S(2)}, u32[]{:S(2)}) %collective-permute-start.7) | collective-permute-done | bytes 135200 | tf_op jit(solution)/shard_map/ppermute | solution.py:52
  37.0 10.1 %shard_map.53.refs_0_ = f32[264,128]{1,0:T(8,128)S(1)} custom-call(s32[4]{0:T(128)S(1)} %pad_add_fusion.here_ref, f32[264,128]{1,0:T(8,128)S(1)} %add_add_fusion.a_ref, f32[264,128]{1,0:T(8,128)S(1)} %collective-permute-done.7.b_ref), custom_call_target="tpu_custom_call" | custom-call | tf_op jit(solution)/shard_map/pallas_call | solution.py:350
  47.1 0.1 collective-permute-start.9
  47.2 2.7 %collective-permute-start.8 = (f32[264,128]{1,0:T(8,128)S(1)}, f32[264,128]{1,0:T(8,128)S(1)}, u32[]{:S(2)}, u32[]{:S(2)}) collective-permute-start(f32[264,128]{1,0:T(8,128)S(1)} %shard_map.53.refs_0_), channel_id=1, source_target_pairs={{0,14},{2,0},{4,2},{6,4},{8,6},{10,8},{12,10},{14,12},{1,15},{3,1}... | collective-permute-start | bytes 405512 | tf_op jit(solution)/shard_map/ppermute | solution.py:43
  49.9 2.8 %collective-permute-start.13 = (f32[264,128]{1,0:T(8,128)S(1)}, f32[264,128]{1,0:T(8,128)S(1)}, u32[]{:S(2)}, u32[]{:S(2)}) collective-permute-start(f32[264,128]{1,0:T(8,128)S(1)} %shard_map.53.refs_0_), channel_id=1, source_target_pairs={{0,16},{16,0},{1,17},{17,1},{2,18},{18,2},{3,19},{19,3},{4,20},{20... | collective-permute-start | bytes 405512 | tf_op jit(solution)/shard_map/ppermute | solution.py:47
  52.7 4.8 %collective-permute-start.11 = (f32[264,128]{1,0:T(8,128)S(1)}, f32[264,128]{1,0:T(8,128)S(1)}, u32[]{:S(2)}, u32[]{:S(2)}) collective-permute-start(f32[264,128]{1,0:T(8,128)S(1)} %shard_map.53.refs_0_), channel_id=1, source_target_pairs={{0,4},{2,6},{4,8},{6,10},{8,12},{10,14},{12,0},{14,2},{1,5},{3,7},... | collective-permute-start | bytes 405512 | tf_op jit(solution)/shard_map/ppermute | solution.py:43
  57.5 0.0 collective-permute-start.10
  57.5 0.0 collective-permute-done.9.refs_2_
  57.5 0.2 collective-permute-start.12
  57.7 0.0 collective-permute-done.8.refs_1_
  57.7 2.7 %collective-permute-start.14 = (f32[264,128]{1,0:T(8,128)S(1)}, f32[264,128]{1,0:T(8,128)S(1)}, u32[]{:S(2)}, u32[]{:S(2)}) collective-permute-start(f32[264,128]{1,0:T(8,128)S(1)} %collective-permute-done.8.refs_1_), channel_id=1, source_target_pairs={{0,16},{16,0},{1,17},{17,1},{2,18},{18,2},{3,19},{19,3},{4,20},{20... | collective-permute-start | bytes 405512 | tf_op jit(solution)/shard_map/ppermute | solution.py:47
  60.5 0.6 collective-permute-done.11.refs_4_
  61.1 3.6 %collective-permute-done.10.refs_3_ = f32[264,128]{1,0:T(8,128)S(1)} collective-permute-done((f32[264,128]{1,0:T(8,128)S(1)}, f32[264,128]{1,0:T(8,128)S(1)}, u32[]{:S(2)}, u32[]{:S(2)}) %collective-permute-start.10) | collective-permute-done | bytes 135200 | tf_op jit(solution)/shard_map/ppermute | solution.py:43
  64.7 0.0 collective-permute-done.12.refs_5_
  64.7 0.0 collective-permute-done.14.refs_7_
  64.7 2.0 %shard_map.54 = (f32[6,256,256]{2,1,0:T(8,128)}, f32[6,8,256]{2,1,0:T(8,128)S(1)}, f32[6,8,256]{2,1,0:T(8,128)S(1)}) custom-call(s32[4]{0:T(128)S(1)} %pad_add_fusion.here_ref, f32[264,128]{1,0:T(8,128)S(1)} %shard_map.53.refs_0_, f32[264,128]{1,0:T(8,128)S(1)} %collective-permute-done.8.refs_1_, f32[264,128]{1,0:T(8,128)S(1)} %collective-permute-done.9.refs_2_, ...), custom_call_target="tpu_custom_call" | custom-call | tf_op jit(solution)/shard_map/pallas_call | solution.py:296
  66.7 0.0 copy-start.1
  66.7 0.0 copy-start.2
  66.7 4.2 %collective-permute-start.15 = (f32[6,8,256]{2,1,0:T(8,128)S(1)}, f32[6,8,256]{2,1,0:T(8,128)S(1)}, u32[]{:S(2)}, u32[]{:S(2)}) collective-permute-start(f32[6,8,256]{2,1,0:T(8,128)S(1)} %get-tuple-element.25), channel_id=1, source_target_pairs={{0,1},{1,0},{2,3},{3,2},{4,5},{5,4},{6,7},{7,6},{8,9},{9,8},{10,11... | collective-permute-start | bytes 147464 | tf_op jit(solution)/shard_map/ppermute | solution.py:56
  70.9 0.9 collective-permute-done.15
  71.8 1.0 %broadcast_in_dim.4 = f32[8,12,8,256]{3,2,1,0:T(8,128)} broadcast(f32[12,8,256]{2,1,0:T(8,128)S(1)} %pad_maximum_fusion), dimensions={1,2,3} | broadcast | bytes 884736 | tf_op jit(solution)/shard_map/broadcast_in_dim | solution.py:359
  72.8 0.4 collective-permute-start.16
  73.1 4.2 %all-to-all-start = ((f32[8,12,8,256]{3,2,1,0:T(8,128)}), f32[8,12,8,256]{3,2,1,0:T(8,128)S(1)}, u32[]{:S(2)}, u32[]{:S(2)}) async-start(f32[8,12,8,256]{3,2,1,0:T(8,128)} %broadcast_in_dim.4), calls=%async_computation | async-start | bytes 1572864 | tf_op jit(solution)/shard_map/all_to_all | solution.py:362
  77.3 0.0 collective-permute-done.16.other_ref
  77.3 9.8 %shard_map.55 = (f32[3072,128]{1,0:T(8,128)}, s32[24]{0:T(128)S(1)}) custom-call(s32[4]{0:T(128)S(1)} %pad_add_fusion.here_ref, s32[8,12]{1,0:T(8,128)S(1)} %copy-done.2, f32[6,256,256]{2,1,0:T(8,128)} %get-tuple-element.26.own_ref, f32[6,256,256]{2,1,0:T(8,128)} %collective-permute-done.16.other_ref, f32[3072,128]{1,0:T(8,128)S(1)} %copy-done.1), custom_call_target="tpu_custom_call" | custom-call | flops 1207959552 | bytes 6291456 | tf_op jit(solution)/shard_map/pallas_call | solution.py:314
  87.2 2.7 %all-to-all-done.rows_ref = f32[8,12,8,256]{3,2,1,0:T(8,128)S(1)} async-done(((f32[8,12,8,256]{3,2,1,0:T(8,128)}), f32[8,12,8,256]{3,2,1,0:T(8,128)S(1)}, u32[]{:S(2)}, u32[]{:S(2)}) %all-to-all-start) | async-done | bytes 786464 | tf_op jit(solution)/shard_map/all_to_all | solution.py:362
  89.9 1.4 %shard_map.56 = f32[24,8,256]{2,1,0:T(8,128)} custom-call(s32[24]{0:T(128)S(1)} %get-tuple-element.28.table_ref, f32[8,12,8,256]{3,2,1,0:T(8,128)S(1)} %all-to-all-done.rows_ref), custom_call_target="tpu_custom_call" | custom-call | tf_op jit(solution)/shard_map/pallas_call | solution.py:364
  (6 shorter events, 0.1 us)
Async XLA Ops:
  0.7 1.4 %copy-start = (bf16[1,256,3072]{2,1,0:T(8,128)(2,1)S(1)}, bf16[1,256,3072]{2,1,0:T(8,128)(2,1)}, u32[]{:S(2)}) copy-start(bf16[1,256,3072]{2,1,0:T(8,128)(2,1)} %param.3) | copy-start | bytes 4718596
  3.1 5.3 %collective-permute-start = (f32[6,264,128]{2,1,0:T(8,128)S(1)}, f32[6,264,128]{2,1,0:T(8,128)S(1)}, u32[]{:S(2)}, u32[]{:S(2)}) collective-permute-start(f32[6,264,128]{2,1,0:T(8,128)S(1)} %shard_map.51), channel_id=1, source_target_pairs={{0,1},{1,0},{2,3},{3,2},{4,5},{5,4},{6,7},{7,6},{8,9},{9,8},{10,11... | collective-permute-start | bytes 2433032 | tf_op jit(solution)/shard_map/ppermute | solution.py:56
  9.2 9.3 %collective-permute-start.4 = (f32[2,264,128]{2,1,0:T(8,128)S(1)}, f32[2,264,128]{2,1,0:T(8,128)S(1)}, u32[]{:S(2)}, u32[]{:S(2)}) collective-permute-start(f32[2,264,128]{2,1,0:T(8,128)S(1)} %get-tuple-element.21), channel_id=1, source_target_pairs={{0,16},{16,0},{1,17},{17,1},{2,18},{18,2},{3,19},{19,3},{4,20},{20... | collective-permute-start | bytes 811016 | tf_op jit(solution)/shard_map/ppermute | solution.py:47
  10.3 12.2 %collective-permute-start.1 = (f32[264,128]{1,0:T(8,128)S(1)}, f32[264,128]{1,0:T(8,128)S(1)}, u32[]{:S(2)}, u32[]{:S(2)}) collective-permute-start(f32[264,128]{1,0:T(8,128)S(1)} %get-tuple-element.17), channel_id=1, source_target_pairs={{0,16},{16,0},{1,17},{17,1},{2,18},{18,2},{3,19},{19,3},{4,20},{20... | collective-permute-start | bytes 405512 | tf_op jit(solution)/shard_map/ppermute | solution.py:47
  12.2 10.3 %collective-permute-start.2 = (f32[264,128]{1,0:T(8,128)S(1)}, f32[264,128]{1,0:T(8,128)S(1)}, u32[]{:S(2)}, u32[]{:S(2)}) collective-permute-start(f32[264,128]{1,0:T(8,128)S(1)} %get-tuple-element.18), channel_id=1, source_target_pairs={{0,4},{2,6},{4,8},{6,10},{8,12},{10,14},{12,0},{14,2},{1,5},{3,7},... | collective-permute-start | bytes 405512 | tf_op jit(solution)/shard_map/ppermute | solution.py:43
  13.5 10.7 %collective-permute-start.3 = (f32[264,128]{1,0:T(8,128)S(1)}, f32[264,128]{1,0:T(8,128)S(1)}, u32[]{:S(2)}, u32[]{:S(2)}) collective-permute-start(f32[264,128]{1,0:T(8,128)S(1)} %get-tuple-element.19), channel_id=1, source_target_pairs={{0,12},{2,14},{4,0},{6,2},{8,4},{10,6},{12,8},{14,10},{1,13},{3,15... | collective-permute-start | bytes 405512 | tf_op jit(solution)/shard_map/ppermute | solution.py:43
  18.5 6.5 %collective-permute-start.5 = (f32[264,128]{1,0:T(8,128)S(1)}, f32[264,128]{1,0:T(8,128)S(1)}, u32[]{:S(2)}, u32[]{:S(2)}) collective-permute-start(f32[264,128]{1,0:T(8,128)S(1)} %get-tuple-element.30), channel_id=1, source_target_pairs={{0,2},{2,4},{4,6},{6,8},{8,10},{10,12},{12,14},{14,0},{1,3},{3,5},... | collective-permute-start | bytes 405512 | tf_op jit(solution)/shard_map/ppermute | solution.py:43
  18.6 8.0 %collective-permute-start.6 = (f32[264,128]{1,0:T(8,128)S(1)}, f32[264,128]{1,0:T(8,128)S(1)}, u32[]{:S(2)}, u32[]{:S(2)}) collective-permute-start(f32[264,128]{1,0:T(8,128)S(1)} %get-tuple-element.31), channel_id=1, source_target_pairs={{0,14},{2,0},{4,2},{6,4},{8,6},{10,8},{12,10},{14,12},{1,15},{3,1}... | collective-permute-start | bytes 405512 | tf_op jit(solution)/shard_map/ppermute | solution.py:43
  26.7 10.4 %collective-permute-start.7 = (f32[264,128]{1,0:T(8,128)S(1)}, f32[264,128]{1,0:T(8,128)S(1)}, u32[]{:S(2)}, u32[]{:S(2)}) collective-permute-start(f32[264,128]{1,0:T(8,128)S(1)} %add_add_fusion.a_ref), channel_id=1, source_target_pairs={{0,24},{2,26},{4,28},{6,30},{8,16},{10,18},{12,20},{14,22},{16,8},... | collective-permute-start | bytes 405512 | tf_op jit(solution)/shard_map/ppermute | solution.py:52
  47.1 10.3 %collective-permute-start.9 = (f32[264,128]{1,0:T(8,128)S(1)}, f32[264,128]{1,0:T(8,128)S(1)}, u32[]{:S(2)}, u32[]{:S(2)}) collective-permute-start(f32[264,128]{1,0:T(8,128)S(1)} %shard_map.53.refs_0_), channel_id=1, source_target_pairs={{0,2},{2,4},{4,6},{6,8},{8,10},{10,12},{12,14},{14,0},{1,3},{3,5},... | collective-permute-start | bytes 405512 | tf_op jit(solution)/shard_map/ppermute | solution.py:43
  47.2 10.5 %collective-permute-start.8 = (f32[264,128]{1,0:T(8,128)S(1)}, f32[264,128]{1,0:T(8,128)S(1)}, u32[]{:S(2)}, u32[]{:S(2)}) collective-permute-start(f32[264,128]{1,0:T(8,128)S(1)} %shard_map.53.refs_0_), channel_id=1, source_target_pairs={{0,14},{2,0},{4,2},{6,4},{8,6},{10,8},{12,10},{14,12},{1,15},{3,1}... | collective-permute-start | bytes 405512 | tf_op jit(solution)/shard_map/ppermute | solution.py:43
  49.9 10.6 %collective-permute-start.13 = (f32[264,128]{1,0:T(8,128)S(1)}, f32[264,128]{1,0:T(8,128)S(1)}, u32[]{:S(2)}, u32[]{:S(2)}) collective-permute-start(f32[264,128]{1,0:T(8,128)S(1)} %shard_map.53.refs_0_), channel_id=1, source_target_pairs={{0,16},{16,0},{1,17},{17,1},{2,18},{18,2},{3,19},{19,3},{4,20},{20... | collective-permute-start | bytes 405512 | tf_op jit(solution)/shard_map/ppermute | solution.py:47
  52.7 8.4 %collective-permute-start.11 = (f32[264,128]{1,0:T(8,128)S(1)}, f32[264,128]{1,0:T(8,128)S(1)}, u32[]{:S(2)}, u32[]{:S(2)}) collective-permute-start(f32[264,128]{1,0:T(8,128)S(1)} %shard_map.53.refs_0_), channel_id=1, source_target_pairs={{0,4},{2,6},{4,8},{6,10},{8,12},{10,14},{12,0},{14,2},{1,5},{3,7},... | collective-permute-start | bytes 405512 | tf_op jit(solution)/shard_map/ppermute | solution.py:43
  57.5 7.2 %collective-permute-start.10 = (f32[264,128]{1,0:T(8,128)S(1)}, f32[264,128]{1,0:T(8,128)S(1)}, u32[]{:S(2)}, u32[]{:S(2)}) collective-permute-start(f32[264,128]{1,0:T(8,128)S(1)} %shard_map.53.refs_0_), channel_id=1, source_target_pairs={{0,12},{2,14},{4,0},{6,2},{8,4},{10,6},{12,8},{14,10},{1,13},{3,15... | collective-permute-start | bytes 405512 | tf_op jit(solution)/shard_map/ppermute | solution.py:43
  57.5 7.2 %collective-permute-start.12 = (f32[264,128]{1,0:T(8,128)S(1)}, f32[264,128]{1,0:T(8,128)S(1)}, u32[]{:S(2)}, u32[]{:S(2)}) collective-permute-start(f32[264,128]{1,0:T(8,128)S(1)} %collective-permute-done.9.refs_2_), channel_id=1, source_target_pairs={{0,16},{16,0},{1,17},{17,1},{2,18},{18,2},{3,19},{19,3},{4,20},{20... | collective-permute-start | bytes 405512 | tf_op jit(solution)/shard_map/ppermute | solution.py:47
  57.7 7.0 %collective-permute-start.14 = (f32[264,128]{1,0:T(8,128)S(1)}, f32[264,128]{1,0:T(8,128)S(1)}, u32[]{:S(2)}, u32[]{:S(2)}) collective-permute-start(f32[264,128]{1,0:T(8,128)S(1)} %collective-permute-done.8.refs_1_), channel_id=1, source_target_pairs={{0,16},{16,0},{1,17},{17,1},{2,18},{18,2},{3,19},{19,3},{4,20},{20... | collective-permute-start | bytes 405512 | tf_op jit(solution)/shard_map/ppermute | solution.py:47
  66.7 10.6 %copy-start.1 = (f32[3072,128]{1,0:T(8,128)S(1)}, f32[3072,128]{1,0:T(8,128)}, u32[]{:S(2)}) copy-start(f32[3072,128]{1,0:T(8,128)} %grad_ref.1) | copy-start | bytes 4718596
  66.7 10.6 %copy-start.2 = (s32[8,12]{1,0:T(8,128)S(1)}, s32[8,12]{1,0:T(8,128)}, u32[]{:S(2)}) copy-start(s32[8,12]{1,0:T(8,128)} %owner_ref.1) | copy-start | bytes 1156
  66.7 5.1 %collective-permute-start.15 = (f32[6,8,256]{2,1,0:T(8,128)S(1)}, f32[6,8,256]{2,1,0:T(8,128)S(1)}, u32[]{:S(2)}, u32[]{:S(2)}) collective-permute-start(f32[6,8,256]{2,1,0:T(8,128)S(1)} %get-tuple-element.25), channel_id=1, source_target_pairs={{0,1},{1,0},{2,3},{3,2},{4,5},{5,4},{6,7},{7,6},{8,9},{9,8},{10,11... | collective-permute-start | bytes 147464 | tf_op jit(solution)/shard_map/ppermute | solution.py:56
  72.8 4.5 %collective-permute-start.16 = (f32[6,256,256]{2,1,0:T(8,128)}, f32[6,256,256]{2,1,0:T(8,128)}, u32[]{:S(2)}, u32[]{:S(2)}) collective-permute-start(f32[6,256,256]{2,1,0:T(8,128)} %get-tuple-element.26.own_ref), channel_id=1, source_target_pairs={{0,1},{1,0},{2,3},{3,2},{4,5},{5,4},{6,7},{7,6},{8,9},{9,8},{10,11... | collective-permute-start | bytes 4718600 | tf_op jit(solution)/shard_map/ppermute | solution.py:56
  73.1 16.8 %all-to-all-start = ((f32[8,12,8,256]{3,2,1,0:T(8,128)}), f32[8,12,8,256]{3,2,1,0:T(8,128)S(1)}, u32[]{:S(2)}, u32[]{:S(2)}) async-start(f32[8,12,8,256]{3,2,1,0:T(8,128)} %broadcast_in_dim.4), calls=%async_computation | async-start | bytes 1572864 | tf_op jit(solution)/shard_map/all_to_all | solution.py:362
